TPU v7x, 256 devices: a whole 4x4x8 slice. The times are simulated.
256 devices in a mesh: space: 64 (over x, z, y_hi), batch: 4 (over y_lo, core).
Axes of the slice: x: 4, y: 4 (y_hi: 2, y_lo: 2; y = y_hi * 2 + y_lo), z: 8, core: 2. Of those that a mesh axis runs over, the one named last changes fastest.
Arguments:
- field: bfloat16 [4, 20, 128, 128, 512], P('batch', None, 'space'), may hold values from -6 to 6
- spectral_weight: bfloat16 [2, 24, 2304, 800], P(None, 'batch', 'space'), may hold values from -6 to 6
- local_weight: bfloat16 [2, 20, 20], replicated, may hold values from -1.25 to 1.25
- bias: float32 [2, 20], replicated, may hold values from -3 to 3
Outputs:
- next_field: bfloat16 [4, 20, 128, 128, 512], P('batch', None, 'space')
All inputs are finite; a program needn't handle non-finite values.
Results may differ from a plain program's by a relative error of at most 0.02.
Values may be sent and summed in bfloat16 or wider, within the bound.
No kernel may reach another device: no remote copies, remote signals or barrier semaphores. Data moves between devices by JAX's collectives and lax.ppermute only.
A program may use at most 128 MiB of HBM per device.

v0:
```python
import math

import jax
import jax.numpy as jnp
import numpy as np
from jax import lax
from jax.experimental import pallas as pl
from jax.experimental.pallas import tpu as pltpu
from jax.sharding import PartitionSpec as P

X = 128
Y = 128
VERTICAL_POINTS = 32
EPOCH_COUNT = 16
ZT = VERTICAL_POINTS * EPOCH_COUNT
C = 20
MX = 24
MY = 24
MZ = 12
MT = 8
LAYERS = 2

QL = 12
QH = MZ * MT // QL
GROUPS = MY * QH
PARTS = 3
HALF = C // 2
LANES = 128
PLANES = 2
OWNERS = X // PLANES
KX_GROUPS = 4
KX_PER = MX // KX_GROUPS
ROWS = 2 * 2 * KX_PER
PAIRS = 2
STEPS = HALF // PAIRS
STRIP = 16

ERF_COEFFICIENTS = (
    7.97884216e-01,
    3.63342831e-02,
    -3.31296180e-05,
    -5.52402773e-05,
    3.96912621e-06,
    -1.33447465e-07,
    1.80564042e-09,
)
ERF_LIMIT = 31.36


def line_table(length, kept_count):
    half = kept_count // 2
    frequency = np.concatenate([np.arange(half), np.arange(length - half, length)])
    angles = 2.0 * math.pi / length * (np.arange(length)[:, None] * frequency[None, :] % length)
    cosine = np.cos(angles) / math.sqrt(length)
    sine = np.sin(angles) / math.sqrt(length)
    forward = np.stack([np.stack([cosine, -sine], 1), np.stack([sine, cosine], 1)], 1)
    inverse = np.stack([np.stack([cosine.T, sine.T], -1), np.stack([-sine.T, cosine.T], -1)], 1)
    return forward, inverse


def depth_table():
    half = MZ // 2
    vertical = np.concatenate([np.arange(half), np.arange(VERTICAL_POINTS - half, VERTICAL_POINTS)])
    clock = np.arange(MT)
    cells = np.arange(ZT)
    turns = (
        (cells // EPOCH_COUNT)[:, None, None] * vertical[None, :, None] * EPOCH_COUNT
        + (cells % EPOCH_COUNT)[:, None, None] * clock[None, None, :] * VERTICAL_POINTS
    ) % ZT
    angles = 2.0 * math.pi / ZT * turns.reshape(ZT, MZ * MT)
    cosine = np.cos(angles) / math.sqrt(ZT)
    sine = np.sin(angles) / math.sqrt(ZT)
    doubling = np.broadcast_to(np.where(clock == 0, 1.0, 2.0)[None, :], (MZ, MT)).reshape(-1)
    kept = MZ * MT
    forward = np.zeros((ZT, 2 * LANES))
    forward[:, :kept] = cosine
    forward[:, LANES : LANES + kept] = -sine
    inverse = np.zeros((2 * LANES, ZT))
    inverse[:kept] = cosine.T * doubling[:, None]
    inverse[LANES : LANES + kept] = -sine.T * doubling[:, None]
    return forward, inverse


def build_tables():
    zt_forward, zt_inverse = depth_table()
    y_forward, y_inverse = line_table(Y, MY)
    x_forward, x_inverse = line_table(X, MX)
    eye = np.eye(2)
    y_fwd = np.einsum("yrjm,ab,uv->maujbrvy", y_forward, eye, eye)
    y_fwd = y_fwd.reshape(MY * 8, 4 * PLANES * Y)
    y_inv = np.einsum("mryj,ab,uv->ajuymbvr", y_inverse, eye, eye)
    y_inv = y_inv.reshape(4 * PLANES * Y, MY * 8)
    x_split = x_forward.reshape(OWNERS, PLANES, 2, 2, KX_GROUPS, KX_PER)
    x_re, x_im = x_split[:, :, :, 0], x_split[:, :, :, 1]
    parts = np.stack([np.stack([x_re, -x_im]), np.stack([x_im, x_re])])
    x_fwd = np.einsum("stiurgm,ab->gsatmibur", parts, eye)
    x_fwd = x_fwd.reshape(KX_GROUPS * 2 * ROWS, OWNERS * 8)
    x_split = x_inverse.reshape(KX_GROUPS, KX_PER, 2, OWNERS, PLANES, 2)
    x_inv = np.einsum("gmsiuj,ab,c,t->iaujgsbctm", x_split, eye, np.ones(2), np.ones(2))
    x_inv = x_inv.reshape(OWNERS * 8, KX_GROUPS * 4 * ROWS)
    spread = np.zeros((LANES, HALF, LANES))
    for channel in range(HALF):
        for ql in range(QL):
            for out in range(HALF):
                spread[channel * QL + ql, channel, out * QL + ql] = 1.0
    spread = spread.reshape(LANES, HALF * LANES)
    tile = np.einsum("pa,qb,o->pqaob", np.eye(PARTS), np.eye(QL), np.ones(HALF))
    tile = tile.reshape(PARTS * QL, PARTS, HALF * QL)
    tile = np.pad(tile, ((0, 0), (0, 0), (0, LANES - HALF * QL))).reshape(PARTS * QL, -1)
    gather = np.einsum("ci,hu,ta,rs,o->chtrsaiuo", np.eye(HALF), eye, eye, eye, np.ones(HALF))
    gather = gather.reshape(HALF * 8, 2 * C * C)
    held = [zt_forward, zt_inverse, y_fwd, y_inv, x_fwd, x_inv, spread, tile, gather]
    names = ["zt_fwd", "zt_inv", "y_fwd", "y_inv", "x_fwd", "x_inv", "spread", "tile", "gather"]
    return {
        name: table.astype(np.float32).astype(jnp.bfloat16) for name, table in zip(names, held)
    }


def lane_index(shape):
    return lax.broadcasted_iota(jnp.int32, shape, len(shape) - 1)


def dot(left, right):
    return jnp.dot(left, right, preferred_element_type=jnp.float32)


def forward_step(step, block, zt_fwd, y_fwd, modes_ref):
    columns = []
    for pair in range(PAIRS):
        rows = []
        for half in range(2):
            z = dot(block(half, pair), zt_fwd).astype(jnp.bfloat16)
            rows += [z[:, :LANES], z[:, LANES:]]
        columns.append(jnp.concatenate(rows, 0))
    modes = dot(y_fwd, jnp.concatenate(columns, 1))
    lane = lane_index((MY * 8, LANES))
    for pair in range(PAIRS):
        channel = step * PAIRS + pair
        own = modes[:, pair * LANES : (pair + 1) * LANES]
        mask = (lane >= channel * QL) & (lane < channel * QL + QL)
        for qh in range(QH):
            shift = lax.rem((channel - qh) * QL + LANES, LANES)
            moved = pltpu.roll(own, shift, 1)
            kept = modes_ref[:, qh].reshape(MY * 8, LANES)
            modes_ref[:, qh] = jnp.where(mask, moved, kept).reshape(MY, 8, LANES)


def forward_kernel(field_ref, zt_ref, y_ref, out_ref, modes_ref):
    step = pl.program_id(0)

    @pl.when(step == 0)
    def _():
        modes_ref[...] = jnp.zeros_like(modes_ref)

    def block(half, pair):
        return field_ref[half, pair].reshape(PLANES * Y, ZT)

    forward_step(step, block, zt_ref[...], y_ref[...], modes_ref)

    @pl.when(step == STEPS - 1)
    def _():
        out_ref[...] = modes_ref[...].reshape(GROUPS * 8, LANES).astype(jnp.bfloat16)


def whole(shape):
    return pl.BlockSpec(shape, lambda *_: (0,) * len(shape), pipeline_mode=pl.Buffered(1))


def field_spec():
    return pl.BlockSpec((2, PAIRS, PLANES, Y, ZT), lambda s: (0, s, 0, 0, 0))


MESSAGE = (GROUPS * 8, LANES)
MODES = pltpu.VMEM((MY, QH, 8, LANES), jnp.float32)


def forward_call(field, tables):
    return pl.pallas_call(
        forward_kernel,
        grid=(STEPS,),
        in_specs=[field_spec(), whole(tables["zt_fwd"].shape), whole(tables["y_fwd"].shape)],
        out_specs=whole(MESSAGE),
        out_shape=jax.ShapeDtypeStruct(MESSAGE, jnp.bfloat16),
        scratch_shapes=[MODES],
        compiler_params=pltpu.CompilerParams(vmem_limit_bytes=48 << 20),
        name="forward_zt_y",
    )(field, tables["zt_fwd"], tables["y_fwd"])


def gelu(x):
    s = jnp.minimum(x * x, ERF_LIMIT)
    p = jnp.float32(ERF_COEFFICIENTS[-1])
    for coefficient in ERF_COEFFICIENTS[-2::-1]:
        p = p * s + jnp.float32(coefficient)
    h = 0.5 * x
    return h + h * jnp.tanh(x * p)


def inverse_step(step, modes_ref, local_ref, y_inv, zt_inv, out_ref):
    lane = lane_index((MY * 8, LANES))
    columns = []
    for pair in range(PAIRS):
        channel = step * PAIRS + pair
        value = jnp.zeros((MY * 8, LANES), jnp.float32)
        for qh in range(QH):
            shift = lax.rem((qh - channel) * QL + LANES, LANES)
            moved = pltpu.roll(modes_ref[:, qh].reshape(MY * 8, LANES), shift, 1)
            value = jnp.where((lane >= qh * QL) & (lane < qh * QL + QL), moved, value)
        columns.append(value.astype(jnp.bfloat16))
    back = dot(y_inv, jnp.concatenate(columns, 1)).astype(jnp.bfloat16)
    span = PLANES * Y
    for pair in range(PAIRS):
        own = back[:, pair * LANES : (pair + 1) * LANES]
        for half in range(2):
            at = 2 * half * span
            rows = jnp.concatenate([own[at : at + span], own[at + span : at + 2 * span]], 1)
            total = dot(rows, zt_inv) + local_ref[half, pair].reshape(span, ZT)
            out_ref[half, pair] = gelu(total).astype(jnp.bfloat16).reshape(PLANES, Y, ZT)


def load_modes(message_ref, modes_ref):
    modes_ref[...] = message_ref[...].astype(jnp.float32).reshape(MY, QH, 8, LANES)


def inverse_kernel(message_ref, local_ref, y_ref, zt_ref, out_ref, modes_ref):
    step = pl.program_id(0)

    @pl.when(step == 0)
    def _():
        load_modes(message_ref, modes_ref)

    inverse_step(step, modes_ref, local_ref, y_ref[...], zt_ref[...], out_ref)


FIELD = (2, HALF, PLANES, Y, ZT)


def inverse_call(message, local, tables):
    return pl.pallas_call(
        inverse_kernel,
        grid=(STEPS,),
        in_specs=[
            whole(MESSAGE),
            field_spec(),
            whole(tables["y_inv"].shape),
            whole(tables["zt_inv"].shape),
        ],
        out_specs=field_spec(),
        out_shape=jax.ShapeDtypeStruct(FIELD, jnp.bfloat16),
        scratch_shapes=[MODES],
        compiler_params=pltpu.CompilerParams(vmem_limit_bytes=48 << 20),
        name="inverse_zt_y",
    )(message, local, tables["y_inv"], tables["zt_inv"])


def mix_kernel(
    place_ref, message_ref, own, near, far, across, x_ref, inv_ref, spread_ref, out_ref, sums_ref
):
    span = OWNERS * 8
    message = message_ref[...].astype(jnp.float32).reshape(OWNERS, PARTS * 8, LANES)
    pieces = [
        message[:, part * 8 : part * 8 + 8].reshape(span, LANES).astype(jnp.bfloat16)
        for part in range(PARTS)
    ]
    group_rows = 2 * ROWS
    for distance, weights in enumerate((own, near, far, across)):
        group = place_ref[0] ^ distance
        table = x_ref[pl.ds(pl.multiple_of(group * group_rows, group_rows), group_rows), :]
        modes = dot(table, jnp.concatenate(pieces, 1)).astype(jnp.bfloat16)
        rows = [modes[:, part * LANES : (part + 1) * LANES] for part in range(PARTS)]
        spread = dot(jnp.concatenate(rows, 0), spread_ref[...])
        for part in range(PARTS):
            for out_half in range(2):
                totals = [None, None]
                for c10 in range(HALF):
                    at = ((c10 * PARTS + part) * 2 + out_half) * ROWS
                    weight = weights[at : at + ROWS, :].astype(jnp.float32)
                    for kind in range(2):
                        top = part * group_rows + kind * ROWS
                        term = spread[top : top + ROWS, c10 * LANES : (c10 + 1) * LANES] * weight
                        totals[kind] = term if c10 == 0 else totals[kind] + term
                for kind in range(2):
                    start = group * (4 * ROWS) + (kind * 2 + out_half) * ROWS
                    sums_ref[
                        pl.ds(pl.multiple_of(start, 8), ROWS), part * LANES : (part + 1) * LANES
                    ] = totals[kind]
    back = dot(inv_ref[...], sums_ref[...].astype(jnp.bfloat16))
    blocks = [
        back[:, part * LANES : (part + 1) * LANES].reshape(OWNERS, 8, LANES)
        for part in range(PARTS)
    ]
    out_ref[...] = jnp.concatenate(blocks, 1).reshape(GROUPS * 8, LANES).astype(jnp.bfloat16)


def mix_call(place, message, weights, tables):
    held = [tables["x_fwd"], tables["x_inv"], tables["spread"]]
    return pl.pallas_call(
        mix_kernel,
        grid=(1,),
        in_specs=[pl.BlockSpec(memory_space=pltpu.SMEM), whole(MESSAGE)]
        + [whole(w.shape) for w in weights]
        + [whole(t.shape) for t in held],
        out_specs=whole(MESSAGE),
        out_shape=jax.ShapeDtypeStruct(MESSAGE, jnp.bfloat16),
        scratch_shapes=[pltpu.VMEM((KX_GROUPS * 4 * ROWS, PARTS * LANES), jnp.float32)],
        compiler_params=pltpu.CompilerParams(vmem_limit_bytes=48 << 20),
        name="mix_x",
    )(place, message, *weights, *held)


def arrange_kernel(weight_ref, tile_ref, gather_ref, out_ref, rows_ref):
    kx = pl.program_id(0)
    tiled = lax.dot_general(
        weight_ref[0, 0],
        tile_ref[...],
        (((0,), (0,)), ((), ())),
        preferred_element_type=jnp.float32,
    )
    row = lax.broadcasted_iota(jnp.int32, tiled.shape, 0)
    place = lax.rem(lane_index(tiled.shape), LANES)
    first = lax.rem(row, HALF) * QL
    kept = jnp.where((place >= first) & (place < first + QL), tiled, 0.0)
    moved = dot(gather_ref[...], kept.astype(jnp.bfloat16))
    for c10 in range(HALF):
        for part in range(PARTS):
            start = (c10 * PARTS + part) * 2 * ROWS
            rows_ref[pl.ds(start + kx, 8, stride=KX_PER), :] = moved[
                c10 * 8 : c10 * 8 + 8, part * LANES : (part + 1) * LANES
            ]

    @pl.when(kx == KX_PER - 1)
    def _():
        out_ref[...] = rows_ref[...].astype(jnp.bfloat16)


def arrange_weights(weights, layer, tables):
    shape = (HALF * PARTS * 2 * ROWS, LANES)
    held = [tables["tile"], tables["gather"]]
    return pl.pallas_call(
        arrange_kernel,
        grid=(KX_PER,),
        in_specs=[pl.BlockSpec((1, 1) + weights.shape[2:], lambda k: (layer, k, 0, 0))]
        + [whole(t.shape) for t in held],
        out_specs=whole(shape),
        out_shape=jax.ShapeDtypeStruct(shape, jnp.bfloat16),
        scratch_shapes=[pltpu.VMEM(shape, jnp.float32)],
        compiler_params=pltpu.CompilerParams(vmem_limit_bytes=48 << 20),
        name="arrange_weights",
    )(weights, *held)


def swap(value, distance):
    return lax.ppermute(value, "batch", [(i, i ^ distance) for i in range(KX_GROUPS)])


def spread_weights(own):
    far = swap(own, 2)
    return own, swap(own, 1), far, swap(far, 1)


def exchange(message):
    grouped = message.reshape(OWNERS, PARTS * 8, LANES)
    moved = lax.all_to_all(grouped, "space", split_axis=0, concat_axis=0, tiled=True)
    return moved.reshape(MESSAGE)


def local_kernel(offset_ref, weight_ref, field_ref, out_ref, mixing_ref):
    size = C * STRIP

    @pl.when((pl.program_id(0) == 0) & (pl.program_id(1) == 0))
    def _():
        row = lax.broadcasted_iota(jnp.int32, (size, C), 0) // STRIP
        pick_out = (row == lane_index((size, C))).astype(jnp.bfloat16)
        lane = lane_index((C, size)) // STRIP
        pick_in = (lax.broadcasted_iota(jnp.int32, (C, size), 0) == lane).astype(jnp.bfloat16)
        rows = dot(pick_out, weight_ref[...]).astype(jnp.bfloat16)
        full = dot(rows, pick_in)
        same = lax.rem(lax.broadcasted_iota(jnp.int32, (size, size), 0), STRIP) == lax.rem(
            lane_index((size, size)), STRIP
        )
        mixing_ref[...] = jnp.where(same, full, 0.0).astype(jnp.bfloat16)

    mixed = dot(mixing_ref[...], field_ref[...].reshape(size, ZT))
    for half in range(2):
        for c10 in range(HALF):
            channel = half * HALF + c10
            rows = mixed[channel * STRIP : (channel + 1) * STRIP]
            out_ref[half, c10, 0] = rows + offset_ref[channel]


def local_term(current, weight, offset):
    spec = pl.BlockSpec((2, HALF, 1, STRIP, ZT), lambda p, y: (0, 0, p, y, 0))
    return pl.pallas_call(
        local_kernel,
        grid=(PLANES, Y // STRIP),
        in_specs=[pl.BlockSpec(memory_space=pltpu.SMEM), whole((C, C)), spec],
        out_specs=spec,
        out_shape=jax.ShapeDtypeStruct(FIELD, jnp.float32),
        scratch_shapes=[pltpu.VMEM((C * STRIP, C * STRIP), jnp.bfloat16)],
        compiler_params=pltpu.CompilerParams(vmem_limit_bytes=48 << 20),
        name="local_mixing",
    )(offset, weight.T, current)


def body(field, spectral_weight, local_weight, bias):
    tables = {name: jnp.asarray(table) for name, table in build_tables().items()}
    place = lax.axis_index("batch").astype(jnp.int32).reshape(1)
    current = field.reshape(FIELD)
    weights = None
    for layer in range(LAYERS):
        with jax.named_scope("forward"):
            message = forward_call(current, tables)
        if weights is None:
            message, spectral_weight = lax.optimization_barrier((message, spectral_weight))
            weights = [
                spread_weights(arrange_weights(spectral_weight, i, tables)) for i in range(LAYERS)
            ]
        received = exchange(message)
        with jax.named_scope("mix"):
            back = mix_call(place, received, weights[layer], tables)
        local = local_term(current, local_weight[layer], bias[layer])
        with jax.named_scope("inverse"):
            current = inverse_call(exchange(back), local, tables)
    return current.reshape(field.shape)


def solution(mesh):
    placed = (P("batch", None, "space", None, None), P(None, "batch", "space", None), P(), P())
    return jax.shard_map(
        body,
        mesh=mesh,
        in_specs=placed,
        out_specs=P("batch", None, "space", None, None),
        check_vma=False,
    )
```

profile of v0, /device:TPU:2, one launch (start us, length us, event | category | flops | bytes accessed | tf_op | source)
XLA Modules:
  0.0 168.9 jit_solution(4005769831778760138)
XLA Ops:
  0.0 1.0 copy-done.3
  1.0 0.9 copy-done.8
  2.0 0.0 copy-start.6
  2.0 0.0 copy-start.10
  2.0 8.2 %forward_zt_y.2 = bf16[1536,128]{1,0:T(8,128)(2,1)} custom-call(bf16[2,10,2,128,512]{4,3,2,1,0:T(8,128)(2,1)} %bitcast.21, bf16[512,256]{1,0:T(8,128)(2,1)S(1)} %copy-done.8, bf16[192,1024]{1,0:T(8,128)(2,1)S(1)} %copy-done.3), custom_call_target="tpu_custom_call" | custom-call | tf_op jit(solution)/shard_map/forward/forward_zt_y/pallas_call | solution.py:178
  10.2 14.8 %all-to-all-start = ((bf16[64,24,128]{2,1,0:T(8,128)(2,1)}), bf16[64,24,128]{2,1,0:T(8,128)(2,1)S(1)}, u32[]{:S(2)}, u32[]{:S(2)}) async-start(bf16[64,24,128]{2,1,0:T(8,128)(2,1)} %bitcast.2), calls=%async_computation | async-start | bytes 786432 | tf_op jit(solution)/shard_map/all_to_all | solution.py:363
  25.0 0.0 copy-done.15
  25.0 0.1 copy.14.weight_ref
  25.1 0.0 copy-done.11
  25.2 0.0 copy-done.14
  25.2 4.1 %arrange_weights.2.own = bf16[1440,128]{1,0:T(8,128)(2,1)S(1)} custom-call(bf16[2,6,36,800]{3,2,1,0:T(8,128)(2,1)S(1)} %copy.14.weight_ref, bf16[36,384]{1,0:T(8,128)(2,1)S(1)} %copy-done.14, bf16[80,800]{1,0:T(8,128)(2,1)S(1)} %copy-done.11), custom_call_target="tpu_custom_call" | custom-call | tf_op jit(solution)/shard_map/arrange_weights/pallas_call | solution.py:339
  29.3 0.8 collective-permute-start.1
  30.0 0.0 collective-permute-start
  30.0 11.7 %collective-permute-done.1.far = bf16[1440,128]{1,0:T(8,128)(2,1)S(1)} collective-permute-done((bf16[1440,128]{1,0:T(8,128)(2,1)S(1)}, bf16[1440,128]{1,0:T(8,128)(2,1)S(1)}, u32[]{:S(2)}, u32[]{:S(2)}) %collective-permute-start.1) | collective-permute-done | bytes 368672 | tf_op jit(solution)/shard_map/ppermute | solution.py:353
  41.7 0.0 collective-permute-start.2
  41.7 0.0 collective-permute-done.near
  41.7 1.8 %collective-permute-done.2.across = bf16[1440,128]{1,0:T(8,128)(2,1)} collective-permute-done((bf16[1440,128]{1,0:T(8,128)(2,1)S(1)}, bf16[1440,128]{1,0:T(8,128)(2,1)}, u32[]{:S(2)}, u32[]{:S(2)}) %collective-permute-start.2) | collective-permute-done | bytes 368672 | tf_op jit(solution)/shard_map/ppermute | solution.py:353
  43.5 0.0 all-to-all-done
  43.5 0.0 copy-done.5
  43.5 0.0 copy-done.10
  43.5 3.6 %mix_x.2 = bf16[1536,128]{1,0:T(8,128)(2,1)} custom-call(s32[1]{0:T(128)} %bitcast.place_ref, bf16[1536,128]{1,0:T(8,128)(2,1)S(1)} %bitcast.23, bf16[1440,128]{1,0:T(8,128)(2,1)S(1)} %arrange_weights.2.own, bf16[1440,128]{1,0:T(8,128)(2,1)} %collective-permute-done.near, bf16[1440,128]{1,0:T(8,128)(2,1)S(1)} %collective-permute-done.1.far, ...), custom_call_target="tpu_custom_call" | custom-call | tf_op jit(solution)/shard_map/mix/mix_x/pallas_call | solution.py:297
  47.1 11.6 %all-to-all-start.1 = ((bf16[64,24,128]{2,1,0:T(8,128)(2,1)}), bf16[64,24,128]{2,1,0:T(8,128)(2,1)S(1)}, u32[]{:S(2)}, u32[]{:S(2)}) async-start(bf16[64,24,128]{2,1,0:T(8,128)(2,1)} %bitcast.4), calls=%async_computation.1 | async-start | bytes 786432 | tf_op jit(solution)/shard_map/inverse/all_to_all | solution.py:363
  58.8 0.0 copy-done.16
  58.8 0.1 copy.18
  58.9 0.0 copy-start.1
  58.9 2.5 %copy-done.1 = bf16[1,20,2,128,512]{4,3,2,1,0:T(8,128)(2,1)S(1)} copy-done((bf16[1,20,2,128,512]{4,3,2,1,0:T(8,128)(2,1)S(1)}, bf16[1,20,2,128,512]{4,3,2,1,0:T(8,128)(2,1)}, u32[]{:S(2)}) %copy-start.1) | copy-done | bytes 5242904
  61.4 10.9 %local_mixing.2.local_ref = f32[2,10,2,128,512]{4,3,2,1,0:T(8,128)} custom-call(f32[20]{0:T(128)S(1)} %get-tuple-element.12.offset_ref, bf16[20,20]{1,0:T(8,128)(2,1)S(1)} %bitcast.27, bf16[2,10,2,128,512]{4,3,2,1,0:T(8,128)(2,1)S(1)} %bitcast.22), custom_call_target="tpu_custom_call" | custom-call | tf_op jit(solution)/shard_map/local_mixing/pallas_call | solution.py:393
  72.3 2.3 %all-to-all-done.1 = bf16[64,24,128]{2,1,0:T(8,128)(2,1)S(1)} async-done(((bf16[64,24,128]{2,1,0:T(8,128)(2,1)}), bf16[64,24,128]{2,1,0:T(8,128)(2,1)S(1)}, u32[]{:S(2)}, u32[]{:S(2)}) %all-to-all-start.1) | async-done | bytes 393248 | tf_op jit(solution)/shard_map/inverse/all_to_all | solution.py:363
  74.6 13.0 %inverse_zt_y.2.field_ref = bf16[2,10,2,128,512]{4,3,2,1,0:T(8,128)(2,1)} custom-call(bf16[1536,128]{1,0:T(8,128)(2,1)S(1)} %bitcast.25, f32[2,10,2,128,512]{4,3,2,1,0:T(8,128)} %local_mixing.2.local_ref, bf16[1024,192]{1,0:T(8,128)(2,1)S(1)} %copy-done.2, bf16[256,512]{1,0:T(8,128)(2,1)S(1)} %copy-done.7), custom_call_target="tpu_custom_call" | custom-call | tf_op jit(solution)/shard_map/inverse/inverse_zt_y/pallas_call | solution.py:239
  87.7 8.1 %forward_zt_y.3 = bf16[1536,128]{1,0:T(8,128)(2,1)} custom-call(bf16[2,10,2,128,512]{4,3,2,1,0:T(8,128)(2,1)} %inverse_zt_y.2.field_ref, bf16[512,256]{1,0:T(8,128)(2,1)S(1)} %copy-done.9, bf16[192,1024]{1,0:T(8,128)(2,1)S(1)} %copy-done.4), custom_call_target="tpu_custom_call" | custom-call | tf_op jit(solution)/shard_map/forward/forward_zt_y/pallas_call | solution.py:178
  95.8 10.5 %all-to-all-start.2 = ((bf16[64,24,128]{2,1,0:T(8,128)(2,1)}), bf16[64,24,128]{2,1,0:T(8,128)(2,1)S(1)}, u32[]{:S(2)}, u32[]{:S(2)}) async-start(bf16[64,24,128]{2,1,0:T(8,128)(2,1)} %bitcast.9), calls=%async_computation.2 | async-start | bytes 786432 | tf_op jit(solution)/shard_map/all_to_all | solution.py:363
  106.3 4.1 %arrange_weights.3.own = bf16[1440,128]{1,0:T(8,128)(2,1)S(1)} custom-call(bf16[2,6,36,800]{3,2,1,0:T(8,128)(2,1)S(1)} %copy.14.weight_ref, bf16[36,384]{1,0:T(8,128)(2,1)S(1)} %copy-done.14, bf16[80,800]{1,0:T(8,128)(2,1)S(1)} %copy-done.11), custom_call_target="tpu_custom_call" | custom-call | tf_op jit(solution)/shard_map/arrange_weights/pallas_call | solution.py:339
  110.4 0.5 collective-permute-start.4
  110.9 0.0 collective-permute-start.3
  110.9 11.5 %collective-permute-done.4.far = bf16[1440,128]{1,0:T(8,128)(2,1)S(1)} collective-permute-done((bf16[1440,128]{1,0:T(8,128)(2,1)S(1)}, bf16[1440,128]{1,0:T(8,128)(2,1)S(1)}, u32[]{:S(2)}, u32[]{:S(2)}) %collective-permute-start.4) | collective-permute-done | bytes 368672 | tf_op jit(solution)/shard_map/ppermute | solution.py:353
  122.4 0.0 collective-permute-start.5
  122.4 0.0 collective-permute-done.3.near
  122.5 1.7 collective-permute-done.5.across
  124.1 0.8 copy-done.12
  124.9 0.0 all-to-all-done.2
  124.9 1.0 copy-done.13
  125.9 2.5 %mix_x.3 = bf16[1536,128]{1,0:T(8,128)(2,1)} custom-call(s32[1]{0:T(128)} %bitcast.place_ref, bf16[1536,128]{1,0:T(8,128)(2,1)S(1)} %bitcast.24, bf16[1440,128]{1,0:T(8,128)(2,1)S(1)} %arrange_weights.3.own, bf16[1440,128]{1,0:T(8,128)(2,1)S(1)} %collective-permute-done.3.near, bf16[1440,128]{1,0:T(8,128)(2,1)S(1)} %collective-permute-done.4.far, ...), custom_call_target="tpu_custom_call" | custom-call | tf_op jit(solution)/shard_map/mix/mix_x/pallas_call | solution.py:297
  128.4 11.7 %all-to-all-start.3 = ((bf16[64,24,128]{2,1,0:T(8,128)(2,1)}), bf16[64,24,128]{2,1,0:T(8,128)(2,1)S(1)}, u32[]{:S(2)}, u32[]{:S(2)}) async-start(bf16[64,24,128]{2,1,0:T(8,128)(2,1)} %bitcast.11), calls=%async_computation.3 | async-start | bytes 786432 | tf_op jit(solution)/shard_map/inverse/all_to_all | solution.py:363
  140.1 0.1 copy.19
  140.2 2.5 %copy-done = bf16[2,10,2,128,512]{4,3,2,1,0:T(8,128)(2,1)S(1)} copy-done((bf16[2,10,2,128,512]{4,3,2,1,0:T(8,128)(2,1)S(1)}, bf16[2,10,2,128,512]{4,3,2,1,0:T(8,128)(2,1)}, u32[]{:S(2)}) %copy-start) | copy-done | bytes 5242904
  142.7 10.9 %local_mixing.3.local_ref = f32[2,10,2,128,512]{4,3,2,1,0:T(8,128)} custom-call(f32[20]{0:T(128)S(1)} %get-tuple-element.11.offset_ref, bf16[20,20]{1,0:T(8,128)(2,1)S(1)} %bitcast.28, bf16[2,10,2,128,512]{4,3,2,1,0:T(8,128)(2,1)S(1)} %copy-done), custom_call_target="tpu_custom_call" | custom-call | tf_op jit(solution)/shard_map/local_mixing/pallas_call | solution.py:393
  153.6 2.4 %all-to-all-done.3 = bf16[64,24,128]{2,1,0:T(8,128)(2,1)S(1)} async-done(((bf16[64,24,128]{2,1,0:T(8,128)(2,1)}), bf16[64,24,128]{2,1,0:T(8,128)(2,1)S(1)}, u32[]{:S(2)}, u32[]{:S(2)}) %all-to-all-start.3) | async-done | bytes 393248 | tf_op jit(solution)/shard_map/inverse/all_to_all | solution.py:363
  156.0 13.0 %inverse_zt_y.3 = bf16[2,10,2,128,512]{4,3,2,1,0:T(8,128)(2,1)} custom-call(bf16[1536,128]{1,0:T(8,128)(2,1)S(1)} %bitcast.26, f32[2,10,2,128,512]{4,3,2,1,0:T(8,128)} %local_mixing.3.local_ref, bf16[1024,192]{1,0:T(8,128)(2,1)S(1)} %copy-done.2, bf16[256,512]{1,0:T(8,128)(2,1)S(1)} %copy-done.7), custom_call_target="tpu_custom_call" | custom-call | tf_op jit(solution)/shard_map/inverse/inverse_zt_y/pallas_call | solution.py:239
  (23 shorter events, 0.1 us)
Async XLA Ops:
  0.0 1.0 copy-start.3
  1.0 0.9 copy-start.8
  1.9 23.1 %copy-start.15 = (bf16[2,6,36,800]{3,0,2,1:T(2,128)(2,1)S(1)}, bf16[2,6,36,800]{3,0,2,1:T(2,128)(2,1)}, u32[]{:S(2)}) copy-start(bf16[2,6,36,800]{3,0,2,1:T(2,128)(2,1)} %param.14) | copy-start | bytes 2073604
  1.9 23.2 %copy-start.11 = (bf16[80,800]{1,0:T(8,128)(2,1)S(1)}, bf16[80,800]{1,0:T(8,128)(2,1)}, u32[]{:S(2)}) copy-start(bf16[80,800]{1,0:T(8,128)(2,1)} %constant.30.clone.gather_ref) | copy-start | bytes 384004
  2.0 23.2 %copy-start.14 = (bf16[36,384]{1,0:T(8,128)(2,1)S(1)}, bf16[36,384]{1,0:T(8,128)(2,1)}, u32[]{:S(2)}) copy-start(bf16[36,384]{1,0:T(8,128)(2,1)} %constant.29.clone.tile_ref) | copy-start | bytes 82948
  2.0 41.6 %copy-start.5 = (bf16[512,384]{1,0:T(8,128)(2,1)S(1)}, bf16[512,384]{1,0:T(8,128)(2,1)}, u32[]{:S(2)}) copy-start(bf16[512,384]{1,0:T(8,128)(2,1)} %constant.27.clone.inv_ref) | copy-start | bytes 1179652
  2.0 41.6 %copy-start.6 = (bf16[128,1280]{1,0:T(8,128)(2,1)S(1)}, bf16[128,1280]{1,0:T(8,128)(2,1)}, u32[]{:S(2)}) copy-start(bf16[128,1280]{1,0:T(8,128)(2,1)} %constant.28.clone.spread_ref) | copy-start | bytes 983044
  2.0 41.6 %copy-start.10 = (bf16[192,512]{1,0:T(8,128)(2,1)S(1)}, bf16[192,512]{1,0:T(8,128)(2,1)}, u32[]{:S(2)}) copy-start(bf16[192,512]{1,0:T(8,128)(2,1)} %constant.26.clone.x_ref) | copy-start | bytes 589828
  10.2 48.5 %copy-start.16 = (bf16[2,20,20]{2,0,1:T(2,128)(2,1)S(1)}, bf16[2,20,20]{2,0,1:T(2,128)(2,1)}, u32[]{:S(2)}) copy-start(bf16[2,20,20]{2,0,1:T(2,128)(2,1)} %param.15) | copy-start | bytes 4804
  10.2 48.7 %copy-start.17 = (f32[2,20]{1,0:T(2,128)S(1)}, f32[2,20]{1,0:T(2,128)}, u32[]{:S(2)}) copy-start(f32[2,20]{1,0:T(2,128)} %param.16) | copy-start | bytes 484
  10.2 33.3 %all-to-all-start = ((bf16[64,24,128]{2,1,0:T(8,128)(2,1)}), bf16[64,24,128]{2,1,0:T(8,128)(2,1)S(1)}, u32[]{:S(2)}, u32[]{:S(2)}) async-start(bf16[64,24,128]{2,1,0:T(8,128)(2,1)} %bitcast.2), calls=%async_computation | async-start | bytes 786432 | tf_op jit(solution)/shard_map/all_to_all | solution.py:363
  29.3 12.4 %collective-permute-start.1 = (bf16[1440,128]{1,0:T(8,128)(2,1)S(1)}, bf16[1440,128]{1,0:T(8,128)(2,1)S(1)}, u32[]{:S(2)}, u32[]{:S(2)}) collective-permute-start(bf16[1440,128]{1,0:T(8,128)(2,1)S(1)} %arrange_weights.2.own), channel_id=1, source_target_pairs={{0,2},{1,3},{2,0},{3,1},{4,6},{5,7},{6,4},{7,5},{8,10},{9,11},{10,... | collective-permute-start | bytes 1105928 | tf_op jit(solution)/shard_map/ppermute | solution.py:353
  30.0 11.7 %collective-permute-start = (bf16[1440,128]{1,0:T(8,128)(2,1)S(1)}, bf16[1440,128]{1,0:T(8,128)(2,1)}, u32[]{:S(2)}, u32[]{:S(2)}) collective-permute-start(bf16[1440,128]{1,0:T(8,128)(2,1)S(1)} %arrange_weights.2.own), channel_id=1, source_target_pairs={{0,1},{1,0},{2,3},{3,2},{4,5},{5,4},{6,7},{7,6},{8,9},{9,8},{10,11... | collective-permute-start | bytes 1105928 | tf_op jit(solution)/shard_map/ppermute | solution.py:353
  41.7 1.8 %collective-permute-start.2 = (bf16[1440,128]{1,0:T(8,128)(2,1)S(1)}, bf16[1440,128]{1,0:T(8,128)(2,1)}, u32[]{:S(2)}, u32[]{:S(2)}) collective-permute-start(bf16[1440,128]{1,0:T(8,128)(2,1)S(1)} %collective-permute-done.1.far), channel_id=1, source_target_pairs={{0,1},{1,0},{2,3},{3,2},{4,5},{5,4},{6,7},{7,6},{8,9},{9,8},{10,11... | collective-permute-start | bytes 1105928 | tf_op jit(solution)/shard_map/ppermute | solution.py:353
  47.1 27.5 %all-to-all-start.1 = ((bf16[64,24,128]{2,1,0:T(8,128)(2,1)}), bf16[64,24,128]{2,1,0:T(8,128)(2,1)S(1)}, u32[]{:S(2)}, u32[]{:S(2)}) async-start(bf16[64,24,128]{2,1,0:T(8,128)(2,1)} %bitcast.4), calls=%async_computation.1 | async-start | bytes 786432 | tf_op jit(solution)/shard_map/inverse/all_to_all | solution.py:363
  58.9 2.5 %copy-start.1 = (bf16[1,20,2,128,512]{4,3,2,1,0:T(8,128)(2,1)S(1)}, bf16[1,20,2,128,512]{4,3,2,1,0:T(8,128)(2,1)}, u32[]{:S(2)}) copy-start(bf16[1,20,2,128,512]{4,3,2,1,0:T(8,128)(2,1)} %param.13) | copy-start | bytes 15728644
  61.4 13.2 %copy-start.2 = (bf16[1024,192]{1,0:T(8,128)(2,1)S(1)}, bf16[1024,192]{1,0:T(8,128)(2,1)}, u32[]{:S(2)}) copy-start(bf16[1024,192]{1,0:T(8,128)(2,1)} %constant.25.clone.y_ref) | copy-start | bytes 1179652
  61.4 13.2 %copy-start.7 = (bf16[256,512]{1,0:T(8,128)(2,1)S(1)}, bf16[256,512]{1,0:T(8,128)(2,1)}, u32[]{:S(2)}) copy-start(bf16[256,512]{1,0:T(8,128)(2,1)} %constant.23.clone.zt_ref) | copy-start | bytes 786436
  74.6 13.1 %copy-start.4 = (bf16[192,1024]{1,0:T(8,128)(2,1)S(1)}, bf16[192,1024]{1,0:T(8,128)(2,1)}, u32[]{:S(2)}) copy-start(bf16[192,1024]{1,0:T(8,128)(2,1)} %constant.24.clone.y_ref) | copy-start | bytes 1179652
  74.6 13.1 %copy-start.9 = (bf16[512,256]{1,0:T(8,128)(2,1)S(1)}, bf16[512,256]{1,0:T(8,128)(2,1)}, u32[]{:S(2)}) copy-start(bf16[512,256]{1,0:T(8,128)(2,1)} %constant.22.clone.zt_ref) | copy-start | bytes 786436
  95.8 29.1 %all-to-all-start.2 = ((bf16[64,24,128]{2,1,0:T(8,128)(2,1)}), bf16[64,24,128]{2,1,0:T(8,128)(2,1)S(1)}, u32[]{:S(2)}, u32[]{:S(2)}) async-start(bf16[64,24,128]{2,1,0:T(8,128)(2,1)} %bitcast.9), calls=%async_computation.2 | async-start | bytes 786432 | tf_op jit(solution)/shard_map/all_to_all | solution.py:363
  110.4 12.1 %collective-permute-start.4 = (bf16[1440,128]{1,0:T(8,128)(2,1)S(1)}, bf16[1440,128]{1,0:T(8,128)(2,1)S(1)}, u32[]{:S(2)}, u32[]{:S(2)}) collective-permute-start(bf16[1440,128]{1,0:T(8,128)(2,1)S(1)} %arrange_weights.3.own), channel_id=1, source_target_pairs={{0,2},{1,3},{2,0},{3,1},{4,6},{5,7},{6,4},{7,5},{8,10},{9,11},{10,... | collective-permute-start | bytes 1105928 | tf_op jit(solution)/shard_map/ppermute | solution.py:353
  110.9 11.5 %collective-permute-start.3 = (bf16[1440,128]{1,0:T(8,128)(2,1)S(1)}, bf16[1440,128]{1,0:T(8,128)(2,1)S(1)}, u32[]{:S(2)}, u32[]{:S(2)}) collective-permute-start(bf16[1440,128]{1,0:T(8,128)(2,1)S(1)} %arrange_weights.3.own), channel_id=1, source_target_pairs={{0,1},{1,0},{2,3},{3,2},{4,5},{5,4},{6,7},{7,6},{8,9},{9,8},{10,11... | collective-permute-start | bytes 1105928 | tf_op jit(solution)/shard_map/ppermute | solution.py:353
  122.4 1.7 collective-permute-start.5
  124.1 0.8 copy-start.12
  124.9 1.0 copy-start.13
  128.4 27.6 %all-to-all-start.3 = ((bf16[64,24,128]{2,1,0:T(8,128)(2,1)}), bf16[64,24,128]{2,1,0:T(8,128)(2,1)S(1)}, u32[]{:S(2)}, u32[]{:S(2)}) async-start(bf16[64,24,128]{2,1,0:T(8,128)(2,1)} %bitcast.11), calls=%async_computation.3 | async-start | bytes 786432 | tf_op jit(solution)/shard_map/inverse/all_to_all | solution.py:363
  140.2 2.5 %copy-start = (bf16[2,10,2,128,512]{4,3,2,1,0:T(8,128)(2,1)S(1)}, bf16[2,10,2,128,512]{4,3,2,1,0:T(8,128)(2,1)}, u32[]{:S(2)}) copy-start(bf16[2,10,2,128,512]{4,3,2,1,0:T(8,128)(2,1)} %inverse_zt_y.2.field_ref) | copy-start | bytes 15728644
where the time goes:
time: 170 us; the launch traced here: 169 us
  Pallas kernels  78.5 us (46%)
  starting transfers between devices  49.9 us (29%)
  waiting for transfers between devices  31.3 us (18%)
  local copies, waits for them, and re-layouts  9.04 us (5%)
    all_to_all x4, starting transfers between devices, exchange(): lax.all_to_all(grouped, 'space', split_axis=0, concat_axis=0, tiled=True)  48.6 us
    ppermute x6, waiting for transfers between devices, swap(): lax.ppermute(value, 'batch', [(i, i ^ distance) for i in range(KX_GROUPS)])  26.7 us
    pallas_call x2, Pallas kernels, inverse_call(): pl.pallas_call(inverse_kernel, grid=(STEPS,), in_specs=[whole(MESSAGE), f...  26 us
    pallas_call x2, Pallas kernels, local_term(): pl.pallas_call(local_kernel, grid=(PLANES, Y // STRIP), in_specs=[pl.Bloc...  21.9 us
    pallas_call x2, Pallas kernels, forward_call(): pl.pallas_call(forward_kernel, grid=(STEPS,), in_specs=[field_spec(), who...  16.4 us
    unnamed x38, local copies, waits for them, and re-layouts  8.92 us
    pallas_call x2, Pallas kernels, arrange_weights(): pl.pallas_call(arrange_kernel, grid=(KX_PER,), in_specs=[pl.BlockSpec((1,...  8.21 us
    pallas_call x2, Pallas kernels, mix_call(): pl.pallas_call(mix_kernel, grid=(1,), in_specs=[pl.BlockSpec(memory_space...  6.08 us
  transfers between devices with their start and end apart: 10, of which 6 were waited for; matrix products, arithmetic and copies ran while one was open for 0% of the time, Pallas kernels for 18%

commit v1 on v0

--- a/solution.py
+++ b/solution.py
@@ -34,6 +34,8 @@
 PAIRS = 2
 STEPS = HALF // PAIRS
 STRIP = 16
+LOCAL_ROWS = 64
+VMEM_BYTES = 58 << 20
 
 ERF_COEFFICIENTS = (
     7.97884216e-01,
@@ -109,11 +111,22 @@
     tile = np.pad(tile, ((0, 0), (0, 0), (0, LANES - HALF * QL))).reshape(PARTS * QL, -1)
     gather = np.einsum("ci,hu,ta,rs,o->chtrsaiuo", np.eye(HALF), eye, eye, eye, np.ones(HALF))
     gather = gather.reshape(HALF * 8, 2 * C * C)
-    held = [zt_forward, zt_inverse, y_fwd, y_inv, x_fwd, x_inv, spread, tile, gather]
-    names = ["zt_fwd", "zt_inv", "y_fwd", "y_inv", "x_fwd", "x_inv", "spread", "tile", "gather"]
-    return {
-        name: table.astype(np.float32).astype(jnp.bfloat16) for name, table in zip(names, held)
+    mask = np.zeros((2 * C * C, LANES))
+    for row in range(2 * C * C):
+        mask[row, row % HALF * QL : (row % HALF + 1) * QL] = 1.0
+    held = {
+        "zt_fwd": zt_forward,
+        "zt_inv": zt_inverse,
+        "y_fwd": y_fwd,
+        "y_inv": y_inv,
+        "x_fwd": x_fwd,
+        "x_inv": x_inv,
+        "spread": spread,
+        "tile": tile,
+        "mask": mask,
+        "gather": gather,
     }
+    return {name: table.astype(np.float32).astype(jnp.bfloat16) for name, table in held.items()}
 
 
 def lane_index(shape):
@@ -182,7 +195,7 @@
         out_specs=whole(MESSAGE),
         out_shape=jax.ShapeDtypeStruct(MESSAGE, jnp.bfloat16),
         scratch_shapes=[MODES],
-        compiler_params=pltpu.CompilerParams(vmem_limit_bytes=48 << 20),
+        compiler_params=pltpu.CompilerParams(vmem_limit_bytes=VMEM_BYTES),
         name="forward_zt_y",
     )(field, tables["zt_fwd"], tables["y_fwd"])
 
@@ -209,13 +222,17 @@
         columns.append(value.astype(jnp.bfloat16))
     back = dot(y_inv, jnp.concatenate(columns, 1)).astype(jnp.bfloat16)
     span = PLANES * Y
+    results = {}
     for pair in range(PAIRS):
         own = back[:, pair * LANES : (pair + 1) * LANES]
         for half in range(2):
             at = 2 * half * span
             rows = jnp.concatenate([own[at : at + span], own[at + span : at + 2 * span]], 1)
             total = dot(rows, zt_inv) + local_ref[half, pair].reshape(span, ZT)
-            out_ref[half, pair] = gelu(total).astype(jnp.bfloat16).reshape(PLANES, Y, ZT)
+            result = gelu(total).astype(jnp.bfloat16)
+            out_ref[half, pair] = result.reshape(PLANES, Y, ZT)
+            results[half, pair] = result
+    return results
 
 
 def load_modes(message_ref, modes_ref):
@@ -248,9 +265,55 @@
         out_specs=field_spec(),
         out_shape=jax.ShapeDtypeStruct(FIELD, jnp.bfloat16),
         scratch_shapes=[MODES],
-        compiler_params=pltpu.CompilerParams(vmem_limit_bytes=48 << 20),
+        compiler_params=pltpu.CompilerParams(vmem_limit_bytes=VMEM_BYTES),
         name="inverse_zt_y",
     )(message, local, tables["y_inv"], tables["zt_inv"])
+
+
+def turn_kernel(
+    message_ref,
+    local_ref,
+    y_inv_ref,
+    zt_inv_ref,
+    zt_ref,
+    y_ref,
+    out_ref,
+    send_ref,
+    modes_ref,
+    next_ref,
+):
+    step = pl.program_id(0)
+
+    @pl.when(step == 0)
+    def _():
+        load_modes(message_ref, modes_ref)
+        next_ref[...] = jnp.zeros_like(next_ref)
+
+    results = inverse_step(step, modes_ref, local_ref, y_inv_ref[...], zt_inv_ref[...], out_ref)
+    forward_step(
+        step, lambda half, pair: results[half, pair], zt_ref[...], y_ref[...], next_ref
+    )
+
+    @pl.when(step == STEPS - 1)
+    def _():
+        send_ref[...] = next_ref[...].reshape(GROUPS * 8, LANES).astype(jnp.bfloat16)
+
+
+def turn_call(message, local, tables):
+    held = [tables[name] for name in ("y_inv", "zt_inv", "zt_fwd", "y_fwd")]
+    return pl.pallas_call(
+        turn_kernel,
+        grid=(STEPS,),
+        in_specs=[whole(MESSAGE), field_spec()] + [whole(t.shape) for t in held],
+        out_specs=[field_spec(), whole(MESSAGE)],
+        out_shape=[
+            jax.ShapeDtypeStruct(FIELD, jnp.bfloat16),
+            jax.ShapeDtypeStruct(MESSAGE, jnp.bfloat16),
+        ],
+        scratch_shapes=[MODES, MODES],
+        compiler_params=pltpu.CompilerParams(vmem_limit_bytes=VMEM_BYTES),
+        name="inverse_then_forward",
+    )(message, local, *held)
 
 
 def mix_kernel(
@@ -303,48 +366,46 @@
         out_specs=whole(MESSAGE),
         out_shape=jax.ShapeDtypeStruct(MESSAGE, jnp.bfloat16),
         scratch_shapes=[pltpu.VMEM((KX_GROUPS * 4 * ROWS, PARTS * LANES), jnp.float32)],
-        compiler_params=pltpu.CompilerParams(vmem_limit_bytes=48 << 20),
+        compiler_params=pltpu.CompilerParams(vmem_limit_bytes=VMEM_BYTES),
         name="mix_x",
     )(place, message, *weights, *held)
 
 
-def arrange_kernel(weight_ref, tile_ref, gather_ref, out_ref, rows_ref):
-    kx = pl.program_id(0)
-    tiled = lax.dot_general(
-        weight_ref[0, 0],
-        tile_ref[...],
-        (((0,), (0,)), ((), ())),
-        preferred_element_type=jnp.float32,
-    )
-    row = lax.broadcasted_iota(jnp.int32, tiled.shape, 0)
-    place = lax.rem(lane_index(tiled.shape), LANES)
-    first = lax.rem(row, HALF) * QL
-    kept = jnp.where((place >= first) & (place < first + QL), tiled, 0.0)
-    moved = dot(gather_ref[...], kept.astype(jnp.bfloat16))
-    for c10 in range(HALF):
-        for part in range(PARTS):
-            start = (c10 * PARTS + part) * 2 * ROWS
-            rows_ref[pl.ds(start + kx, 8, stride=KX_PER), :] = moved[
-                c10 * 8 : c10 * 8 + 8, part * LANES : (part + 1) * LANES
-            ]
-
-    @pl.when(kx == KX_PER - 1)
-    def _():
-        out_ref[...] = rows_ref[...].astype(jnp.bfloat16)
+def arrange_kernel(weight_ref, tile_ref, mask_ref, gather_ref, out_ref, rows_ref):
+    own = mask_ref[...]
+    for kx in range(KX_PER):
+        tiled = lax.dot_general(
+            weight_ref[0, kx],
+            tile_ref[...],
+            (((0,), (0,)), ((), ())),
+            preferred_element_type=jnp.float32,
+        )
+        kept = [
+            tiled[:, part * LANES : (part + 1) * LANES].astype(jnp.bfloat16) * own
+            for part in range(PARTS)
+        ]
+        moved = dot(gather_ref[...], jnp.concatenate(kept, 1))
+        for c10 in range(HALF):
+            for part in range(PARTS):
+                start = (c10 * PARTS + part) * 2 * ROWS
+                rows_ref[pl.ds(start + kx, 8, stride=KX_PER), :] = moved[
+                    c10 * 8 : c10 * 8 + 8, part * LANES : (part + 1) * LANES
+                ]
+    out_ref[...] = rows_ref[...].astype(jnp.bfloat16)
 
 
 def arrange_weights(weights, layer, tables):
     shape = (HALF * PARTS * 2 * ROWS, LANES)
-    held = [tables["tile"], tables["gather"]]
+    held = [tables["tile"], tables["mask"], tables["gather"]]
     return pl.pallas_call(
         arrange_kernel,
-        grid=(KX_PER,),
-        in_specs=[pl.BlockSpec((1, 1) + weights.shape[2:], lambda k: (layer, k, 0, 0))]
+        grid=(1,),
+        in_specs=[pl.BlockSpec((1,) + weights.shape[1:], lambda k: (layer, 0, 0, 0))]
         + [whole(t.shape) for t in held],
         out_specs=whole(shape),
         out_shape=jax.ShapeDtypeStruct(shape, jnp.bfloat16),
         scratch_shapes=[pltpu.VMEM(shape, jnp.float32)],
-        compiler_params=pltpu.CompilerParams(vmem_limit_bytes=48 << 20),
+        compiler_params=pltpu.CompilerParams(vmem_limit_bytes=VMEM_BYTES),
         name="arrange_weights",
     )(weights, *held)
 
@@ -380,48 +441,50 @@
         )
         mixing_ref[...] = jnp.where(same, full, 0.0).astype(jnp.bfloat16)
 
-    mixed = dot(mixing_ref[...], field_ref[...].reshape(size, ZT))
-    for half in range(2):
-        for c10 in range(HALF):
-            channel = half * HALF + c10
-            rows = mixed[channel * STRIP : (channel + 1) * STRIP]
-            out_ref[half, c10, 0] = rows + offset_ref[channel]
+    for first in range(0, LOCAL_ROWS, STRIP):
+        mixed = dot(mixing_ref[...], field_ref[:, :, 0, first : first + STRIP].reshape(size, ZT))
+        for half in range(2):
+            for c10 in range(HALF):
+                channel = half * HALF + c10
+                rows = mixed[channel * STRIP : (channel + 1) * STRIP] + offset_ref[channel]
+                out_ref[half, c10, 0, first : first + STRIP] = rows.astype(jnp.bfloat16)
 
 
 def local_term(current, weight, offset):
-    spec = pl.BlockSpec((2, HALF, 1, STRIP, ZT), lambda p, y: (0, 0, p, y, 0))
+    spec = pl.BlockSpec((2, HALF, 1, LOCAL_ROWS, ZT), lambda p, y: (0, 0, p, y, 0))
     return pl.pallas_call(
         local_kernel,
-        grid=(PLANES, Y // STRIP),
+        grid=(PLANES, Y // LOCAL_ROWS),
         in_specs=[pl.BlockSpec(memory_space=pltpu.SMEM), whole((C, C)), spec],
         out_specs=spec,
-        out_shape=jax.ShapeDtypeStruct(FIELD, jnp.float32),
+        out_shape=jax.ShapeDtypeStruct(FIELD, jnp.bfloat16),
         scratch_shapes=[pltpu.VMEM((C * STRIP, C * STRIP), jnp.bfloat16)],
-        compiler_params=pltpu.CompilerParams(vmem_limit_bytes=48 << 20),
+        compiler_params=pltpu.CompilerParams(vmem_limit_bytes=VMEM_BYTES),
         name="local_mixing",
     )(offset, weight.T, current)
+
+
+def after(value, *others):
+    return lax.optimization_barrier((value,) + others)[0]
 
 
 def body(field, spectral_weight, local_weight, bias):
     tables = {name: jnp.asarray(table) for name, table in build_tables().items()}
     place = lax.axis_index("batch").astype(jnp.int32).reshape(1)
-    current = field.reshape(FIELD)
-    weights = None
-    for layer in range(LAYERS):
-        with jax.named_scope("forward"):
-            message = forward_call(current, tables)
-        if weights is None:
-            message, spectral_weight = lax.optimization_barrier((message, spectral_weight))
-            weights = [
-                spread_weights(arrange_weights(spectral_weight, i, tables)) for i in range(LAYERS)
-            ]
-        received = exchange(message)
-        with jax.named_scope("mix"):
-            back = mix_call(place, received, weights[layer], tables)
-        local = local_term(current, local_weight[layer], bias[layer])
-        with jax.named_scope("inverse"):
-            current = inverse_call(exchange(back), local, tables)
-    return current.reshape(field.shape)
+    field = field.reshape(FIELD)
+    own = arrange_weights(spectral_weight, 0, tables)
+    weights = spread_weights(own)
+    message = forward_call(field, dict(tables, zt_fwd=after(tables["zt_fwd"], own)))
+    local = local_term(field, after(local_weight[0], message), bias[0])
+    received = after(exchange(message), local)
+    back = mix_call(place, received, weights, tables)
+    own = arrange_weights(after(spectral_weight, back), 1, tables)
+    weights = spread_weights(own)
+    current, message = turn_call(after(exchange(back), own), local, tables)
+    local = local_term(current, local_weight[1], bias[1])
+    received = after(exchange(message), local)
+    back = mix_call(place, received, weights, tables)
+    return inverse_call(exchange(back), local, tables).reshape(1, C, PLANES, Y, ZT)
 
 
 def solution(mesh):

time: 170 us -> 169 us (level)
  blocking collectives: 0 us -> 28.5 us
  starting transfers between devices: 49.9 us -> 30.2 us
  Pallas kernels: 78.5 us -> 71.1 us
    all_to_all x0 -> x1, blocking collectives: none -> 28.5 us  [exchange(): lax.all_to_all(grouped, 'space', split_axis=0, concat_axis=0, tiled=True)]
    all_to_all x4 -> x3, starting transfers between devices: 48.6 us -> 27.8 us  [exchange(): lax.all_to_all(grouped, 'space', split_axis=0, concat_axis=0, tiled=True)]
    ppermute x6, waiting for transfers between devices: 26.7 us -> 13.1 us  [swap(): lax.ppermute(value, 'batch', [(i, i ^ distance) for i in range(KX_GROUPS)])]
    pallas_call x2 -> x1, Pallas kernels: 26 us -> 13.2 us  [inverse_call(): pl.pallas_call(inverse_kernel, grid=(STEPS,), in_specs=[whole(MESSAGE), f...]
    all_to_all x4 -> x3, waiting for transfers between devices: 4.64 us -> 16.7 us  [exchange(): lax.all_to_all(grouped, 'space', split_axis=0, concat_axis=0, tiled=True)]
    pallas_call x4 -> x5, Pallas kernels: 30.1 us -> 41.3 us  [the longest x1 18.4 us: turn_call(): pl.pallas_call(turn_kernel, grid=(STEPS,), in_specs=[whole(MESSAGE), fiel...]
    pallas_call x2 -> x1, Pallas kernels: 16.4 us -> 8.28 us  [forward_call(): pl.pallas_call(forward_kernel, grid=(STEPS,), in_specs=[field_spec(), who...]
    pallas_call x2, Pallas kernels: 6.08 us -> 8.37 us  [mix_call(): pl.pallas_call(mix_kernel, grid=(1,), in_specs=[pl.BlockSpec(memory_space...]
  transfers between devices with their start and end apart: 10 -> 9, of which waited for: 6 -> 3; matrix products, arithmetic and copies ran while one was open for 0% -> 2% of each run, Pallas kernels for 18% -> 16%
where the time goes in v1:
time: 169 us; the launch traced here: 168 us
  Pallas kernels  71.1 us (42%)
  starting transfers between devices  30.2 us (18%)
  waiting for transfers between devices  29.8 us (18%)
  blocking collectives  28.5 us (17%)
  local copies, waits for them, and re-layouts  8.54 us (5%)
    all_to_all x1, blocking collectives, exchange(): lax.all_to_all(grouped, 'space', split_axis=0, concat_axis=0, tiled=True)  28.5 us
    all_to_all x3, starting transfers between devices, exchange(): lax.all_to_all(grouped, 'space', split_axis=0, concat_axis=0, tiled=True)  27.8 us
    pallas_call x1, Pallas kernels, turn_call(): pl.pallas_call(turn_kernel, grid=(STEPS,), in_specs=[whole(MESSAGE), fiel...  18.4 us
    all_to_all x3, waiting for transfers between devices, exchange(): lax.all_to_all(grouped, 'space', split_axis=0, concat_axis=0, tiled=True)  16.7 us
    pallas_call x2, Pallas kernels, local_term(): pl.pallas_call(local_kernel, grid=(PLANES, Y // LOCAL_ROWS), in_specs=[pl...  14.5 us
    pallas_call x1, Pallas kernels, inverse_call(): pl.pallas_call(inverse_kernel, grid=(STEPS,), in_specs=[whole(MESSAGE), f...  13.2 us
    ppermute x6, waiting for transfers between devices, swap(): lax.ppermute(value, 'batch', [(i, i ^ distance) for i in range(KX_GROUPS)])  13.1 us
    pallas_call x2, Pallas kernels, arrange_weights(): pl.pallas_call(arrange_kernel, grid=(1,), in_specs=[pl.BlockSpec((1,) + w...  8.46 us
  transfers between devices with their start and end apart: 9, of which 3 were waited for; matrix products, arithmetic and copies ran while one was open for 2% of the time, Pallas kernels for 16%

profile of v1, /device:TPU:2, one launch (start us, length us, event | category | flops | bytes accessed | tf_op | source)
XLA Modules:
  0.0 168.3 jit_solution(5056245090498057788)
XLA Ops:
  0.0 2.2 %copy.15.weight_ref = bf16[2,6,36,800]{3,2,1,0:T(8,128)(2,1)} copy(bf16[2,6,36,800]{3,0,2,1:T(2,128)(2,1)} %param.15) | data formatting | bytes 1382400 | tf_op args[1]
  2.2 4.2 %arrange_weights.2.own = bf16[1440,128]{1,0:T(8,128)(2,1)} custom-call(bf16[2,6,36,800]{3,2,1,0:T(8,128)(2,1)} %copy.15.weight_ref, bf16[36,384]{1,0:T(8,128)(2,1)} %constant.31.clone.tile_ref, bf16[800,128]{1,0:T(8,128)(2,1)} %constant.32.clone.mask_ref, bf16[80,800]{1,0:T(8,128)(2,1)} %constant.33.clone.gather_ref), custom_call_target="tpu_custom_call" | custom-call | tf_op jit(solution)/shard_map/arrange_weights/pallas_call | solution.py:400
  6.4 1.6 collective-permute-start.1
  8.0 8.3 %forward_zt_y.1 = bf16[1536,128]{1,0:T(8,128)(2,1)} custom-call(bf16[2,10,2,128,512]{4,3,2,1,0:T(8,128)(2,1)} %bitcast.20, bf16[512,256]{1,0:T(8,128)(2,1)} %constant.24.clone.zt_ref, bf16[192,1024]{1,0:T(8,128)(2,1)} %constant.26.clone.y_ref), custom_call_target="tpu_custom_call" | custom-call | tf_op jit(solution)/shard_map/forward_zt_y/pallas_call | solution.py:191
  16.3 14.4 %all-to-all-start = ((bf16[64,24,128]{2,1,0:T(8,128)(2,1)}), bf16[64,24,128]{2,1,0:T(8,128)(2,1)S(1)}, u32[]{:S(2)}, u32[]{:S(2)}) async-start(bf16[64,24,128]{2,1,0:T(8,128)(2,1)} %bitcast.23), calls=%async_computation | async-start | bytes 786432 | tf_op jit(solution)/shard_map/all_to_all | solution.py:424
  30.6 0.0 copy-done.5
  30.6 0.1 collective-permute-start
  30.7 0.0 collective-permute-done.1.far
  30.8 0.0 copy-start.6
  30.8 0.5 collective-permute-start.2
  31.2 0.0 copy-done.12
  31.3 0.7 copy.19
  32.0 0.0 copy-done.13
  32.0 0.6 slice_bitcast_fusion
  32.6 7.3 %local_mixing.2.local_ref = bf16[2,10,2,128,512]{4,3,2,1,0:T(8,128)(2,1)} custom-call(f32[20]{0:T(128)} %get-tuple-element.24.offset_ref, bf16[20,20]{1,0:T(8,128)(2,1)} %bitcast.30, bf16[2,10,2,128,512]{4,3,2,1,0:T(8,128)(2,1)} %bitcast.21), custom_call_target="tpu_custom_call" | custom-call | tf_op jit(solution)/shard_map/local_mixing/pallas_call | solution.py:455
  39.8 0.0 copy-done.6
  39.8 6.2 %all-to-all-done = bf16[64,24,128]{2,1,0:T(8,128)(2,1)S(1)} async-done(((bf16[64,24,128]{2,1,0:T(8,128)(2,1)}), bf16[64,24,128]{2,1,0:T(8,128)(2,1)S(1)}, u32[]{:S(2)}, u32[]{:S(2)}) %all-to-all-start) | async-done | bytes 393248 | tf_op jit(solution)/shard_map/all_to_all | solution.py:424
  46.0 0.0 collective-permute-done.near
  46.0 0.0 collective-permute-done.2.across
  46.0 0.0 copy-start.10
  46.0 0.7 copy-done.2
  46.8 0.1 copy-done.7
  46.9 0.1 copy-done.10
  47.0 4.2 %mix_x.2 = bf16[1536,128]{1,0:T(8,128)(2,1)} custom-call(s32[1]{0:T(128)} %bitcast.place_ref, bf16[1536,128]{1,0:T(8,128)(2,1)} %bitcast.25, bf16[1440,128]{1,0:T(8,128)(2,1)} %arrange_weights.2.own, bf16[1440,128]{1,0:T(8,128)(2,1)} %copy-done.7, bf16[1440,128]{1,0:T(8,128)(2,1)} %copy-done.6, bf16[1440,128]{1,0:T(8,128)(2,1)} %copy-done.10, ...), custom_call_target="tpu_custom_call" | custom-call | tf_op jit(solution)/shard_map/mix_x/pallas_call | solution.py:360
  51.2 6.7 %all-to-all-start.1 = ((bf16[64,24,128]{2,1,0:T(8,128)(2,1)}), bf16[64,24,128]{2,1,0:T(8,128)(2,1)S(1)}, u32[]{:S(2)}, u32[]{:S(2)}) async-start(bf16[64,24,128]{2,1,0:T(8,128)(2,1)} %bitcast.27), calls=%async_computation.1 | async-start | bytes 786432 | tf_op jit(solution)/shard_map/all_to_all | solution.py:424
  57.9 0.0 copy-done
  57.9 1.0 copy.17.weight_ref
  59.0 4.2 %arrange_weights.3.own = bf16[1440,128]{1,0:T(8,128)(2,1)} custom-call(bf16[2,6,36,800]{3,2,1,0:T(8,128)(2,1)} %copy.17.weight_ref, bf16[36,384]{1,0:T(8,128)(2,1)} %constant.31.clone.tile_ref, bf16[800,128]{1,0:T(8,128)(2,1)} %constant.32.clone.mask_ref, bf16[80,800]{1,0:T(8,128)(2,1)} %constant.33.clone.gather_ref), custom_call_target="tpu_custom_call" | custom-call | tf_op jit(solution)/shard_map/arrange_weights/pallas_call | solution.py:400
  63.2 10.5 %all-to-all-done.1 = bf16[64,24,128]{2,1,0:T(8,128)(2,1)S(1)} async-done(((bf16[64,24,128]{2,1,0:T(8,128)(2,1)}), bf16[64,24,128]{2,1,0:T(8,128)(2,1)S(1)}, u32[]{:S(2)}, u32[]{:S(2)}) %all-to-all-start.1) | async-done | bytes 393248 | tf_op jit(solution)/shard_map/all_to_all | solution.py:424
  73.7 0.8 copy-done.1
  74.4 18.4 %inverse_then_forward.1 = (bf16[2,10,2,128,512]{4,3,2,1,0:T(8,128)(2,1)}, bf16[1536,128]{1,0:T(8,128)(2,1)}) custom-call(bf16[1536,128]{1,0:T(8,128)(2,1)} %bitcast.24, bf16[2,10,2,128,512]{4,3,2,1,0:T(8,128)(2,1)} %local_mixing.2.local_ref, bf16[1024,192]{1,0:T(8,128)(2,1)} %constant.27.clone.y_inv_ref.y_ref, ...), custom_call_target="tpu_custom_call" | custom-call | tf_op jit(solution)/shard_map/inverse_then_forward/pallas_call | solution.py:304
  92.8 6.7 %all-to-all-start.2 = ((bf16[64,24,128]{2,1,0:T(8,128)(2,1)}), bf16[64,24,128]{2,1,0:T(8,128)(2,1)S(1)}, u32[]{:S(2)}, u32[]{:S(2)}) async-start(bf16[64,24,128]{2,1,0:T(8,128)(2,1)} %bitcast.29), calls=%async_computation.2 | async-start | bytes 786432 | tf_op jit(solution)/shard_map/all_to_all | solution.py:424
  99.6 0.2 collective-permute-start.4
  99.8 0.0 collective-permute-start.3
  99.8 13.1 %collective-permute-done.4.far = bf16[1440,128]{1,0:T(8,128)(2,1)S(1)} collective-permute-done((bf16[1440,128]{1,0:T(8,128)(2,1)S(1)}, bf16[1440,128]{1,0:T(8,128)(2,1)S(1)}, u32[]{:S(2)}, u32[]{:S(2)}) %collective-permute-start.4) | collective-permute-done | bytes 368672 | tf_op jit(solution)/shard_map/ppermute | solution.py:414
  112.9 0.0 collective-permute-start.5
  112.9 0.7 copy.20
  113.6 7.2 %local_mixing.3.local_ref = bf16[2,10,2,128,512]{4,3,2,1,0:T(8,128)(2,1)} custom-call(f32[20]{0:T(128)} %get-tuple-element.23.offset_ref, bf16[20,20]{1,0:T(8,128)(2,1)} %bitcast.31, bf16[2,10,2,128,512]{4,3,2,1,0:T(8,128)(2,1)} %get-tuple-element.19.field_ref), custom_call_target="tpu_custom_call" | custom-call | tf_op jit(solution)/shard_map/local_mixing/pallas_call | solution.py:455
  120.8 0.0 all-to-all-done.2
  120.9 0.0 copy-start.3
  120.9 0.0 collective-permute-done.3.near
  120.9 0.0 collective-permute-done.5.across
  120.9 0.7 copy-done.3
  121.6 0.1 copy-done.9
  121.7 0.7 copy-done.11
  122.5 4.2 %mix_x.3 = bf16[1536,128]{1,0:T(8,128)(2,1)} custom-call(s32[1]{0:T(128)} %bitcast.place_ref, bf16[1536,128]{1,0:T(8,128)(2,1)} %bitcast.26, bf16[1440,128]{1,0:T(8,128)(2,1)} %arrange_weights.3.own, bf16[1440,128]{1,0:T(8,128)(2,1)} %copy-done.9, bf16[1440,128]{1,0:T(8,128)(2,1)} %copy-done.8, bf16[1440,128]{1,0:T(8,128)(2,1)} %copy-done.11, ...), custom_call_target="tpu_custom_call" | custom-call | tf_op jit(solution)/shard_map/mix_x/pallas_call | solution.py:360
  126.6 28.5 %all_to_all.20 = bf16[64,24,128]{2,1,0:T(8,128)(2,1)} all-to-all(bf16[64,24,128]{2,1,0:T(8,128)(2,1)} %bitcast.28), channel_id=1, replica_groups=mesh['space'=64,'batch'=4] {'space'}, dimensions={0} | all-to-all | bytes 786432 | tf_op jit(solution)/shard_map/all_to_all | solution.py:424
  155.1 13.2 %inverse_zt_y.1 = bf16[2,10,2,128,512]{4,3,2,1,0:T(8,128)(2,1)} custom-call(bf16[1536,128]{1,0:T(8,128)(2,1)} %bitcast.22, bf16[2,10,2,128,512]{4,3,2,1,0:T(8,128)(2,1)} %local_mixing.3.local_ref, bf16[1024,192]{1,0:T(8,128)(2,1)} %constant.27.clone.y_inv_ref.y_ref, bf16[256,512]{1,0:T(8,128)(2,1)} %constant.25.clone.zt_inv_ref.zt_ref), custom_call_target="tpu_custom_call" | custom-call | tf_op jit(solution)/shard_map/inverse_zt_y/pallas_call | solution.py:256
  (14 shorter events, 0.0 us)
Async XLA Ops:
  0.0 31.2 %copy-start.12 = (bf16[2,20,20]{2,0,1:T(2,128)(2,1)S(1)}, bf16[2,20,20]{2,0,1:T(2,128)(2,1)}, u32[]{:S(2)}) copy-start(bf16[2,20,20]{2,0,1:T(2,128)(2,1)} %param.16) | copy-start | bytes 4804
  0.0 32.0 %copy-start.13 = (f32[2,20]{1,0:T(2,128)S(1)}, f32[2,20]{1,0:T(2,128)}, u32[]{:S(2)}) copy-start(f32[2,20]{1,0:T(2,128)} %param.17) | copy-start | bytes 484
  6.4 24.2 %copy-start.5 = (bf16[1440,128]{1,0:T(8,128)(2,1)S(1)}, bf16[1440,128]{1,0:T(8,128)(2,1)}, u32[]{:S(2)}) copy-start(bf16[1440,128]{1,0:T(8,128)(2,1)} %arrange_weights.2.own) | copy-start | bytes 1105924
  6.4 24.4 %collective-permute-start.1 = (bf16[1440,128]{1,0:T(8,128)(2,1)}, bf16[1440,128]{1,0:T(8,128)(2,1)S(1)}, u32[]{:S(2)}, u32[]{:S(2)}) collective-permute-start(bf16[1440,128]{1,0:T(8,128)(2,1)} %arrange_weights.2.own), channel_id=1, source_target_pairs={{0,2},{1,3},{2,0},{3,1},{4,6},{5,7},{6,4},{7,5},{8,10},{9,11},{10,... | collective-permute-start | bytes 1105928 | tf_op jit(solution)/shard_map/ppermute | solution.py:414
  16.3 29.7 %all-to-all-start = ((bf16[64,24,128]{2,1,0:T(8,128)(2,1)}), bf16[64,24,128]{2,1,0:T(8,128)(2,1)S(1)}, u32[]{:S(2)}, u32[]{:S(2)}) async-start(bf16[64,24,128]{2,1,0:T(8,128)(2,1)} %bitcast.23), calls=%async_computation | async-start | bytes 786432 | tf_op jit(solution)/shard_map/all_to_all | solution.py:424
  30.6 15.4 %collective-permute-start = (bf16[1440,128]{1,0:T(8,128)(2,1)S(1)}, bf16[1440,128]{1,0:T(8,128)(2,1)S(1)}, u32[]{:S(2)}, u32[]{:S(2)}) collective-permute-start(bf16[1440,128]{1,0:T(8,128)(2,1)S(1)} %copy-done.5), channel_id=1, source_target_pairs={{0,1},{1,0},{2,3},{3,2},{4,5},{5,4},{6,7},{7,6},{8,9},{9,8},{10,11... | collective-permute-start | bytes 1105928 | tf_op jit(solution)/shard_map/ppermute | solution.py:414
  30.8 9.1 %copy-start.6 = (bf16[1440,128]{1,0:T(8,128)(2,1)}, bf16[1440,128]{1,0:T(8,128)(2,1)S(1)}, u32[]{:S(2)}) copy-start(bf16[1440,128]{1,0:T(8,128)(2,1)S(1)} %collective-permute-done.1.far) | copy-start | bytes 1105924
  30.8 15.2 %collective-permute-start.2 = (bf16[1440,128]{1,0:T(8,128)(2,1)S(1)}, bf16[1440,128]{1,0:T(8,128)(2,1)S(1)}, u32[]{:S(2)}, u32[]{:S(2)}) collective-permute-start(bf16[1440,128]{1,0:T(8,128)(2,1)S(1)} %collective-permute-done.1.far), channel_id=1, source_target_pairs={{0,1},{1,0},{2,3},{3,2},{4,5},{5,4},{6,7},{7,6},{8,9},{9,8},{10,11... | collective-permute-start | bytes 1105928 | tf_op jit(solution)/shard_map/ppermute | solution.py:414
  32.6 25.4 %copy-start = (bf16[2,6,36,800]{3,0,2,1:T(2,128)(2,1)S(1)}, bf16[2,6,36,800]{3,0,2,1:T(2,128)(2,1)}, u32[]{:S(2)}) copy-start(bf16[2,6,36,800]{3,0,2,1:T(2,128)(2,1)} %param.15) | copy-start | bytes 2073604
  46.0 0.8 copy-start.2
  46.0 0.9 copy-start.7
  46.0 1.0 copy-start.10
  51.2 22.5 %all-to-all-start.1 = ((bf16[64,24,128]{2,1,0:T(8,128)(2,1)}), bf16[64,24,128]{2,1,0:T(8,128)(2,1)S(1)}, u32[]{:S(2)}, u32[]{:S(2)}) async-start(bf16[64,24,128]{2,1,0:T(8,128)(2,1)} %bitcast.27), calls=%async_computation.1 | async-start | bytes 786432 | tf_op jit(solution)/shard_map/all_to_all | solution.py:424
  63.2 36.4 %copy-start.4 = (bf16[1440,128]{1,0:T(8,128)(2,1)S(1)}, bf16[1440,128]{1,0:T(8,128)(2,1)}, u32[]{:S(2)}) copy-start(bf16[1440,128]{1,0:T(8,128)(2,1)} %arrange_weights.3.own) | copy-start | bytes 1105924
  73.7 0.8 copy-start.1
  92.8 28.0 %all-to-all-start.2 = ((bf16[64,24,128]{2,1,0:T(8,128)(2,1)}), bf16[64,24,128]{2,1,0:T(8,128)(2,1)S(1)}, u32[]{:S(2)}, u32[]{:S(2)}) async-start(bf16[64,24,128]{2,1,0:T(8,128)(2,1)} %bitcast.29), calls=%async_computation.2 | async-start | bytes 786432 | tf_op jit(solution)/shard_map/all_to_all | solution.py:424
  99.6 13.3 %collective-permute-start.4 = (bf16[1440,128]{1,0:T(8,128)(2,1)S(1)}, bf16[1440,128]{1,0:T(8,128)(2,1)S(1)}, u32[]{:S(2)}, u32[]{:S(2)}) collective-permute-start(bf16[1440,128]{1,0:T(8,128)(2,1)S(1)} %copy-done.4), channel_id=1, source_target_pairs={{0,2},{1,3},{2,0},{3,1},{4,6},{5,7},{6,4},{7,5},{8,10},{9,11},{10,... | collective-permute-start | bytes 1105928 | tf_op jit(solution)/shard_map/ppermute | solution.py:414
  99.8 21.0 %collective-permute-start.3 = (bf16[1440,128]{1,0:T(8,128)(2,1)S(1)}, bf16[1440,128]{1,0:T(8,128)(2,1)S(1)}, u32[]{:S(2)}, u32[]{:S(2)}) collective-permute-start(bf16[1440,128]{1,0:T(8,128)(2,1)S(1)} %copy-done.4), channel_id=1, source_target_pairs={{0,1},{1,0},{2,3},{3,2},{4,5},{5,4},{6,7},{7,6},{8,9},{9,8},{10,11... | collective-permute-start | bytes 1105928 | tf_op jit(solution)/shard_map/ppermute | solution.py:414
  112.9 7.9 %copy-start.8 = (bf16[1440,128]{1,0:T(8,128)(2,1)}, bf16[1440,128]{1,0:T(8,128)(2,1)S(1)}, u32[]{:S(2)}) copy-start(bf16[1440,128]{1,0:T(8,128)(2,1)S(1)} %collective-permute-done.4.far) | copy-start | bytes 1105924
  112.9 8.0 %collective-permute-start.5 = (bf16[1440,128]{1,0:T(8,128)(2,1)S(1)}, bf16[1440,128]{1,0:T(8,128)(2,1)S(1)}, u32[]{:S(2)}, u32[]{:S(2)}) collective-permute-start(bf16[1440,128]{1,0:T(8,128)(2,1)S(1)} %collective-permute-done.4.far), channel_id=1, source_target_pairs={{0,1},{1,0},{2,3},{3,2},{4,5},{5,4},{6,7},{7,6},{8,9},{9,8},{10,11... | collective-permute-start | bytes 1105928 | tf_op jit(solution)/shard_map/ppermute | solution.py:414
  120.9 0.7 copy-start.3
  120.9 0.8 copy-start.9
  121.7 0.7 copy-start.11

commit v2 on v1

--- a/solution.py
+++ b/solution.py
@@ -35,7 +35,7 @@
 STEPS = HALF // PAIRS
 STRIP = 16
 LOCAL_ROWS = 64
-VMEM_BYTES = 58 << 20
+VMEM_BYTES = 48 << 20
 
 ERF_COEFFICIENTS = (
     7.97884216e-01,
@@ -106,14 +106,15 @@
             for out in range(HALF):
                 spread[channel * QL + ql, channel, out * QL + ql] = 1.0
     spread = spread.reshape(LANES, HALF * LANES)
-    tile = np.einsum("pa,qb,o->pqaob", np.eye(PARTS), np.eye(QL), np.ones(HALF))
-    tile = tile.reshape(PARTS * QL, PARTS, HALF * QL)
-    tile = np.pad(tile, ((0, 0), (0, 0), (0, LANES - HALF * QL))).reshape(PARTS * QL, -1)
-    gather = np.einsum("ci,hu,ta,rs,o->chtrsaiuo", np.eye(HALF), eye, eye, eye, np.ones(HALF))
-    gather = gather.reshape(HALF * 8, 2 * C * C)
-    mask = np.zeros((2 * C * C, LANES))
-    for row in range(2 * C * C):
-        mask[row, row % HALF * QL : (row % HALF + 1) * QL] = 1.0
+    select = np.einsum("ci,hu,ta,rs,op->rtchopiuas", np.eye(HALF), eye, eye, eye, np.eye(HALF))
+    select = select.reshape(2 * C * C, HALF, 8 * HALF)
+    select = np.pad(select, ((0, 0), (0, 0), (0, LANES - 8 * HALF))).reshape(2 * C * C, -1)
+    place = np.einsum(
+        "or,pa,qb,lm->opqlmarb", np.eye(HALF), np.eye(PARTS), np.eye(QL), np.eye(LAYERS)
+    )
+    place = place.reshape(HALF * PARTS * QL * LAYERS, LAYERS * PARTS, HALF * QL)
+    place = np.pad(place, ((0, 0), (0, 0), (0, LANES - HALF * QL)))
+    place = place.reshape(HALF * PARTS * QL * LAYERS, -1)
     held = {
         "zt_fwd": zt_forward,
         "zt_inv": zt_inverse,
@@ -122,9 +123,8 @@
         "x_fwd": x_fwd,
         "x_inv": x_inv,
         "spread": spread,
-        "tile": tile,
-        "mask": mask,
-        "gather": gather,
+        "select": select,
+        "place": place,
     }
     return {name: table.astype(np.float32).astype(jnp.bfloat16) for name, table in held.items()}
 
@@ -137,7 +137,8 @@
     return jnp.dot(left, right, preferred_element_type=jnp.float32)
 
 
-def forward_step(step, block, zt_fwd, y_fwd, modes_ref):
+def forward_step(step, block, zt_table, y_table, modes_ref):
+    zt_fwd = zt_table[...]
     columns = []
     for pair in range(PAIRS):
         rows = []
@@ -145,7 +146,7 @@
             z = dot(block(half, pair), zt_fwd).astype(jnp.bfloat16)
             rows += [z[:, :LANES], z[:, LANES:]]
         columns.append(jnp.concatenate(rows, 0))
-    modes = dot(y_fwd, jnp.concatenate(columns, 1))
+    modes = dot(y_table[...], jnp.concatenate(columns, 1))
     lane = lane_index((MY * 8, LANES))
     for pair in range(PAIRS):
         channel = step * PAIRS + pair
@@ -168,11 +169,22 @@
     def block(half, pair):
         return field_ref[half, pair].reshape(PLANES * Y, ZT)
 
-    forward_step(step, block, zt_ref[...], y_ref[...], modes_ref)
+    forward_step(step, block, zt_ref, y_ref, modes_ref)
 
     @pl.when(step == STEPS - 1)
     def _():
         out_ref[...] = modes_ref[...].reshape(GROUPS * 8, LANES).astype(jnp.bfloat16)
+
+
+IN_VMEM = pl.BlockSpec(memory_space=pltpu.VMEM)
+
+
+def in_vmem(arrays):
+    return [pltpu.with_memory_space_constraint(array, pltpu.VMEM) for array in arrays]
+
+
+def in_hbm(array):
+    return pltpu.with_memory_space_constraint(array, pltpu.HBM)
 
 
 def whole(shape):
@@ -191,13 +203,13 @@
     return pl.pallas_call(
         forward_kernel,
         grid=(STEPS,),
-        in_specs=[field_spec(), whole(tables["zt_fwd"].shape), whole(tables["y_fwd"].shape)],
+        in_specs=[field_spec(), IN_VMEM, IN_VMEM],
         out_specs=whole(MESSAGE),
         out_shape=jax.ShapeDtypeStruct(MESSAGE, jnp.bfloat16),
         scratch_shapes=[MODES],
         compiler_params=pltpu.CompilerParams(vmem_limit_bytes=VMEM_BYTES),
         name="forward_zt_y",
-    )(field, tables["zt_fwd"], tables["y_fwd"])
+    )(in_hbm(field), *in_vmem((tables["zt_fwd"], tables["y_fwd"])))
 
 
 def gelu(x):
@@ -209,7 +221,7 @@
     return h + h * jnp.tanh(x * p)
 
 
-def inverse_step(step, modes_ref, local_ref, y_inv, zt_inv, out_ref):
+def inverse_step(step, modes_ref, local_ref, y_table, zt_table, out_ref):
     lane = lane_index((MY * 8, LANES))
     columns = []
     for pair in range(PAIRS):
@@ -220,7 +232,8 @@
             moved = pltpu.roll(modes_ref[:, qh].reshape(MY * 8, LANES), shift, 1)
             value = jnp.where((lane >= qh * QL) & (lane < qh * QL + QL), moved, value)
         columns.append(value.astype(jnp.bfloat16))
-    back = dot(y_inv, jnp.concatenate(columns, 1)).astype(jnp.bfloat16)
+    back = dot(y_table[...], jnp.concatenate(columns, 1)).astype(jnp.bfloat16)
+    zt_inv = zt_table[...]
     span = PLANES * Y
     results = {}
     for pair in range(PAIRS):
@@ -239,48 +252,35 @@
     modes_ref[...] = message_ref[...].astype(jnp.float32).reshape(MY, QH, 8, LANES)
 
 
-def inverse_kernel(message_ref, local_ref, y_ref, zt_ref, out_ref, modes_ref):
+def inverse_kernel(local_ref, message_ref, y_ref, zt_ref, out_ref, modes_ref):
     step = pl.program_id(0)
 
     @pl.when(step == 0)
     def _():
         load_modes(message_ref, modes_ref)
 
-    inverse_step(step, modes_ref, local_ref, y_ref[...], zt_ref[...], out_ref)
+    inverse_step(step, modes_ref, local_ref, y_ref, zt_ref, out_ref)
 
 
 FIELD = (2, HALF, PLANES, Y, ZT)
 
 
 def inverse_call(message, local, tables):
+    held = [message, tables["y_inv"], tables["zt_inv"]]
     return pl.pallas_call(
         inverse_kernel,
         grid=(STEPS,),
-        in_specs=[
-            whole(MESSAGE),
-            field_spec(),
-            whole(tables["y_inv"].shape),
-            whole(tables["zt_inv"].shape),
-        ],
+        in_specs=[field_spec()] + [IN_VMEM] * 3,
         out_specs=field_spec(),
-        out_shape=jax.ShapeDtypeStruct(FIELD, jnp.bfloat16),
+        out_shape=pltpu.HBM(FIELD, jnp.bfloat16),
         scratch_shapes=[MODES],
         compiler_params=pltpu.CompilerParams(vmem_limit_bytes=VMEM_BYTES),
         name="inverse_zt_y",
-    )(message, local, tables["y_inv"], tables["zt_inv"])
+    )(in_hbm(local), *in_vmem(held))
 
 
 def turn_kernel(
-    message_ref,
-    local_ref,
-    y_inv_ref,
-    zt_inv_ref,
-    zt_ref,
-    y_ref,
-    out_ref,
-    send_ref,
-    modes_ref,
-    next_ref,
+    local_ref, message_ref, y_inv, zt_inv, zt_fwd, y_fwd, out_ref, send_ref, modes_ref, next_ref
 ):
     step = pl.program_id(0)
 
@@ -289,10 +289,12 @@
         load_modes(message_ref, modes_ref)
         next_ref[...] = jnp.zeros_like(next_ref)
 
-    results = inverse_step(step, modes_ref, local_ref, y_inv_ref[...], zt_inv_ref[...], out_ref)
-    forward_step(
-        step, lambda half, pair: results[half, pair], zt_ref[...], y_ref[...], next_ref
-    )
+    results = inverse_step(step, modes_ref, local_ref, y_inv, zt_inv, out_ref)
+
+    def block(half, pair):
+        return results[half, pair]
+
+    forward_step(step, block, zt_fwd, y_fwd, next_ref)
 
     @pl.when(step == STEPS - 1)
     def _():
@@ -300,24 +302,24 @@
 
 
 def turn_call(message, local, tables):
-    held = [tables[name] for name in ("y_inv", "zt_inv", "zt_fwd", "y_fwd")]
+    held = [message] + [tables[name] for name in ("y_inv", "zt_inv", "zt_fwd", "y_fwd")]
     return pl.pallas_call(
         turn_kernel,
         grid=(STEPS,),
-        in_specs=[whole(MESSAGE), field_spec()] + [whole(t.shape) for t in held],
+        in_specs=[field_spec()] + [IN_VMEM] * len(held),
         out_specs=[field_spec(), whole(MESSAGE)],
         out_shape=[
-            jax.ShapeDtypeStruct(FIELD, jnp.bfloat16),
+            pltpu.HBM(FIELD, jnp.bfloat16),
             jax.ShapeDtypeStruct(MESSAGE, jnp.bfloat16),
         ],
         scratch_shapes=[MODES, MODES],
         compiler_params=pltpu.CompilerParams(vmem_limit_bytes=VMEM_BYTES),
         name="inverse_then_forward",
-    )(message, local, *held)
+    )(in_hbm(local), *in_vmem(held))
 
 
 def mix_kernel(
-    place_ref, message_ref, own, near, far, across, x_ref, inv_ref, spread_ref, out_ref, sums_ref
+    place_ref, message_ref, x_table, spread_table, weights_ref, inv_ref, out_ref, sums_ref
 ):
     span = OWNERS * 8
     message = message_ref[...].astype(jnp.float32).reshape(OWNERS, PARTS * 8, LANES)
@@ -325,19 +327,20 @@
         message[:, part * 8 : part * 8 + 8].reshape(span, LANES).astype(jnp.bfloat16)
         for part in range(PARTS)
     ]
+    pieces = jnp.concatenate(pieces, 1)
     group_rows = 2 * ROWS
-    for distance, weights in enumerate((own, near, far, across)):
+    for distance in range(KX_GROUPS):
         group = place_ref[0] ^ distance
-        table = x_ref[pl.ds(pl.multiple_of(group * group_rows, group_rows), group_rows), :]
-        modes = dot(table, jnp.concatenate(pieces, 1)).astype(jnp.bfloat16)
+        table = x_table[pl.ds(pl.multiple_of(group * group_rows, group_rows), group_rows), :]
+        modes = dot(table, pieces).astype(jnp.bfloat16)
         rows = [modes[:, part * LANES : (part + 1) * LANES] for part in range(PARTS)]
-        spread = dot(jnp.concatenate(rows, 0), spread_ref[...])
+        spread = dot(jnp.concatenate(rows, 0), spread_table[...])
         for part in range(PARTS):
             for out_half in range(2):
                 totals = [None, None]
                 for c10 in range(HALF):
                     at = ((c10 * PARTS + part) * 2 + out_half) * ROWS
-                    weight = weights[at : at + ROWS, :].astype(jnp.float32)
+                    weight = weights_ref[distance, at : at + ROWS, :].astype(jnp.float32)
                     for kind in range(2):
                         top = part * group_rows + kind * ROWS
                         term = spread[top : top + ROWS, c10 * LANES : (c10 + 1) * LANES] * weight
@@ -356,67 +359,73 @@
 
 
 def mix_call(place, message, weights, tables):
-    held = [tables["x_fwd"], tables["x_inv"], tables["spread"]]
+    held = [message, tables["x_fwd"], tables["spread"], tables["x_inv"]]
     return pl.pallas_call(
         mix_kernel,
         grid=(1,),
-        in_specs=[pl.BlockSpec(memory_space=pltpu.SMEM), whole(MESSAGE)]
-        + [whole(w.shape) for w in weights]
-        + [whole(t.shape) for t in held],
+        in_specs=[pl.BlockSpec(memory_space=pltpu.SMEM)] + [IN_VMEM] * 5,
         out_specs=whole(MESSAGE),
         out_shape=jax.ShapeDtypeStruct(MESSAGE, jnp.bfloat16),
         scratch_shapes=[pltpu.VMEM((KX_GROUPS * 4 * ROWS, PARTS * LANES), jnp.float32)],
         compiler_params=pltpu.CompilerParams(vmem_limit_bytes=VMEM_BYTES),
         name="mix_x",
-    )(place, message, *weights, *held)
-
-
-def arrange_kernel(weight_ref, tile_ref, mask_ref, gather_ref, out_ref, rows_ref):
-    own = mask_ref[...]
-    for kx in range(KX_PER):
-        tiled = lax.dot_general(
-            weight_ref[0, kx],
-            tile_ref[...],
+    )(place, *in_vmem(held[:3] + [weights] + held[3:]))
+
+
+WEIGHT_ROWS = HALF * PARTS * 2 * ROWS
+WEIGHTS = (KX_GROUPS, WEIGHT_ROWS, LANES)
+
+
+def arrange_kernel(own, near, far, across, select_ref, place_ref, first_ref, second_ref, rows_ref):
+    rows = PARTS * QL * LAYERS
+    for distance, weights in enumerate((own, near, far, across)):
+        split = dot(weights[...].reshape(KX_PER * rows, 2 * C * C), select_ref[...])
+        columns = []
+        for kx in range(KX_PER):
+            block = split[kx * rows : (kx + 1) * rows]
+            stacked = [block[:, out * LANES : (out + 1) * LANES] for out in range(HALF)]
+            columns.append(jnp.concatenate(stacked, 0).astype(jnp.bfloat16))
+        moved = lax.dot_general(
+            jnp.concatenate(columns, 1),
+            place_ref[...],
             (((0,), (0,)), ((), ())),
             preferred_element_type=jnp.float32,
         )
-        kept = [
-            tiled[:, part * LANES : (part + 1) * LANES].astype(jnp.bfloat16) * own
-            for part in range(PARTS)
-        ]
-        moved = dot(gather_ref[...], jnp.concatenate(kept, 1))
-        for c10 in range(HALF):
+        for layer, out_ref in enumerate((first_ref, second_ref)):
             for part in range(PARTS):
-                start = (c10 * PARTS + part) * 2 * ROWS
-                rows_ref[pl.ds(start + kx, 8, stride=KX_PER), :] = moved[
-                    c10 * 8 : c10 * 8 + 8, part * LANES : (part + 1) * LANES
-                ]
-    out_ref[...] = rows_ref[...].astype(jnp.bfloat16)
-
-
-def arrange_weights(weights, layer, tables):
-    shape = (HALF * PARTS * 2 * ROWS, LANES)
-    held = [tables["tile"], tables["mask"], tables["gather"]]
+                lane = (layer * PARTS + part) * LANES
+                for kx in range(KX_PER):
+                    for c10 in range(HALF):
+                        row = kx * LANES + c10 * 8
+                        start = (c10 * PARTS + part) * 2 * ROWS + kx
+                        rows_ref[layer, pl.ds(start, 8, stride=KX_PER), :] = moved[
+                            row : row + 8, lane : lane + LANES
+                        ]
+            out_ref[distance] = rows_ref[layer].astype(jnp.bfloat16)
+
+
+def arrange_weights(shards, tables):
+    held = shards + [tables["select"], tables["place"]]
     return pl.pallas_call(
         arrange_kernel,
         grid=(1,),
-        in_specs=[pl.BlockSpec((1,) + weights.shape[1:], lambda k: (layer, 0, 0, 0))]
-        + [whole(t.shape) for t in held],
-        out_specs=whole(shape),
-        out_shape=jax.ShapeDtypeStruct(shape, jnp.bfloat16),
-        scratch_shapes=[pltpu.VMEM(shape, jnp.float32)],
+        in_specs=[IN_VMEM] * len(held),
+        out_specs=[IN_VMEM] * LAYERS,
+        out_shape=[pltpu.VMEM(WEIGHTS, jnp.bfloat16)] * LAYERS,
+        scratch_shapes=[pltpu.VMEM((LAYERS, WEIGHT_ROWS, LANES), jnp.float32)],
         compiler_params=pltpu.CompilerParams(vmem_limit_bytes=VMEM_BYTES),
         name="arrange_weights",
-    )(weights, *held)
+    )(*in_vmem(held))
 
 
 def swap(value, distance):
     return lax.ppermute(value, "batch", [(i, i ^ distance) for i in range(KX_GROUPS)])
 
 
-def spread_weights(own):
+def gather_weights(weights):
+    own = jnp.transpose(weights, (1, 2, 0, 3))
     far = swap(own, 2)
-    return own, swap(own, 1), far, swap(far, 1)
+    return [own, swap(own, 1), far, swap(far, 1)]
 
 
 def exchange(message):
@@ -457,11 +466,11 @@
         grid=(PLANES, Y // LOCAL_ROWS),
         in_specs=[pl.BlockSpec(memory_space=pltpu.SMEM), whole((C, C)), spec],
         out_specs=spec,
-        out_shape=jax.ShapeDtypeStruct(FIELD, jnp.bfloat16),
+        out_shape=pltpu.HBM(FIELD, jnp.bfloat16),
         scratch_shapes=[pltpu.VMEM((C * STRIP, C * STRIP), jnp.bfloat16)],
         compiler_params=pltpu.CompilerParams(vmem_limit_bytes=VMEM_BYTES),
         name="local_mixing",
-    )(offset, weight.T, current)
+    )(offset, weight.T, in_hbm(current))
 
 
 def after(value, *others):
@@ -472,18 +481,14 @@
     tables = {name: jnp.asarray(table) for name, table in build_tables().items()}
     place = lax.axis_index("batch").astype(jnp.int32).reshape(1)
     field = field.reshape(FIELD)
-    own = arrange_weights(spectral_weight, 0, tables)
-    weights = spread_weights(own)
-    message = forward_call(field, dict(tables, zt_fwd=after(tables["zt_fwd"], own)))
-    local = local_term(field, after(local_weight[0], message), bias[0])
-    received = after(exchange(message), local)
-    back = mix_call(place, received, weights, tables)
-    own = arrange_weights(after(spectral_weight, back), 1, tables)
-    weights = spread_weights(own)
-    current, message = turn_call(after(exchange(back), own), local, tables)
+    shards = gather_weights(spectral_weight)
+    message = forward_call(field, tables)
+    weights = arrange_weights(shards, dict(tables, place=after(tables["place"], message)))
+    back = mix_call(place, exchange(message), weights[0], tables)
+    local = local_term(field, after(local_weight[0], back), bias[0])
+    current, message = turn_call(exchange(back), local, tables)
     local = local_term(current, local_weight[1], bias[1])
-    received = after(exchange(message), local)
-    back = mix_call(place, received, weights, tables)
+    back = mix_call(place, after(exchange(message), local), weights[1], tables)
     return inverse_call(exchange(back), local, tables).reshape(1, C, PLANES, Y, ZT)
 
 

time: 169 us -> 155 us (0.917)
  waiting for transfers between devices: 29.8 us -> 19.4 us
  blocking collectives: 28.5 us -> 21.4 us
  starting transfers between devices: 30.2 us -> 36.2 us
  Pallas kernels: 71.1 us -> 68.3 us
    ppermute x6 -> x3, waiting for transfers between devices: 13.1 us -> 3.2 us  [swap(): lax.ppermute(value, 'batch', [(i, i ^ distance) for i in range(KX_GROUPS)])]
    all_to_all x1, blocking collectives: 28.5 us -> 21.4 us  [exchange(): lax.all_to_all(grouped, 'space', split_axis=0, concat_axis=0, tiled=True)]
    all_to_all x3, starting transfers between devices: 27.8 us -> 34 us  [exchange(): lax.all_to_all(grouped, 'space', split_axis=0, concat_axis=0, tiled=True)]
    pallas_call x2, Pallas kernels: 8.37 us -> 4.19 us  [mix_call(): pl.pallas_call(mix_kernel, grid=(1,), in_specs=[pl.BlockSpec(memory_space...]
    unnamed x31 -> x40, local copies, waits for them, and re-layouts: 6.9 us -> 9.07 us
    pallas_call x5 -> x4, Pallas kernels: 48.3 us -> 49.4 us  [the longest x1 17.8 us: turn_call(): pl.pallas_call(turn_kernel, grid=(STEPS,), in_specs=[field_spec()] + [IN_...]
  transfers between devices with their start and end apart: 9 -> 6, of which waited for: 3 -> 4; matrix products, arithmetic and copies ran while one was open for 2% -> 0% of each run, Pallas kernels for 16% -> 22%
where the time goes in v2:
time: 155 us; the launch traced here: 154 us
  Pallas kernels  68.3 us (44%)
  starting transfers between devices  36.2 us (23%)
  blocking collectives  21.4 us (14%)
  waiting for transfers between devices  19.4 us (13%)
  local copies, waits for them, and re-layouts  9.1 us (6%)
    all_to_all x3, starting transfers between devices, exchange(): lax.all_to_all(grouped, 'space', split_axis=0, concat_axis=0, tiled=True)  34 us
    all_to_all x1, blocking collectives, exchange(): lax.all_to_all(grouped, 'space', split_axis=0, concat_axis=0, tiled=True)  21.4 us
    pallas_call x1, Pallas kernels, turn_call(): pl.pallas_call(turn_kernel, grid=(STEPS,), in_specs=[field_spec()] + [IN_...  17.8 us
    all_to_all x3, waiting for transfers between devices, exchange(): lax.all_to_all(grouped, 'space', split_axis=0, concat_axis=0, tiled=True)  16.2 us
    pallas_call x2, Pallas kernels, local_term(): pl.pallas_call(local_kernel, grid=(PLANES, Y // LOCAL_ROWS), in_specs=[pl...  14.7 us
    pallas_call x1, Pallas kernels, inverse_call(): pl.pallas_call(inverse_kernel, grid=(STEPS,), in_specs=[field_spec()] + [...  12.8 us
    pallas_call x1, Pallas kernels, arrange_weights(): pl.pallas_call(arrange_kernel, grid=(1,), in_specs=[IN_VMEM] * len(held),...  10.5 us
    unnamed x40, local copies, waits for them, and re-layouts  9.07 us
  transfers between devices with their start and end apart: 6, of which 4 were waited for; matrix products, arithmetic and copies ran while one was open for 0% of the time, Pallas kernels for 22%

profile of v2, /device:TPU:2, one launch (start us, length us, event | category | flops | bytes accessed | tf_op | source)
XLA Modules:
  0.0 154.5 jit_solution(2071842822881835390)
XLA Ops:
  0.0 1.6 %collective-permute-start.1 = (bf16[6,36,2,800]{3,2,1,0:T(2,128)(2,1)}, bf16[6,36,2,800]{3,2,1,0:T(2,128)(2,1)}, u32[]{:S(2)}, u32[]{:S(2)}) collective-permute-start(bf16[6,36,2,800]{3,2,1,0:T(2,128)(2,1)} %bitcast.26), channel_id=1, source_target_pairs={{0,2},{1,3},{2,0},{3,1},{4,6},{5,7},{6,4},{7,5},{8,10},{9,11},{10,... | collective-permute-start | bytes 2073608 | tf_op jit(solution)/shard_map/ppermute | solution.py:422
  1.6 1.0 copy-done.2
  2.6 0.9 copy-done.12
  3.5 8.2 %forward_zt_y.1 = bf16[1536,128]{1,0:T(8,128)(2,1)} custom-call(bf16[2,10,2,128,512]{4,3,2,1,0:T(8,128)(2,1)} %bitcast.31, bf16[512,256]{1,0:T(8,128)(2,1)S(1)} %copy-done.12, bf16[192,1024]{1,0:T(8,128)(2,1)S(1)} %copy-done.2), custom_call_target="tpu_custom_call" | custom-call | tf_op jit(solution)/shard_map/forward_zt_y/pallas_call | solution.py:203
  11.7 14.5 %all-to-all-start = ((bf16[64,24,128]{2,1,0:T(8,128)(2,1)}), bf16[64,24,128]{2,1,0:T(8,128)(2,1)S(1)}, u32[]{:S(2)}, u32[]{:S(2)}) async-start(bf16[64,24,128]{2,1,0:T(8,128)(2,1)} %bitcast.7), calls=%async_computation | async-start | bytes 786432 | tf_op jit(solution)/shard_map/all_to_all | solution.py:433
  26.2 0.0 copy-start.18
  26.2 0.1 collective-permute-start
  26.3 0.0 collective-permute-done.1.far
  26.3 0.5 collective-permute-start.2
  26.8 2.1 %collective-permute-done.near = bf16[6,36,2,800]{3,2,1,0:T(2,128)(2,1)} collective-permute-done((bf16[6,36,2,800]{3,2,1,0:T(2,128)(2,1)}, bf16[6,36,2,800]{3,2,1,0:T(2,128)(2,1)}, u32[]{:S(2)}, u32[]{:S(2)}) %collective-permute-start) | collective-permute-done | bytes 691232 | tf_op jit(solution)/shard_map/ppermute | solution.py:422
  28.9 1.1 collective-permute-done.2.across
  30.0 0.0 copy-done.1
  30.0 1.2 copy-done.10
  31.3 1.1 copy-done.16
  32.4 10.5 %arrange_weights.1 = (bf16[4,1440,128]{2,1,0:T(8,128)(2,1)S(1)}, bf16[4,1440,128]{2,1,0:T(8,128)(2,1)S(1)}) custom-call(bf16[6,36,2,800]{3,2,1,0:T(2,128)(2,1)S(1)} %bitcast.28, bf16[6,36,2,800]{3,2,1,0:T(2,128)(2,1)} %collective-permute-done.near, bf16[6,36,2,800]{3,2,1,0:T(2,128)(2,1)} %collective-permute-done.1.far, ...), custom_call_target="tpu_custom_call" | custom-call | tf_op jit(solution)/shard_map/arrange_weights/pallas_call | solution.py:409
  43.0 0.0 copy-start.5
  43.0 1.1 copy-done.5
  44.1 1.1 copy-done.7
  45.2 0.0 all-to-all-done
  45.2 0.0 copy-done.4
  45.2 0.0 copy-done.9
  45.2 0.0 copy-done.14
  45.2 0.0 copy-start.8
  45.2 1.4 copy-done.8
  46.6 2.5 %mix_x.2 = bf16[1536,128]{1,0:T(8,128)(2,1)} custom-call(s32[1]{0:T(128)} %bitcast.5.place_ref, bf16[1536,128]{1,0:T(8,128)(2,1)S(1)} %bitcast.23, bf16[192,512]{1,0:T(8,128)(2,1)S(1)} %copy-done.14, bf16[128,1280]{1,0:T(8,128)(2,1)S(1)} %copy-done.9, bf16[4,1440,128]{2,1,0:T(8,128)(2,1)S(1)} %copy-done.8, bf16[512,384]{1,0:T(8,128)(2,1)S(1)} %copy-done.4), custom_call_target="tpu_custom_call" | custom-call | tf_op jit(solution)/shard_map/mix_x/pallas_call | solution.py:363
  49.0 12.7 %all-to-all-start.1 = ((bf16[64,24,128]{2,1,0:T(8,128)(2,1)}), bf16[64,24,128]{2,1,0:T(8,128)(2,1)S(1)}, u32[]{:S(2)}, u32[]{:S(2)}) async-start(bf16[64,24,128]{2,1,0:T(8,128)(2,1)} %bitcast.11), calls=%async_computation.1 | async-start | bytes 786432 | tf_op jit(solution)/shard_map/all_to_all | solution.py:433
  61.8 0.0 copy-done.17
  61.8 0.1 copy.17
  61.9 0.0 copy-done.18
  61.9 0.0 copy-start
  62.0 0.0 copy-start.3
  62.0 0.0 copy-start.11
  62.0 0.0 copy-start.13
  62.0 7.3 %local_mixing.2.local_ref = bf16[2,10,2,128,512]{4,3,2,1,0:T(8,128)(2,1)} custom-call(f32[20]{0:T(128)S(1)} %get-tuple-element.21.offset_ref, bf16[20,20]{1,0:T(8,128)(2,1)S(1)} %bitcast.30, bf16[2,10,2,128,512]{4,3,2,1,0:T(8,128)(2,1)} %bitcast.32), custom_call_target="tpu_custom_call" | custom-call | tf_op jit(solution)/shard_map/local_mixing/pallas_call | solution.py:464
  69.3 8.3 %all-to-all-done.1 = bf16[64,24,128]{2,1,0:T(8,128)(2,1)S(1)} async-done(((bf16[64,24,128]{2,1,0:T(8,128)(2,1)}), bf16[64,24,128]{2,1,0:T(8,128)(2,1)S(1)}, u32[]{:S(2)}, u32[]{:S(2)}) %all-to-all-start.1) | async-done | bytes 393248 | tf_op jit(solution)/shard_map/all_to_all | solution.py:433
  77.7 0.0 copy-done
  77.7 0.0 copy-done.3
  77.7 0.0 copy-done.11
  77.7 0.0 copy-done.13
  77.7 17.8 %inverse_then_forward.1 = (bf16[2,10,2,128,512]{4,3,2,1,0:T(8,128)(2,1)}, bf16[1536,128]{1,0:T(8,128)(2,1)}) custom-call(bf16[2,10,2,128,512]{4,3,2,1,0:T(8,128)(2,1)} %local_mixing.2.local_ref, bf16[1536,128]{1,0:T(8,128)(2,1)S(1)} %bitcast.22, bf16[1024,192]{1,0:T(8,128)(2,1)S(1)} %copy-done, bf16[256,512]{1,0:T(8,128)(2,1)S(1)} %copy-done.11, ...), custom_call_target="tpu_custom_call" | custom-call | tf_op jit(solution)/shard_map/inverse_then_forward/pallas_call | solution.py:306
  95.5 6.8 %all-to-all-start.2 = ((bf16[64,24,128]{2,1,0:T(8,128)(2,1)}), bf16[64,24,128]{2,1,0:T(8,128)(2,1)S(1)}, u32[]{:S(2)}, u32[]{:S(2)}) async-start(bf16[64,24,128]{2,1,0:T(8,128)(2,1)} %bitcast.13), calls=%async_computation.2 | async-start | bytes 786432 | tf_op jit(solution)/shard_map/all_to_all | solution.py:433
  102.3 0.1 copy.16
  102.4 7.4 %local_mixing.3.local_ref = bf16[2,10,2,128,512]{4,3,2,1,0:T(8,128)(2,1)} custom-call(f32[20]{0:T(128)S(1)} %get-tuple-element.22.offset_ref, bf16[20,20]{1,0:T(8,128)(2,1)S(1)} %bitcast.29, bf16[2,10,2,128,512]{4,3,2,1,0:T(8,128)(2,1)} %get-tuple-element.15.field_ref), custom_call_target="tpu_custom_call" | custom-call | tf_op jit(solution)/shard_map/local_mixing/pallas_call | solution.py:464
  109.8 7.8 %all-to-all-done.2 = bf16[64,24,128]{2,1,0:T(8,128)(2,1)S(1)} async-done(((bf16[64,24,128]{2,1,0:T(8,128)(2,1)}), bf16[64,24,128]{2,1,0:T(8,128)(2,1)S(1)}, u32[]{:S(2)}, u32[]{:S(2)}) %all-to-all-start.2) | async-done | bytes 393248 | tf_op jit(solution)/shard_map/all_to_all | solution.py:433
  117.6 0.9 copy-done.15
  118.5 1.7 %mix_x.3 = bf16[1536,128]{1,0:T(8,128)(2,1)S(1)} custom-call(s32[1]{0:T(128)} %bitcast.5.place_ref, bf16[1536,128]{1,0:T(8,128)(2,1)S(1)} %bitcast.24, bf16[192,512]{1,0:T(8,128)(2,1)S(1)} %copy-done.15, bf16[128,1280]{1,0:T(8,128)(2,1)S(1)} %copy-done.9, bf16[4,1440,128]{2,1,0:T(8,128)(2,1)S(1)} %copy-done.6, bf16[512,384]{1,0:T(8,128)(2,1)S(1)} %copy-done.4), custom_call_target="tpu_custom_call" | custom-call | tf_op jit(solution)/shard_map/mix_x/pallas_call | solution.py:363
  120.2 21.4 %all_to_all.20 = bf16[64,24,128]{2,1,0:T(8,128)(2,1)S(1)} all-to-all(bf16[64,24,128]{2,1,0:T(8,128)(2,1)S(1)} %bitcast.25), channel_id=1, replica_groups=mesh['space'=64,'batch'=4] {'space'}, dimensions={0} | all-to-all | bytes 786432 | tf_op jit(solution)/shard_map/all_to_all | solution.py:433
  141.6 12.8 %inverse_zt_y.1 = bf16[2,10,2,128,512]{4,3,2,1,0:T(8,128)(2,1)} custom-call(bf16[2,10,2,128,512]{4,3,2,1,0:T(8,128)(2,1)} %local_mixing.3.local_ref, bf16[1536,128]{1,0:T(8,128)(2,1)S(1)} %bitcast.21, bf16[1024,192]{1,0:T(8,128)(2,1)S(1)} %copy-done, bf16[256,512]{1,0:T(8,128)(2,1)S(1)} %copy-done.11), custom_call_target="tpu_custom_call" | custom-call | tf_op jit(solution)/shard_map/inverse_zt_y/pallas_call | solution.py:270
  (15 shorter events, 0.0 us)
Async XLA Ops:
  0.0 30.0 %copy-start.1 = (bf16[800,1280]{1,0:T(8,128)(2,1)S(1)}, bf16[800,1280]{1,0:T(8,128)(2,1)}, u32[]{:S(2)}) copy-start(bf16[800,1280]{1,0:T(8,128)(2,1)} %constant.29.clone.select_ref) | copy-start | bytes 6144004
  0.0 26.3 %collective-permute-start.1 = (bf16[6,36,2,800]{3,2,1,0:T(2,128)(2,1)}, bf16[6,36,2,800]{3,2,1,0:T(2,128)(2,1)}, u32[]{:S(2)}, u32[]{:S(2)}) collective-permute-start(bf16[6,36,2,800]{3,2,1,0:T(2,128)(2,1)} %bitcast.26), channel_id=1, source_target_pairs={{0,2},{1,3},{2,0},{3,1},{4,6},{5,7},{6,4},{7,5},{8,10},{9,11},{10,... | collective-permute-start | bytes 2073608 | tf_op jit(solution)/shard_map/ppermute | solution.py:422
  1.6 1.0 copy-start.2
  2.6 0.9 copy-start.12
  3.5 41.7 %copy-start.4 = (bf16[512,384]{1,0:T(8,128)(2,1)S(1)}, bf16[512,384]{1,0:T(8,128)(2,1)}, u32[]{:S(2)}) copy-start(bf16[512,384]{1,0:T(8,128)(2,1)} %constant.27.clone.inv_ref) | copy-start | bytes 1179652
  3.5 41.7 %copy-start.9 = (bf16[128,1280]{1,0:T(8,128)(2,1)S(1)}, bf16[128,1280]{1,0:T(8,128)(2,1)}, u32[]{:S(2)}) copy-start(bf16[128,1280]{1,0:T(8,128)(2,1)} %constant.28.clone.spread_table) | copy-start | bytes 983044
  3.5 41.7 %copy-start.14 = (bf16[192,512]{1,0:T(8,128)(2,1)S(1)}, bf16[192,512]{1,0:T(8,128)(2,1)}, u32[]{:S(2)}) copy-start(bf16[192,512]{1,0:T(8,128)(2,1)} %constant.26.clone.x_table) | copy-start | bytes 589828
  11.7 50.1 %copy-start.17 = (bf16[2,20,20]{2,0,1:T(2,128)(2,1)S(1)}, bf16[2,20,20]{2,0,1:T(2,128)(2,1)}, u32[]{:S(2)}) copy-start(bf16[2,20,20]{2,0,1:T(2,128)(2,1)} %param.15) | copy-start | bytes 4804
  11.7 33.4 %all-to-all-start = ((bf16[64,24,128]{2,1,0:T(8,128)(2,1)}), bf16[64,24,128]{2,1,0:T(8,128)(2,1)S(1)}, u32[]{:S(2)}, u32[]{:S(2)}) async-start(bf16[64,24,128]{2,1,0:T(8,128)(2,1)} %bitcast.7), calls=%async_computation | async-start | bytes 786432 | tf_op jit(solution)/shard_map/all_to_all | solution.py:433
  26.2 35.7 %copy-start.18 = (f32[2,20]{1,0:T(2,128)S(1)}, f32[2,20]{1,0:T(2,128)}, u32[]{:S(2)}) copy-start(f32[2,20]{1,0:T(2,128)} %param.16) | copy-start | bytes 484
  26.2 2.7 %collective-permute-start = (bf16[6,36,2,800]{3,2,1,0:T(2,128)(2,1)}, bf16[6,36,2,800]{3,2,1,0:T(2,128)(2,1)}, u32[]{:S(2)}, u32[]{:S(2)}) collective-permute-start(bf16[6,36,2,800]{3,2,1,0:T(2,128)(2,1)} %bitcast.27), channel_id=1, source_target_pairs={{0,1},{1,0},{2,3},{3,2},{4,5},{5,4},{6,7},{7,6},{8,9},{9,8},{10,11... | collective-permute-start | bytes 2073608 | tf_op jit(solution)/shard_map/ppermute | solution.py:422
  26.3 3.7 %collective-permute-start.2 = (bf16[6,36,2,800]{3,2,1,0:T(2,128)(2,1)}, bf16[6,36,2,800]{3,2,1,0:T(2,128)(2,1)}, u32[]{:S(2)}, u32[]{:S(2)}) collective-permute-start(bf16[6,36,2,800]{3,2,1,0:T(2,128)(2,1)} %collective-permute-done.1.far), channel_id=1, source_target_pairs={{0,1},{1,0},{2,3},{3,2},{4,5},{5,4},{6,7},{7,6},{8,9},{9,8},{10,11... | collective-permute-start | bytes 2073608 | tf_op jit(solution)/shard_map/ppermute | solution.py:422
  30.0 1.2 copy-start.10
  31.3 1.1 copy-start.16
  43.0 1.1 copy-start.5
  44.1 1.1 copy-start.7
  45.2 1.4 copy-start.8
  49.0 28.6 %all-to-all-start.1 = ((bf16[64,24,128]{2,1,0:T(8,128)(2,1)}), bf16[64,24,128]{2,1,0:T(8,128)(2,1)S(1)}, u32[]{:S(2)}, u32[]{:S(2)}) async-start(bf16[64,24,128]{2,1,0:T(8,128)(2,1)} %bitcast.11), calls=%async_computation.1 | async-start | bytes 786432 | tf_op jit(solution)/shard_map/all_to_all | solution.py:433
  61.9 15.7 %copy-start = (bf16[1024,192]{1,0:T(8,128)(2,1)S(1)}, bf16[1024,192]{1,0:T(8,128)(2,1)}, u32[]{:S(2)}) copy-start(bf16[1024,192]{1,0:T(8,128)(2,1)} %constant.25.clone.y_inv.y_ref) | copy-start | bytes 1179652
  62.0 15.7 %copy-start.3 = (bf16[192,1024]{1,0:T(8,128)(2,1)S(1)}, bf16[192,1024]{1,0:T(8,128)(2,1)}, u32[]{:S(2)}) copy-start(bf16[192,1024]{1,0:T(8,128)(2,1)} %constant.24.clone.y_ref.y_fwd) | copy-start | bytes 1179652
  62.0 15.7 %copy-start.11 = (bf16[256,512]{1,0:T(8,128)(2,1)S(1)}, bf16[256,512]{1,0:T(8,128)(2,1)}, u32[]{:S(2)}) copy-start(bf16[256,512]{1,0:T(8,128)(2,1)} %constant.23.clone.zt_inv.zt_ref) | copy-start | bytes 786436
  62.0 15.7 %copy-start.13 = (bf16[512,256]{1,0:T(8,128)(2,1)S(1)}, bf16[512,256]{1,0:T(8,128)(2,1)}, u32[]{:S(2)}) copy-start(bf16[512,256]{1,0:T(8,128)(2,1)} %constant.22.clone.zt_ref.zt_fwd) | copy-start | bytes 786436
  95.5 22.1 %all-to-all-start.2 = ((bf16[64,24,128]{2,1,0:T(8,128)(2,1)}), bf16[64,24,128]{2,1,0:T(8,128)(2,1)S(1)}, u32[]{:S(2)}, u32[]{:S(2)}) async-start(bf16[64,24,128]{2,1,0:T(8,128)(2,1)} %bitcast.13), calls=%async_computation.2 | async-start | bytes 786432 | tf_op jit(solution)/shard_map/all_to_all | solution.py:433
  102.4 15.2 %copy-start.6 = (bf16[4,1440,128]{2,1,0:T(8,128)(2,1)S(1)}, bf16[4,1440,128]{2,1,0:T(8,128)(2,1)}, u32[]{:S(2)}) copy-start(bf16[4,1440,128]{2,1,0:T(8,128)(2,1)} %copy-done.5) | copy-start | bytes 4423684
  117.6 0.9 copy-start.15

commit v3 on v2

--- a/solution.py
+++ b/solution.py
@@ -46,7 +46,7 @@
     -1.33447465e-07,
     1.80564042e-09,
 )
-ERF_LIMIT = 31.36
+HALVED_COEFFICIENTS = tuple(2.0 * 4.0**i * c for i, c in enumerate(ERF_COEFFICIENTS))
 
 
 def line_table(length, kept_count):
@@ -80,7 +80,7 @@
     inverse = np.zeros((2 * LANES, ZT))
     inverse[:kept] = cosine.T * doubling[:, None]
     inverse[LANES : LANES + kept] = -sine.T * doubling[:, None]
-    return forward, inverse
+    return forward, 0.5 * inverse
 
 
 def build_tables():
@@ -100,12 +100,8 @@
     x_split = x_inverse.reshape(KX_GROUPS, KX_PER, 2, OWNERS, PLANES, 2)
     x_inv = np.einsum("gmsiuj,ab,c,t->iaujgsbctm", x_split, eye, np.ones(2), np.ones(2))
     x_inv = x_inv.reshape(OWNERS * 8, KX_GROUPS * 4 * ROWS)
-    spread = np.zeros((LANES, HALF, LANES))
-    for channel in range(HALF):
-        for ql in range(QL):
-            for out in range(HALF):
-                spread[channel * QL + ql, channel, out * QL + ql] = 1.0
-    spread = spread.reshape(LANES, HALF * LANES)
+    same = np.tile(np.eye(QL), (HALF, HALF))
+    same = np.pad(same, (0, LANES - HALF * QL))
     select = np.einsum("ci,hu,ta,rs,op->rtchopiuas", np.eye(HALF), eye, eye, eye, np.eye(HALF))
     select = select.reshape(2 * C * C, HALF, 8 * HALF)
     select = np.pad(select, ((0, 0), (0, 0), (0, LANES - 8 * HALF))).reshape(2 * C * C, -1)
@@ -122,7 +118,7 @@
         "y_inv": y_inv,
         "x_fwd": x_fwd,
         "x_inv": x_inv,
-        "spread": spread,
+        "same": same,
         "select": select,
         "place": place,
     }
@@ -177,6 +173,7 @@
 
 
 IN_VMEM = pl.BlockSpec(memory_space=pltpu.VMEM)
+IN_HBM = pl.BlockSpec(memory_space=pltpu.HBM)
 
 
 def in_vmem(arrays):
@@ -205,20 +202,19 @@
         grid=(STEPS,),
         in_specs=[field_spec(), IN_VMEM, IN_VMEM],
         out_specs=whole(MESSAGE),
-        out_shape=jax.ShapeDtypeStruct(MESSAGE, jnp.bfloat16),
+        out_shape=pltpu.HBM(MESSAGE, jnp.bfloat16),
         scratch_shapes=[MODES],
         compiler_params=pltpu.CompilerParams(vmem_limit_bytes=VMEM_BYTES),
         name="forward_zt_y",
     )(in_hbm(field), *in_vmem((tables["zt_fwd"], tables["y_fwd"])))
 
 
-def gelu(x):
-    s = jnp.minimum(x * x, ERF_LIMIT)
-    p = jnp.float32(ERF_COEFFICIENTS[-1])
-    for coefficient in ERF_COEFFICIENTS[-2::-1]:
+def gelu(h):
+    s = h * h
+    p = jnp.float32(HALVED_COEFFICIENTS[-1])
+    for coefficient in HALVED_COEFFICIENTS[-2::-1]:
         p = p * s + jnp.float32(coefficient)
-    h = 0.5 * x
-    return h + h * jnp.tanh(x * p)
+    return h + h * jnp.tanh(h * p)
 
 
 def inverse_step(step, modes_ref, local_ref, y_table, zt_table, out_ref):
@@ -310,7 +306,7 @@
         out_specs=[field_spec(), whole(MESSAGE)],
         out_shape=[
             pltpu.HBM(FIELD, jnp.bfloat16),
-            jax.ShapeDtypeStruct(MESSAGE, jnp.bfloat16),
+            pltpu.HBM(MESSAGE, jnp.bfloat16),
         ],
         scratch_shapes=[MODES, MODES],
         compiler_params=pltpu.CompilerParams(vmem_limit_bytes=VMEM_BYTES),
@@ -319,8 +315,18 @@
 
 
 def mix_kernel(
-    place_ref, message_ref, x_table, spread_table, weights_ref, inv_ref, out_ref, sums_ref
+    place_ref, message_ref, x_hbm, same_hbm, inv_hbm, weights_hbm, out_ref, sums_ref, x_table,
+    same_ref, inv_ref, weights_ref, arrived
 ):
+    pairs = [(x_hbm, x_table), (same_hbm, same_ref)]
+    pairs += [(weights_hbm.at[i], weights_ref.at[i]) for i in range(KX_GROUPS)]
+    pairs.append((inv_hbm, inv_ref))
+    copies = [
+        pltpu.make_async_copy(source, target, arrived.at[i])
+        for i, (source, target) in enumerate(pairs)
+    ]
+    for copy in copies:
+        copy.start()
     span = OWNERS * 8
     message = message_ref[...].astype(jnp.float32).reshape(OWNERS, PARTS * 8, LANES)
     pieces = [
@@ -328,13 +334,22 @@
         for part in range(PARTS)
     ]
     pieces = jnp.concatenate(pieces, 1)
+    copies[0].wait()
+    copies[1].wait()
+    same = same_ref[...].astype(jnp.float32)
+    row = lax.broadcasted_iota(jnp.int32, same.shape, 0)
+    spread_table = [
+        jnp.where((row >= c10 * QL) & (row < c10 * QL + QL), same, 0.0) for c10 in range(HALF)
+    ]
+    spread_table = jnp.concatenate(spread_table, 1).astype(jnp.bfloat16)
     group_rows = 2 * ROWS
     for distance in range(KX_GROUPS):
         group = place_ref[0] ^ distance
         table = x_table[pl.ds(pl.multiple_of(group * group_rows, group_rows), group_rows), :]
         modes = dot(table, pieces).astype(jnp.bfloat16)
         rows = [modes[:, part * LANES : (part + 1) * LANES] for part in range(PARTS)]
-        spread = dot(jnp.concatenate(rows, 0), spread_table[...])
+        spread = dot(jnp.concatenate(rows, 0), spread_table)
+        copies[2 + distance].wait()
         for part in range(PARTS):
             for out_half in range(2):
                 totals = [None, None]
@@ -350,6 +365,7 @@
                     sums_ref[
                         pl.ds(pl.multiple_of(start, 8), ROWS), part * LANES : (part + 1) * LANES
                     ] = totals[kind]
+    copies[6].wait()
     back = dot(inv_ref[...], sums_ref[...].astype(jnp.bfloat16))
     blocks = [
         back[:, part * LANES : (part + 1) * LANES].reshape(OWNERS, 8, LANES)
@@ -359,27 +375,39 @@
 
 
 def mix_call(place, message, weights, tables):
-    held = [message, tables["x_fwd"], tables["spread"], tables["x_inv"]]
+    held = [tables["x_fwd"], tables["same"], tables["x_inv"]]
     return pl.pallas_call(
         mix_kernel,
         grid=(1,),
-        in_specs=[pl.BlockSpec(memory_space=pltpu.SMEM)] + [IN_VMEM] * 5,
+        in_specs=[pl.BlockSpec(memory_space=pltpu.SMEM), IN_VMEM] + [IN_HBM] * 4,
         out_specs=whole(MESSAGE),
-        out_shape=jax.ShapeDtypeStruct(MESSAGE, jnp.bfloat16),
-        scratch_shapes=[pltpu.VMEM((KX_GROUPS * 4 * ROWS, PARTS * LANES), jnp.float32)],
+        out_shape=pltpu.HBM(MESSAGE, jnp.bfloat16),
+        scratch_shapes=[pltpu.VMEM((KX_GROUPS * 4 * ROWS, PARTS * LANES), jnp.float32)]
+        + [pltpu.VMEM(table.shape, table.dtype) for table in held]
+        + [pltpu.VMEM(WEIGHTS, jnp.bfloat16), pltpu.SemaphoreType.DMA((7,))],
         compiler_params=pltpu.CompilerParams(vmem_limit_bytes=VMEM_BYTES),
         name="mix_x",
-    )(place, *in_vmem(held[:3] + [weights] + held[3:]))
+    )(place, *in_vmem([message]), *map(in_hbm, held + [weights]))
 
 
 WEIGHT_ROWS = HALF * PARTS * 2 * ROWS
 WEIGHTS = (KX_GROUPS, WEIGHT_ROWS, LANES)
 
 
-def arrange_kernel(own, near, far, across, select_ref, place_ref, first_ref, second_ref, rows_ref):
+def arrange_kernel(
+    own, near, far, across, select_ref, place_ref, first_ref, second_ref, shards_ref, rows_ref, done_ref, arrived, left
+):
     rows = PARTS * QL * LAYERS
-    for distance, weights in enumerate((own, near, far, across)):
-        split = dot(weights[...].reshape(KX_PER * rows, 2 * C * C), select_ref[...])
+    arriving = [
+        pltpu.make_async_copy(shard, shards_ref.at[i], arrived.at[i])
+        for i, shard in enumerate((own, near, far, across))
+    ]
+    for copy in arriving:
+        copy.start()
+    leaving = []
+    for distance in range(KX_GROUPS):
+        arriving[distance].wait()
+        split = dot(shards_ref[distance].reshape(KX_PER * rows, 2 * C * C), select_ref[...])
         columns = []
         for kx in range(KX_PER):
             block = split[kx * rows : (kx + 1) * rows]
@@ -401,21 +429,34 @@
                         rows_ref[layer, pl.ds(start, 8, stride=KX_PER), :] = moved[
                             row : row + 8, lane : lane + LANES
                         ]
-            out_ref[distance] = rows_ref[layer].astype(jnp.bfloat16)
+            done_ref[layer, distance] = rows_ref[layer].astype(jnp.bfloat16)
+            copy = pltpu.make_async_copy(
+                done_ref.at[layer, distance], out_ref.at[distance], left.at[layer, distance]
+            )
+            copy.start()
+            leaving.append(copy)
+    for copy in leaving:
+        copy.wait()
 
 
 def arrange_weights(shards, tables):
-    held = shards + [tables["select"], tables["place"]]
+    held = [tables["select"], tables["place"]]
     return pl.pallas_call(
         arrange_kernel,
         grid=(1,),
-        in_specs=[IN_VMEM] * len(held),
-        out_specs=[IN_VMEM] * LAYERS,
-        out_shape=[pltpu.VMEM(WEIGHTS, jnp.bfloat16)] * LAYERS,
-        scratch_shapes=[pltpu.VMEM((LAYERS, WEIGHT_ROWS, LANES), jnp.float32)],
+        in_specs=[IN_HBM] * KX_GROUPS + [IN_VMEM] * 2,
+        out_specs=[IN_HBM] * LAYERS,
+        out_shape=[pltpu.HBM(WEIGHTS, jnp.bfloat16)] * LAYERS,
+        scratch_shapes=[
+            pltpu.VMEM((KX_GROUPS,) + shards[0].shape, shards[0].dtype),
+            pltpu.VMEM((LAYERS, WEIGHT_ROWS, LANES), jnp.float32),
+            pltpu.VMEM((LAYERS,) + WEIGHTS, jnp.bfloat16),
+            pltpu.SemaphoreType.DMA((KX_GROUPS,)),
+            pltpu.SemaphoreType.DMA((LAYERS, KX_GROUPS)),
+        ],
         compiler_params=pltpu.CompilerParams(vmem_limit_bytes=VMEM_BYTES),
         name="arrange_weights",
-    )(*in_vmem(held))
+    )(*map(in_hbm, shards), *in_vmem(held))
 
 
 def swap(value, distance):
@@ -455,7 +496,7 @@
         for half in range(2):
             for c10 in range(HALF):
                 channel = half * HALF + c10
-                rows = mixed[channel * STRIP : (channel + 1) * STRIP] + offset_ref[channel]
+                rows = mixed[channel * STRIP : (channel + 1) * STRIP] + 0.5 * offset_ref[channel]
                 out_ref[half, c10, 0, first : first + STRIP] = rows.astype(jnp.bfloat16)
 
 
@@ -470,7 +511,7 @@
         scratch_shapes=[pltpu.VMEM((C * STRIP, C * STRIP), jnp.bfloat16)],
         compiler_params=pltpu.CompilerParams(vmem_limit_bytes=VMEM_BYTES),
         name="local_mixing",
-    )(offset, weight.T, in_hbm(current))
+    )(offset, (0.5 * weight).T, in_hbm(current))
 
 
 def after(value, *others):
@@ -481,9 +522,9 @@
     tables = {name: jnp.asarray(table) for name, table in build_tables().items()}
     place = lax.axis_index("batch").astype(jnp.int32).reshape(1)
     field = field.reshape(FIELD)
-    shards = gather_weights(spectral_weight)
+    own, near, far, across = gather_weights(spectral_weight)
     message = forward_call(field, tables)
-    weights = arrange_weights(shards, dict(tables, place=after(tables["place"], message)))
+    weights = arrange_weights([after(own, message), near, far, across], tables)
     back = mix_call(place, exchange(message), weights[0], tables)
     local = local_term(field, after(local_weight[0], back), bias[0])
     current, message = turn_call(exchange(back), local, tables)

time: 155 us -> 153 us (0.987)
  local copies, waits for them, and re-layouts: 9.1 us -> 3 us
  Pallas kernels: 68.3 us -> 72.2 us
    unnamed x40 -> x20, local copies, waits for them, and re-layouts: 9.07 us -> 2.19 us
    pallas_call x2, Pallas kernels: 4.19 us -> 7.99 us  [mix_call(): pl.pallas_call(mix_kernel, grid=(1,), in_specs=[pl.BlockSpec(memory_space...]
    pallas_call x1, Pallas kernels: 10.5 us -> 12.4 us  [arrange_weights(): pl.pallas_call(arrange_kernel, grid=(1,), in_specs=[IN_HBM] * KX_GROUPS +...]
  transfers between devices with their start and end apart: 6 -> 6, of which waited for: 4 -> 4; matrix products, arithmetic and copies ran while one was open for 0% -> 1% of each run, Pallas kernels for 22% -> 23%
where the time goes in v3:
time: 153 us; the launch traced here: 152 us
  Pallas kernels  72.2 us (47%)
  starting transfers between devices  36.2 us (24%)
  blocking collectives  21.6 us (14%)
  waiting for transfers between devices  18.7 us (12%)
  local copies, waits for them, and re-layouts  3 us (2%)
    all_to_all x3, starting transfers between devices, exchange(): lax.all_to_all(grouped, 'space', split_axis=0, concat_axis=0, tiled=True)  34 us
    all_to_all x1, blocking collectives, exchange(): lax.all_to_all(grouped, 'space', split_axis=0, concat_axis=0, tiled=True)  21.6 us
    pallas_call x1, Pallas kernels, turn_call(): pl.pallas_call(turn_kernel, grid=(STEPS,), in_specs=[field_spec()] + [IN_...  17.1 us
    all_to_all x3, waiting for transfers between devices, exchange(): lax.all_to_all(grouped, 'space', split_axis=0, concat_axis=0, tiled=True)  15.5 us
    pallas_call x2, Pallas kernels, local_term(): pl.pallas_call(local_kernel, grid=(PLANES, Y // LOCAL_ROWS), in_specs=[pl...  14.6 us
    pallas_call x1, Pallas kernels, arrange_weights(): pl.pallas_call(arrange_kernel, grid=(1,), in_specs=[IN_HBM] * KX_GROUPS +...  12.4 us
    pallas_call x1, Pallas kernels, inverse_call(): pl.pallas_call(inverse_kernel, grid=(STEPS,), in_specs=[field_spec()] + [...  12 us
    pallas_call x1, Pallas kernels, forward_call(): pl.pallas_call(forward_kernel, grid=(STEPS,), in_specs=[field_spec(), IN_...  8.2 us
  transfers between devices with their start and end apart: 6, of which 4 were waited for; matrix products, arithmetic and copies ran while one was open for 1% of the time, Pallas kernels for 23%

profile of v3, /device:TPU:2, one launch (start us, length us, event | category | flops | bytes accessed | tf_op | source)
XLA Modules:
  0.0 151.8 jit_solution(17429516287759220413)
XLA Ops:
  0.0 0.0 copy-start.1
  0.0 1.6 %collective-permute-start.1 = (bf16[6,36,2,800]{3,2,1,0:T(2,128)(2,1)}, bf16[6,36,2,800]{3,2,1,0:T(2,128)(2,1)}, u32[]{:S(2)}, u32[]{:S(2)}) collective-permute-start(bf16[6,36,2,800]{3,2,1,0:T(2,128)(2,1)} %bitcast.32), channel_id=1, source_target_pairs={{0,2},{1,3},{2,0},{3,1},{4,6},{5,7},{6,4},{7,5},{8,10},{9,11},{10,... | collective-permute-start | bytes 2073608 | tf_op jit(solution)/shard_map/ppermute | solution.py:463
  1.6 0.0 copy-start.2
  1.6 1.0 copy-done.2
  2.6 0.0 copy-start.6
  2.6 0.9 copy-done.6
  3.5 0.0 copy-start.4
  3.5 8.2 %forward_zt_y.1 = bf16[1536,128]{1,0:T(8,128)(2,1)} custom-call(bf16[2,10,2,128,512]{4,3,2,1,0:T(8,128)(2,1)} %bitcast.27, bf16[512,256]{1,0:T(8,128)(2,1)S(1)} %copy-done.6, bf16[192,1024]{1,0:T(8,128)(2,1)S(1)} %copy-done.2), custom_call_target="tpu_custom_call" | custom-call | tf_op jit(solution)/shard_map/forward_zt_y/pallas_call | solution.py:200
  11.7 0.0 copy-start.8
  11.7 14.5 %all-to-all-start = ((bf16[64,24,128]{2,1,0:T(8,128)(2,1)}), bf16[64,24,128]{2,1,0:T(8,128)(2,1)S(1)}, u32[]{:S(2)}, u32[]{:S(2)}) async-start(bf16[64,24,128]{2,1,0:T(8,128)(2,1)} %bitcast.29), calls=%async_computation | async-start | bytes 786432 | tf_op jit(solution)/shard_map/all_to_all | solution.py:474
  26.2 0.1 collective-permute-start
  26.3 0.0 collective-permute-done.1.far
  26.3 0.5 collective-permute-start.2
  26.8 2.1 %collective-permute-done.near = bf16[6,36,2,800]{3,2,1,0:T(2,128)(2,1)} collective-permute-done((bf16[6,36,2,800]{3,2,1,0:T(2,128)(2,1)}, bf16[6,36,2,800]{3,2,1,0:T(2,128)(2,1)}, u32[]{:S(2)}, u32[]{:S(2)}) %collective-permute-start) | collective-permute-done | bytes 691232 | tf_op jit(solution)/shard_map/ppermute | solution.py:463
  28.9 1.1 collective-permute-done.2.across
  30.0 0.0 copy-done.1
  30.0 0.0 copy-done.4
  30.0 12.4 %arrange_weights.1 = (bf16[4,1440,128]{2,1,0:T(8,128)(2,1)}, bf16[4,1440,128]{2,1,0:T(8,128)(2,1)}) custom-call(bf16[6,36,2,800]{3,2,1,0:T(2,128)(2,1)} %bitcast.34, bf16[6,36,2,800]{3,2,1,0:T(2,128)(2,1)} %collective-permute-done.near, bf16[6,36,2,800]{3,2,1,0:T(2,128)(2,1)} %collective-permute-done.1.far, ...), custom_call_target="tpu_custom_call" | custom-call | tf_op jit(solution)/shard_map/arrange_weights/pallas_call | solution.py:444
  42.4 0.0 all-to-all-done
  42.4 4.0 %mix_x.2 = bf16[1536,128]{1,0:T(8,128)(2,1)} custom-call(s32[1]{0:T(128)} %bitcast.5.place_ref, bf16[1536,128]{1,0:T(8,128)(2,1)S(1)} %bitcast.24, bf16[192,512]{1,0:T(8,128)(2,1)} %constant.28.clone.x_hbm, bf16[128,128]{1,0:T(8,128)(2,1)} %constant.30.clone.same_hbm, bf16[512,384]{1,0:T(8,128)(2,1)} %constant.29.clone.inv_hbm, ...), custom_call_target="tpu_custom_call" | custom-call | tf_op jit(solution)/shard_map/mix_x/pallas_call | solution.py:379
  46.4 12.7 %all-to-all-start.1 = ((bf16[64,24,128]{2,1,0:T(8,128)(2,1)}), bf16[64,24,128]{2,1,0:T(8,128)(2,1)S(1)}, u32[]{:S(2)}, u32[]{:S(2)}) async-start(bf16[64,24,128]{2,1,0:T(8,128)(2,1)} %bitcast.30), calls=%async_computation.1 | async-start | bytes 786432 | tf_op jit(solution)/shard_map/all_to_all | solution.py:474
  59.2 0.8 fusion
  60.0 0.1 copy.17
  60.1 0.0 copy-done.8
  60.1 0.0 copy-start
  60.1 0.0 copy-start.3
  60.1 0.0 copy-start.5
  60.1 0.0 copy-start.7
  60.1 7.3 %local_mixing.2.local_ref = bf16[2,10,2,128,512]{4,3,2,1,0:T(8,128)(2,1)} custom-call(f32[20]{0:T(128)S(1)} %get-tuple-element.21.offset_ref, bf16[20,20]{1,0:T(8,128)(2,1)S(1)} %multiply_bitcast_fusion.weight_ref, bf16[2,10,2,128,512]{4,3,2,1,0:T(8,128)(2,1)} %bitcast.28), custom_call_target="tpu_custom_call" | custom-call | tf_op jit(solution)/shard_map/local_mixing/pallas_call | solution.py:505
  67.5 7.6 %all-to-all-done.1 = bf16[64,24,128]{2,1,0:T(8,128)(2,1)S(1)} async-done(((bf16[64,24,128]{2,1,0:T(8,128)(2,1)}), bf16[64,24,128]{2,1,0:T(8,128)(2,1)S(1)}, u32[]{:S(2)}, u32[]{:S(2)}) %all-to-all-start.1) | async-done | bytes 393248 | tf_op jit(solution)/shard_map/all_to_all | solution.py:474
  75.0 0.0 copy-done
  75.0 0.0 copy-done.3
  75.0 0.0 copy-done.5
  75.0 0.0 copy-done.7
  75.1 17.1 %inverse_then_forward.1 = (bf16[2,10,2,128,512]{4,3,2,1,0:T(8,128)(2,1)}, bf16[1536,128]{1,0:T(8,128)(2,1)}) custom-call(bf16[2,10,2,128,512]{4,3,2,1,0:T(8,128)(2,1)} %local_mixing.2.local_ref, bf16[1536,128]{1,0:T(8,128)(2,1)S(1)} %bitcast.25, bf16[1024,192]{1,0:T(8,128)(2,1)S(1)} %copy-done, bf16[256,512]{1,0:T(8,128)(2,1)S(1)} %copy-done.5, ...), custom_call_target="tpu_custom_call" | custom-call | tf_op jit(solution)/shard_map/inverse_then_forward/pallas_call | solution.py:302
  92.2 6.8 %all-to-all-start.2 = ((bf16[64,24,128]{2,1,0:T(8,128)(2,1)}), bf16[64,24,128]{2,1,0:T(8,128)(2,1)S(1)}, u32[]{:S(2)}, u32[]{:S(2)}) async-start(bf16[64,24,128]{2,1,0:T(8,128)(2,1)} %bitcast.35), calls=%async_computation.2 | async-start | bytes 786432 | tf_op jit(solution)/shard_map/all_to_all | solution.py:474
  99.0 0.1 copy.16
  99.1 7.2 %local_mixing.3.local_ref = bf16[2,10,2,128,512]{4,3,2,1,0:T(8,128)(2,1)} custom-call(f32[20]{0:T(128)S(1)} %get-tuple-element.22.offset_ref, bf16[20,20]{1,0:T(8,128)(2,1)S(1)} %multiply_bitcast_fusion.1.weight_ref, bf16[2,10,2,128,512]{4,3,2,1,0:T(8,128)(2,1)} %get-tuple-element.15.field_ref), custom_call_target="tpu_custom_call" | custom-call | tf_op jit(solution)/shard_map/local_mixing/pallas_call | solution.py:505
  106.3 7.9 %all-to-all-done.2 = bf16[64,24,128]{2,1,0:T(8,128)(2,1)S(1)} async-done(((bf16[64,24,128]{2,1,0:T(8,128)(2,1)}), bf16[64,24,128]{2,1,0:T(8,128)(2,1)S(1)}, u32[]{:S(2)}, u32[]{:S(2)}) %all-to-all-start.2) | async-done | bytes 393248 | tf_op jit(solution)/shard_map/all_to_all | solution.py:474
  114.2 4.0 %mix_x.3 = bf16[1536,128]{1,0:T(8,128)(2,1)} custom-call(s32[1]{0:T(128)} %bitcast.5.place_ref, bf16[1536,128]{1,0:T(8,128)(2,1)S(1)} %bitcast.26, bf16[192,512]{1,0:T(8,128)(2,1)} %constant.28.clone.x_hbm, bf16[128,128]{1,0:T(8,128)(2,1)} %constant.30.clone.same_hbm, bf16[512,384]{1,0:T(8,128)(2,1)} %constant.29.clone.inv_hbm, ...), custom_call_target="tpu_custom_call" | custom-call | tf_op jit(solution)/shard_map/mix_x/pallas_call | solution.py:379
  118.2 21.6 %all_to_all.20 = bf16[64,24,128]{2,1,0:T(8,128)(2,1)S(1)} all-to-all(bf16[64,24,128]{2,1,0:T(8,128)(2,1)} %bitcast.31), channel_id=1, replica_groups=mesh['space'=64,'batch'=4] {'space'}, dimensions={0} | all-to-all | bytes 786432 | tf_op jit(solution)/shard_map/all_to_all | solution.py:474
  139.8 12.0 %inverse_zt_y.1 = bf16[2,10,2,128,512]{4,3,2,1,0:T(8,128)(2,1)} custom-call(bf16[2,10,2,128,512]{4,3,2,1,0:T(8,128)(2,1)} %local_mixing.3.local_ref, bf16[1536,128]{1,0:T(8,128)(2,1)S(1)} %bitcast.23, bf16[1024,192]{1,0:T(8,128)(2,1)S(1)} %copy-done, bf16[256,512]{1,0:T(8,128)(2,1)S(1)} %copy-done.5), custom_call_target="tpu_custom_call" | custom-call | tf_op jit(solution)/shard_map/inverse_zt_y/pallas_call | solution.py:266
  (3 shorter events, 0.0 us)
Async XLA Ops:
  0.0 30.0 %copy-start.1 = (bf16[800,1280]{1,0:T(8,128)(2,1)S(1)}, bf16[800,1280]{1,0:T(8,128)(2,1)}, u32[]{:S(2)}) copy-start(bf16[800,1280]{1,0:T(8,128)(2,1)} %constant.31.clone.select_ref) | copy-start | bytes 6144004
  0.0 26.3 %collective-permute-start.1 = (bf16[6,36,2,800]{3,2,1,0:T(2,128)(2,1)}, bf16[6,36,2,800]{3,2,1,0:T(2,128)(2,1)}, u32[]{:S(2)}, u32[]{:S(2)}) collective-permute-start(bf16[6,36,2,800]{3,2,1,0:T(2,128)(2,1)} %bitcast.32), channel_id=1, source_target_pairs={{0,2},{1,3},{2,0},{3,1},{4,6},{5,7},{6,4},{7,5},{8,10},{9,11},{10,... | collective-permute-start | bytes 2073608 | tf_op jit(solution)/shard_map/ppermute | solution.py:463
  1.6 1.0 copy-start.2
  2.6 0.9 copy-start.6
  3.5 26.5 %copy-start.4 = (bf16[720,768]{1,0:T(8,128)(2,1)S(1)}, bf16[720,768]{1,0:T(8,128)(2,1)}, u32[]{:S(2)}) copy-start(bf16[720,768]{1,0:T(8,128)(2,1)} %constant.32.clone.place_ref) | copy-start | bytes 3317764
  11.7 48.3 %copy-start.8 = (f32[2,20]{1,0:T(2,128)S(1)}, f32[2,20]{1,0:T(2,128)}, u32[]{:S(2)}) copy-start(f32[2,20]{1,0:T(2,128)} %param.16) | copy-start | bytes 484
  11.7 30.7 %all-to-all-start = ((bf16[64,24,128]{2,1,0:T(8,128)(2,1)}), bf16[64,24,128]{2,1,0:T(8,128)(2,1)S(1)}, u32[]{:S(2)}, u32[]{:S(2)}) async-start(bf16[64,24,128]{2,1,0:T(8,128)(2,1)} %bitcast.29), calls=%async_computation | async-start | bytes 786432 | tf_op jit(solution)/shard_map/all_to_all | solution.py:474
  26.2 2.7 %collective-permute-start = (bf16[6,36,2,800]{3,2,1,0:T(2,128)(2,1)}, bf16[6,36,2,800]{3,2,1,0:T(2,128)(2,1)}, u32[]{:S(2)}, u32[]{:S(2)}) collective-permute-start(bf16[6,36,2,800]{3,2,1,0:T(2,128)(2,1)} %bitcast.33), channel_id=1, source_target_pairs={{0,1},{1,0},{2,3},{3,2},{4,5},{5,4},{6,7},{7,6},{8,9},{9,8},{10,11... | collective-permute-start | bytes 2073608 | tf_op jit(solution)/shard_map/ppermute | solution.py:463
  26.3 3.7 %collective-permute-start.2 = (bf16[6,36,2,800]{3,2,1,0:T(2,128)(2,1)}, bf16[6,36,2,800]{3,2,1,0:T(2,128)(2,1)}, u32[]{:S(2)}, u32[]{:S(2)}) collective-permute-start(bf16[6,36,2,800]{3,2,1,0:T(2,128)(2,1)} %collective-permute-done.1.far), channel_id=1, source_target_pairs={{0,1},{1,0},{2,3},{3,2},{4,5},{5,4},{6,7},{7,6},{8,9},{9,8},{10,11... | collective-permute-start | bytes 2073608 | tf_op jit(solution)/shard_map/ppermute | solution.py:463
  46.4 28.6 %all-to-all-start.1 = ((bf16[64,24,128]{2,1,0:T(8,128)(2,1)}), bf16[64,24,128]{2,1,0:T(8,128)(2,1)S(1)}, u32[]{:S(2)}, u32[]{:S(2)}) async-start(bf16[64,24,128]{2,1,0:T(8,128)(2,1)} %bitcast.30), calls=%async_computation.1 | async-start | bytes 786432 | tf_op jit(solution)/shard_map/all_to_all | solution.py:474
  60.1 14.9 %copy-start = (bf16[1024,192]{1,0:T(8,128)(2,1)S(1)}, bf16[1024,192]{1,0:T(8,128)(2,1)}, u32[]{:S(2)}) copy-start(bf16[1024,192]{1,0:T(8,128)(2,1)} %constant.27.clone.y_inv.y_ref) | copy-start | bytes 1179652
  60.1 14.9 %copy-start.3 = (bf16[192,1024]{1,0:T(8,128)(2,1)S(1)}, bf16[192,1024]{1,0:T(8,128)(2,1)}, u32[]{:S(2)}) copy-start(bf16[192,1024]{1,0:T(8,128)(2,1)} %constant.26.clone.y_ref.y_fwd) | copy-start | bytes 1179652
  60.1 14.9 %copy-start.5 = (bf16[256,512]{1,0:T(8,128)(2,1)S(1)}, bf16[256,512]{1,0:T(8,128)(2,1)}, u32[]{:S(2)}) copy-start(bf16[256,512]{1,0:T(8,128)(2,1)} %constant.25.clone.zt_inv.zt_ref) | copy-start | bytes 786436
  60.1 14.9 %copy-start.7 = (bf16[512,256]{1,0:T(8,128)(2,1)S(1)}, bf16[512,256]{1,0:T(8,128)(2,1)}, u32[]{:S(2)}) copy-start(bf16[512,256]{1,0:T(8,128)(2,1)} %constant.24.clone.zt_ref.zt_fwd) | copy-start | bytes 786436
  92.2 22.1 %all-to-all-start.2 = ((bf16[64,24,128]{2,1,0:T(8,128)(2,1)}), bf16[64,24,128]{2,1,0:T(8,128)(2,1)S(1)}, u32[]{:S(2)}, u32[]{:S(2)}) async-start(bf16[64,24,128]{2,1,0:T(8,128)(2,1)} %bitcast.35), calls=%async_computation.2 | async-start | bytes 786432 | tf_op jit(solution)/shard_map/all_to_all | solution.py:474

commit v4 on v3

--- a/solution.py
+++ b/solution.py
@@ -143,24 +143,54 @@
             rows += [z[:, :LANES], z[:, LANES:]]
         columns.append(jnp.concatenate(rows, 0))
     modes = dot(y_table[...], jnp.concatenate(columns, 1))
+    for pair in range(PAIRS):
+        modes_ref[step * PAIRS + pair] = modes[:, pair * LANES : (pair + 1) * LANES]
+
+
+def group_masks():
     lane = lane_index((MY * 8, LANES))
-    for pair in range(PAIRS):
-        channel = step * PAIRS + pair
-        own = modes[:, pair * LANES : (pair + 1) * LANES]
-        mask = (lane >= channel * QL) & (lane < channel * QL + QL)
+    return [(lane >= g * QL) & (lane < g * QL + QL) for g in range(HALF)]
+
+
+OFFSETS = range(1 - QH, HALF)
+
+
+def pack_modes(modes_ref, turned_ref):
+    masks = group_masks()
+    for place, offset in enumerate(OFFSETS):
+        value = jnp.zeros((MY * 8, LANES), jnp.float32)
         for qh in range(QH):
-            shift = lax.rem((channel - qh) * QL + LANES, LANES)
-            moved = pltpu.roll(own, shift, 1)
-            kept = modes_ref[:, qh].reshape(MY * 8, LANES)
-            modes_ref[:, qh] = jnp.where(mask, moved, kept).reshape(MY, 8, LANES)
-
-
-def forward_kernel(field_ref, zt_ref, y_ref, out_ref, modes_ref):
+            if 0 <= qh + offset < HALF:
+                value = jnp.where(masks[qh], modes_ref[qh + offset], value)
+        turned_ref[place] = pltpu.roll(value, offset * QL % LANES, 1)
+    strips = []
+    for qh in range(QH):
+        value = jnp.zeros((MY * 8, LANES), jnp.float32)
+        for channel in range(HALF):
+            value = jnp.where(masks[channel], turned_ref[channel - qh + QH - 1], value)
+        strips.append(value.reshape(MY, 1, 8, LANES))
+    return jnp.concatenate(strips, 1).reshape(GROUPS * 8, LANES).astype(jnp.bfloat16)
+
+
+def unpack_modes(message_ref, modes_ref, turned_ref):
+    masks = group_masks()
+    message = message_ref[...].astype(jnp.float32).reshape(MY, QH, 8, LANES)
+    strips = [message[:, qh].reshape(MY * 8, LANES) for qh in range(QH)]
+    for place, offset in enumerate(OFFSETS):
+        value = jnp.zeros((MY * 8, LANES), jnp.float32)
+        for qh in range(QH):
+            if 0 <= qh + offset < HALF:
+                value = jnp.where(masks[qh + offset], strips[qh], value)
+        turned_ref[place] = pltpu.roll(value, -offset * QL % LANES, 1)
+    for channel in range(HALF):
+        value = jnp.zeros((MY * 8, LANES), jnp.float32)
+        for qh in range(QH):
+            value = jnp.where(masks[qh], turned_ref[channel - qh + QH - 1], value)
+        modes_ref[channel] = value.astype(jnp.bfloat16)
+
+
+def forward_kernel(field_ref, zt_ref, y_ref, out_ref, modes_ref, turned_ref):
     step = pl.program_id(0)
-
-    @pl.when(step == 0)
-    def _():
-        modes_ref[...] = jnp.zeros_like(modes_ref)
 
     def block(half, pair):
         return field_ref[half, pair].reshape(PLANES * Y, ZT)
@@ -169,7 +199,7 @@
 
     @pl.when(step == STEPS - 1)
     def _():
-        out_ref[...] = modes_ref[...].reshape(GROUPS * 8, LANES).astype(jnp.bfloat16)
+        out_ref[...] = pack_modes(modes_ref, turned_ref)
 
 
 IN_VMEM = pl.BlockSpec(memory_space=pltpu.VMEM)
@@ -193,20 +223,22 @@
 
 
 MESSAGE = (GROUPS * 8, LANES)
-MODES = pltpu.VMEM((MY, QH, 8, LANES), jnp.float32)
+SENT_MODES = pltpu.VMEM((HALF, MY * 8, LANES), jnp.float32)
+GOT_MODES = pltpu.VMEM((HALF, MY * 8, LANES), jnp.bfloat16)
+TURNED = pltpu.VMEM((len(OFFSETS), MY * 8, LANES), jnp.float32)
 
 
 def forward_call(field, tables):
     return pl.pallas_call(
         forward_kernel,
         grid=(STEPS,),
-        in_specs=[field_spec(), IN_VMEM, IN_VMEM],
+        in_specs=[field_spec()] + [whole(tables[name].shape) for name in ("zt_fwd", "y_fwd")],
         out_specs=whole(MESSAGE),
         out_shape=pltpu.HBM(MESSAGE, jnp.bfloat16),
-        scratch_shapes=[MODES],
+        scratch_shapes=[SENT_MODES, TURNED],
         compiler_params=pltpu.CompilerParams(vmem_limit_bytes=VMEM_BYTES),
         name="forward_zt_y",
-    )(in_hbm(field), *in_vmem((tables["zt_fwd"], tables["y_fwd"])))
+    )(in_hbm(field), in_hbm(tables["zt_fwd"]), in_hbm(tables["y_fwd"]))
 
 
 def gelu(h):
@@ -218,16 +250,7 @@
 
 
 def inverse_step(step, modes_ref, local_ref, y_table, zt_table, out_ref):
-    lane = lane_index((MY * 8, LANES))
-    columns = []
-    for pair in range(PAIRS):
-        channel = step * PAIRS + pair
-        value = jnp.zeros((MY * 8, LANES), jnp.float32)
-        for qh in range(QH):
-            shift = lax.rem((qh - channel) * QL + LANES, LANES)
-            moved = pltpu.roll(modes_ref[:, qh].reshape(MY * 8, LANES), shift, 1)
-            value = jnp.where((lane >= qh * QL) & (lane < qh * QL + QL), moved, value)
-        columns.append(value.astype(jnp.bfloat16))
+    columns = [modes_ref[step * PAIRS + pair] for pair in range(PAIRS)]
     back = dot(y_table[...], jnp.concatenate(columns, 1)).astype(jnp.bfloat16)
     zt_inv = zt_table[...]
     span = PLANES * Y
@@ -244,16 +267,12 @@
     return results
 
 
-def load_modes(message_ref, modes_ref):
-    modes_ref[...] = message_ref[...].astype(jnp.float32).reshape(MY, QH, 8, LANES)
-
-
-def inverse_kernel(local_ref, message_ref, y_ref, zt_ref, out_ref, modes_ref):
+def inverse_kernel(local_ref, message_ref, y_ref, zt_ref, out_ref, modes_ref, turned_ref):
     step = pl.program_id(0)
 
     @pl.when(step == 0)
     def _():
-        load_modes(message_ref, modes_ref)
+        unpack_modes(message_ref, modes_ref, turned_ref)
 
     inverse_step(step, modes_ref, local_ref, y_ref, zt_ref, out_ref)
 
@@ -269,21 +288,20 @@
         in_specs=[field_spec()] + [IN_VMEM] * 3,
         out_specs=field_spec(),
         out_shape=pltpu.HBM(FIELD, jnp.bfloat16),
-        scratch_shapes=[MODES],
+        scratch_shapes=[GOT_MODES, TURNED],
         compiler_params=pltpu.CompilerParams(vmem_limit_bytes=VMEM_BYTES),
         name="inverse_zt_y",
     )(in_hbm(local), *in_vmem(held))
 
 
 def turn_kernel(
-    local_ref, message_ref, y_inv, zt_inv, zt_fwd, y_fwd, out_ref, send_ref, modes_ref, next_ref
+    local_ref, message_ref, y_inv, zt_inv, zt_fwd, y_fwd, out_ref, send_ref, modes_ref, next_ref, turned_ref
 ):
     step = pl.program_id(0)
 
     @pl.when(step == 0)
     def _():
-        load_modes(message_ref, modes_ref)
-        next_ref[...] = jnp.zeros_like(next_ref)
+        unpack_modes(message_ref, modes_ref, turned_ref)
 
     results = inverse_step(step, modes_ref, local_ref, y_inv, zt_inv, out_ref)
 
@@ -294,7 +312,7 @@
 
     @pl.when(step == STEPS - 1)
     def _():
-        send_ref[...] = next_ref[...].reshape(GROUPS * 8, LANES).astype(jnp.bfloat16)
+        send_ref[...] = pack_modes(next_ref, turned_ref)
 
 
 def turn_call(message, local, tables):
@@ -308,7 +326,7 @@
             pltpu.HBM(FIELD, jnp.bfloat16),
             pltpu.HBM(MESSAGE, jnp.bfloat16),
         ],
-        scratch_shapes=[MODES, MODES],
+        scratch_shapes=[GOT_MODES, SENT_MODES, TURNED],
         compiler_params=pltpu.CompilerParams(vmem_limit_bytes=VMEM_BYTES),
         name="inverse_then_forward",
     )(in_hbm(local), *in_vmem(held))

time: 153 us -> 147 us (0.961)
  Pallas kernels: 72.2 us -> 69 us
  local copies, waits for them, and re-layouts: 3 us -> 1.05 us
    pallas_call x1, Pallas kernels: 17.1 us -> 15 us  [turn_call(): pl.pallas_call(turn_kernel, grid=(STEPS,), in_specs=[field_spec()] + [IN_...]
    unnamed x20 -> x16, local copies, waits for them, and re-layouts: 2.19 us -> 0.25 us
  transfers between devices with their start and end apart: 6 -> 6, of which waited for: 4 -> 4; matrix products, arithmetic and copies ran while one was open for 1% -> 1% of each run, Pallas kernels for 23% -> 24%
where the time goes in v4:
time: 147 us
  Pallas kernels  69 us (47%)
  starting transfers between devices  36.2 us (25%)
  blocking collectives  21.6 us (15%)
  waiting for transfers between devices  18.6 us (13%)
    all_to_all x3, starting transfers between devices, exchange(): lax.all_to_all(grouped, 'space', split_axis=0, concat_axis=0, tiled=True)  34 us
    all_to_all x1, blocking collectives, exchange(): lax.all_to_all(grouped, 'space', split_axis=0, concat_axis=0, tiled=True)  21.6 us
    all_to_all x3, waiting for transfers between devices, exchange(): lax.all_to_all(grouped, 'space', split_axis=0, concat_axis=0, tiled=True)  15.4 us
    pallas_call x1, Pallas kernels, turn_call(): pl.pallas_call(turn_kernel, grid=(STEPS,), in_specs=[field_spec()] + [IN_...  15 us
    pallas_call x2, Pallas kernels, local_term(): pl.pallas_call(local_kernel, grid=(PLANES, Y // LOCAL_ROWS), in_specs=[pl...  14.6 us
    pallas_call x1, Pallas kernels, arrange_weights(): pl.pallas_call(arrange_kernel, grid=(1,), in_specs=[IN_HBM] * KX_GROUPS +...  12.4 us
    pallas_call x1, Pallas kernels, inverse_call(): pl.pallas_call(inverse_kernel, grid=(STEPS,), in_specs=[field_spec()] + [...  11.4 us
    pallas_call x2, Pallas kernels, mix_call(): pl.pallas_call(mix_kernel, grid=(1,), in_specs=[pl.BlockSpec(memory_space...  7.98 us
  transfers between devices with their start and end apart: 6, of which 4 were waited for; matrix products, arithmetic and copies ran while one was open for 1% of the time, Pallas kernels for 24%

profile of v4, /device:TPU:2, one launch (start us, length us, event | category | flops | bytes accessed | tf_op | source)
XLA Modules:
  0.0 146.7 jit_solution(10397302118744141393)
XLA Ops:
  0.0 0.0 copy-start.3
  0.0 0.0 copy-start.1
  0.0 1.6 %collective-permute-start.1 = (bf16[6,36,2,800]{3,2,1,0:T(2,128)(2,1)}, bf16[6,36,2,800]{3,2,1,0:T(2,128)(2,1)}, u32[]{:S(2)}, u32[]{:S(2)}) collective-permute-start(bf16[6,36,2,800]{3,2,1,0:T(2,128)(2,1)} %bitcast.32), channel_id=1, source_target_pairs={{0,2},{1,3},{2,0},{3,1},{4,6},{5,7},{6,4},{7,5},{8,10},{9,11},{10,... | collective-permute-start | bytes 2073608 | tf_op jit(solution)/shard_map/ppermute | solution.py:481
  1.6 7.6 %forward_zt_y.1 = bf16[1536,128]{1,0:T(8,128)(2,1)} custom-call(bf16[2,10,2,128,512]{4,3,2,1,0:T(8,128)(2,1)} %bitcast.27, bf16[512,256]{1,0:T(8,128)(2,1)} %constant.24.clone.zt_ref.zt_fwd, bf16[192,1024]{1,0:T(8,128)(2,1)} %constant.26.clone.y_ref.y_fwd), custom_call_target="tpu_custom_call" | custom-call | tf_op jit(solution)/shard_map/forward_zt_y/pallas_call | solution.py:232
  9.2 0.0 copy-start.6
  9.2 14.5 %all-to-all-start = ((bf16[64,24,128]{2,1,0:T(8,128)(2,1)}), bf16[64,24,128]{2,1,0:T(8,128)(2,1)S(1)}, u32[]{:S(2)}, u32[]{:S(2)}) async-start(bf16[64,24,128]{2,1,0:T(8,128)(2,1)} %bitcast.29), calls=%async_computation | async-start | bytes 786432 | tf_op jit(solution)/shard_map/all_to_all | solution.py:492
  23.7 0.1 collective-permute-start
  23.8 0.0 collective-permute-done.1.far
  23.8 0.5 collective-permute-start.2
  24.3 2.1 %collective-permute-done.near = bf16[6,36,2,800]{3,2,1,0:T(2,128)(2,1)} collective-permute-done((bf16[6,36,2,800]{3,2,1,0:T(2,128)(2,1)}, bf16[6,36,2,800]{3,2,1,0:T(2,128)(2,1)}, u32[]{:S(2)}, u32[]{:S(2)}) %collective-permute-start) | collective-permute-done | bytes 691232 | tf_op jit(solution)/shard_map/ppermute | solution.py:481
  26.4 1.1 collective-permute-done.2.across
  27.5 0.0 copy-done.3
  27.5 0.0 copy-done.1
  27.5 12.4 %arrange_weights.1 = (bf16[4,1440,128]{2,1,0:T(8,128)(2,1)}, bf16[4,1440,128]{2,1,0:T(8,128)(2,1)}) custom-call(bf16[6,36,2,800]{3,2,1,0:T(2,128)(2,1)} %bitcast.34, bf16[6,36,2,800]{3,2,1,0:T(2,128)(2,1)} %collective-permute-done.near, bf16[6,36,2,800]{3,2,1,0:T(2,128)(2,1)} %collective-permute-done.1.far, ...), custom_call_target="tpu_custom_call" | custom-call | tf_op jit(solution)/shard_map/arrange_weights/pallas_call | solution.py:462
  39.9 0.0 all-to-all-done
  39.9 4.0 %mix_x.2 = bf16[1536,128]{1,0:T(8,128)(2,1)} custom-call(s32[1]{0:T(128)} %bitcast.5.place_ref, bf16[1536,128]{1,0:T(8,128)(2,1)S(1)} %bitcast.24, bf16[192,512]{1,0:T(8,128)(2,1)} %constant.28.clone.x_hbm, bf16[128,128]{1,0:T(8,128)(2,1)} %constant.30.clone.same_hbm, bf16[512,384]{1,0:T(8,128)(2,1)} %constant.29.clone.inv_hbm, ...), custom_call_target="tpu_custom_call" | custom-call | tf_op jit(solution)/shard_map/mix_x/pallas_call | solution.py:397
  43.9 12.8 %all-to-all-start.1 = ((bf16[64,24,128]{2,1,0:T(8,128)(2,1)}), bf16[64,24,128]{2,1,0:T(8,128)(2,1)S(1)}, u32[]{:S(2)}, u32[]{:S(2)}) async-start(bf16[64,24,128]{2,1,0:T(8,128)(2,1)} %bitcast.30), calls=%async_computation.1 | async-start | bytes 786432 | tf_op jit(solution)/shard_map/all_to_all | solution.py:492
  56.7 0.8 fusion
  57.5 0.1 copy.17
  57.6 0.0 copy-done.6
  57.6 0.0 copy-start
  57.6 0.0 copy-start.2
  57.7 0.0 copy-start.4
  57.7 0.0 copy-start.5
  57.7 7.3 %local_mixing.2.local_ref = bf16[2,10,2,128,512]{4,3,2,1,0:T(8,128)(2,1)} custom-call(f32[20]{0:T(128)S(1)} %get-tuple-element.21.offset_ref, bf16[20,20]{1,0:T(8,128)(2,1)S(1)} %multiply_bitcast_fusion.weight_ref, bf16[2,10,2,128,512]{4,3,2,1,0:T(8,128)(2,1)} %bitcast.28), custom_call_target="tpu_custom_call" | custom-call | tf_op jit(solution)/shard_map/local_mixing/pallas_call | solution.py:523
  65.0 7.6 %all-to-all-done.1 = bf16[64,24,128]{2,1,0:T(8,128)(2,1)S(1)} async-done(((bf16[64,24,128]{2,1,0:T(8,128)(2,1)}), bf16[64,24,128]{2,1,0:T(8,128)(2,1)S(1)}, u32[]{:S(2)}, u32[]{:S(2)}) %all-to-all-start.1) | async-done | bytes 393248 | tf_op jit(solution)/shard_map/all_to_all | solution.py:492
  72.6 0.0 copy-done
  72.6 0.0 copy-done.2
  72.6 0.0 copy-done.4
  72.6 0.0 copy-done.5
  72.6 15.0 %inverse_then_forward.1 = (bf16[2,10,2,128,512]{4,3,2,1,0:T(8,128)(2,1)}, bf16[1536,128]{1,0:T(8,128)(2,1)}) custom-call(bf16[2,10,2,128,512]{4,3,2,1,0:T(8,128)(2,1)} %local_mixing.2.local_ref, bf16[1536,128]{1,0:T(8,128)(2,1)S(1)} %bitcast.25, bf16[1024,192]{1,0:T(8,128)(2,1)S(1)} %copy-done, bf16[256,512]{1,0:T(8,128)(2,1)S(1)} %copy-done.4, ...), custom_call_target="tpu_custom_call" | custom-call | tf_op jit(solution)/shard_map/inverse_then_forward/pallas_call | solution.py:320
  87.6 6.8 %all-to-all-start.2 = ((bf16[64,24,128]{2,1,0:T(8,128)(2,1)}), bf16[64,24,128]{2,1,0:T(8,128)(2,1)S(1)}, u32[]{:S(2)}, u32[]{:S(2)}) async-start(bf16[64,24,128]{2,1,0:T(8,128)(2,1)} %bitcast.35), calls=%async_computation.2 | async-start | bytes 786432 | tf_op jit(solution)/shard_map/all_to_all | solution.py:492
  94.4 0.1 copy.16
  94.5 7.2 %local_mixing.3.local_ref = bf16[2,10,2,128,512]{4,3,2,1,0:T(8,128)(2,1)} custom-call(f32[20]{0:T(128)S(1)} %get-tuple-element.22.offset_ref, bf16[20,20]{1,0:T(8,128)(2,1)S(1)} %multiply_bitcast_fusion.1.weight_ref, bf16[2,10,2,128,512]{4,3,2,1,0:T(8,128)(2,1)} %get-tuple-element.15.field_ref), custom_call_target="tpu_custom_call" | custom-call | tf_op jit(solution)/shard_map/local_mixing/pallas_call | solution.py:523
  101.8 7.9 %all-to-all-done.2 = bf16[64,24,128]{2,1,0:T(8,128)(2,1)S(1)} async-done(((bf16[64,24,128]{2,1,0:T(8,128)(2,1)}), bf16[64,24,128]{2,1,0:T(8,128)(2,1)S(1)}, u32[]{:S(2)}, u32[]{:S(2)}) %all-to-all-start.2) | async-done | bytes 393248 | tf_op jit(solution)/shard_map/all_to_all | solution.py:492
  109.6 4.0 %mix_x.3 = bf16[1536,128]{1,0:T(8,128)(2,1)} custom-call(s32[1]{0:T(128)} %bitcast.5.place_ref, bf16[1536,128]{1,0:T(8,128)(2,1)S(1)} %bitcast.26, bf16[192,512]{1,0:T(8,128)(2,1)} %constant.28.clone.x_hbm, bf16[128,128]{1,0:T(8,128)(2,1)} %constant.30.clone.same_hbm, bf16[512,384]{1,0:T(8,128)(2,1)} %constant.29.clone.inv_hbm, ...), custom_call_target="tpu_custom_call" | custom-call | tf_op jit(solution)/shard_map/mix_x/pallas_call | solution.py:397
  113.6 21.6 %all_to_all.20 = bf16[64,24,128]{2,1,0:T(8,128)(2,1)S(1)} all-to-all(bf16[64,24,128]{2,1,0:T(8,128)(2,1)} %bitcast.31), channel_id=1, replica_groups=mesh['space'=64,'batch'=4] {'space'}, dimensions={0} | all-to-all | bytes 786432 | tf_op jit(solution)/shard_map/all_to_all | solution.py:492
  135.3 11.4 %inverse_zt_y.1 = bf16[2,10,2,128,512]{4,3,2,1,0:T(8,128)(2,1)} custom-call(bf16[2,10,2,128,512]{4,3,2,1,0:T(8,128)(2,1)} %local_mixing.3.local_ref, bf16[1536,128]{1,0:T(8,128)(2,1)S(1)} %bitcast.23, bf16[1024,192]{1,0:T(8,128)(2,1)S(1)} %copy-done, bf16[256,512]{1,0:T(8,128)(2,1)S(1)} %copy-done.4), custom_call_target="tpu_custom_call" | custom-call | tf_op jit(solution)/shard_map/inverse_zt_y/pallas_call | solution.py:285
  (3 shorter events, 0.0 us)
Async XLA Ops:
  0.0 27.5 %copy-start.3 = (bf16[720,768]{1,0:T(8,128)(2,1)S(1)}, bf16[720,768]{1,0:T(8,128)(2,1)}, u32[]{:S(2)}) copy-start(bf16[720,768]{1,0:T(8,128)(2,1)} %constant.32.clone.place_ref) | copy-start | bytes 3317764
  0.0 27.5 %copy-start.1 = (bf16[800,1280]{1,0:T(8,128)(2,1)S(1)}, bf16[800,1280]{1,0:T(8,128)(2,1)}, u32[]{:S(2)}) copy-start(bf16[800,1280]{1,0:T(8,128)(2,1)} %constant.31.clone.select_ref) | copy-start | bytes 6144004
  0.0 23.8 %collective-permute-start.1 = (bf16[6,36,2,800]{3,2,1,0:T(2,128)(2,1)}, bf16[6,36,2,800]{3,2,1,0:T(2,128)(2,1)}, u32[]{:S(2)}, u32[]{:S(2)}) collective-permute-start(bf16[6,36,2,800]{3,2,1,0:T(2,128)(2,1)} %bitcast.32), channel_id=1, source_target_pairs={{0,2},{1,3},{2,0},{3,1},{4,6},{5,7},{6,4},{7,5},{8,10},{9,11},{10,... | collective-permute-start | bytes 2073608 | tf_op jit(solution)/shard_map/ppermute | solution.py:481
  9.2 48.4 %copy-start.6 = (f32[2,20]{1,0:T(2,128)S(1)}, f32[2,20]{1,0:T(2,128)}, u32[]{:S(2)}) copy-start(f32[2,20]{1,0:T(2,128)} %param.16) | copy-start | bytes 484
  9.2 30.8 %all-to-all-start = ((bf16[64,24,128]{2,1,0:T(8,128)(2,1)}), bf16[64,24,128]{2,1,0:T(8,128)(2,1)S(1)}, u32[]{:S(2)}, u32[]{:S(2)}) async-start(bf16[64,24,128]{2,1,0:T(8,128)(2,1)} %bitcast.29), calls=%async_computation | async-start | bytes 786432 | tf_op jit(solution)/shard_map/all_to_all | solution.py:492
  23.7 2.7 %collective-permute-start = (bf16[6,36,2,800]{3,2,1,0:T(2,128)(2,1)}, bf16[6,36,2,800]{3,2,1,0:T(2,128)(2,1)}, u32[]{:S(2)}, u32[]{:S(2)}) collective-permute-start(bf16[6,36,2,800]{3,2,1,0:T(2,128)(2,1)} %bitcast.33), channel_id=1, source_target_pairs={{0,1},{1,0},{2,3},{3,2},{4,5},{5,4},{6,7},{7,6},{8,9},{9,8},{10,11... | collective-permute-start | bytes 2073608 | tf_op jit(solution)/shard_map/ppermute | solution.py:481
  23.8 3.7 %collective-permute-start.2 = (bf16[6,36,2,800]{3,2,1,0:T(2,128)(2,1)}, bf16[6,36,2,800]{3,2,1,0:T(2,128)(2,1)}, u32[]{:S(2)}, u32[]{:S(2)}) collective-permute-start(bf16[6,36,2,800]{3,2,1,0:T(2,128)(2,1)} %collective-permute-done.1.far), channel_id=1, source_target_pairs={{0,1},{1,0},{2,3},{3,2},{4,5},{5,4},{6,7},{7,6},{8,9},{9,8},{10,11... | collective-permute-start | bytes 2073608 | tf_op jit(solution)/shard_map/ppermute | solution.py:481
  43.9 28.6 %all-to-all-start.1 = ((bf16[64,24,128]{2,1,0:T(8,128)(2,1)}), bf16[64,24,128]{2,1,0:T(8,128)(2,1)S(1)}, u32[]{:S(2)}, u32[]{:S(2)}) async-start(bf16[64,24,128]{2,1,0:T(8,128)(2,1)} %bitcast.30), calls=%async_computation.1 | async-start | bytes 786432 | tf_op jit(solution)/shard_map/all_to_all | solution.py:492
  57.6 14.9 %copy-start = (bf16[1024,192]{1,0:T(8,128)(2,1)S(1)}, bf16[1024,192]{1,0:T(8,128)(2,1)}, u32[]{:S(2)}) copy-start(bf16[1024,192]{1,0:T(8,128)(2,1)} %constant.27.clone.y_inv.y_ref) | copy-start | bytes 1179652
  57.6 14.9 %copy-start.2 = (bf16[192,1024]{1,0:T(8,128)(2,1)S(1)}, bf16[192,1024]{1,0:T(8,128)(2,1)}, u32[]{:S(2)}) copy-start(bf16[192,1024]{1,0:T(8,128)(2,1)} %constant.26.clone.y_ref.y_fwd) | copy-start | bytes 1179652
  57.7 14.9 %copy-start.4 = (bf16[256,512]{1,0:T(8,128)(2,1)S(1)}, bf16[256,512]{1,0:T(8,128)(2,1)}, u32[]{:S(2)}) copy-start(bf16[256,512]{1,0:T(8,128)(2,1)} %constant.25.clone.zt_inv.zt_ref) | copy-start | bytes 786436
  57.7 14.9 %copy-start.5 = (bf16[512,256]{1,0:T(8,128)(2,1)S(1)}, bf16[512,256]{1,0:T(8,128)(2,1)}, u32[]{:S(2)}) copy-start(bf16[512,256]{1,0:T(8,128)(2,1)} %constant.24.clone.zt_ref.zt_fwd) | copy-start | bytes 786436
  87.6 22.0 %all-to-all-start.2 = ((bf16[64,24,128]{2,1,0:T(8,128)(2,1)}), bf16[64,24,128]{2,1,0:T(8,128)(2,1)S(1)}, u32[]{:S(2)}, u32[]{:S(2)}) async-start(bf16[64,24,128]{2,1,0:T(8,128)(2,1)} %bitcast.35), calls=%async_computation.2 | async-start | bytes 786432 | tf_op jit(solution)/shard_map/all_to_all | solution.py:492

commit v5 on v4

--- a/solution.py
+++ b/solution.py
@@ -392,12 +392,12 @@
     out_ref[...] = jnp.concatenate(blocks, 1).reshape(GROUPS * 8, LANES).astype(jnp.bfloat16)
 
 
-def mix_call(place, message, weights, tables):
+def mix_call(place, message, weights, tables, pin):
     held = [tables["x_fwd"], tables["same"], tables["x_inv"]]
     return pl.pallas_call(
         mix_kernel,
         grid=(1,),
-        in_specs=[pl.BlockSpec(memory_space=pltpu.SMEM), IN_VMEM] + [IN_HBM] * 4,
+        in_specs=[pl.BlockSpec(memory_space=pltpu.SMEM), IN_VMEM] + [pl.BlockSpec(memory_space=pl.ANY)] * 4,
         out_specs=whole(MESSAGE),
         out_shape=pltpu.HBM(MESSAGE, jnp.bfloat16),
         scratch_shapes=[pltpu.VMEM((KX_GROUPS * 4 * ROWS, PARTS * LANES), jnp.float32)]
@@ -405,7 +405,7 @@
         + [pltpu.VMEM(WEIGHTS, jnp.bfloat16), pltpu.SemaphoreType.DMA((7,))],
         compiler_params=pltpu.CompilerParams(vmem_limit_bytes=VMEM_BYTES),
         name="mix_x",
-    )(place, *in_vmem([message]), *map(in_hbm, held + [weights]))
+    )(place, *in_vmem([message]), *pin(held + [weights]))
 
 
 WEIGHT_ROWS = HALF * PARTS * 2 * ROWS
@@ -542,12 +542,13 @@
     field = field.reshape(FIELD)
     own, near, far, across = gather_weights(spectral_weight)
     message = forward_call(field, tables)
+    message = after(message, near)
     weights = arrange_weights([after(own, message), near, far, across], tables)
-    back = mix_call(place, exchange(message), weights[0], tables)
+    back = mix_call(place, exchange(message), weights[0], tables, lambda arrays: map(in_hbm, arrays))
     local = local_term(field, after(local_weight[0], back), bias[0])
     current, message = turn_call(exchange(back), local, tables)
     local = local_term(current, local_weight[1], bias[1])
-    back = mix_call(place, after(exchange(message), local), weights[1], tables)
+    back = mix_call(place, after(exchange(message), local), weights[1], tables, in_vmem)
     return inverse_call(exchange(back), local, tables).reshape(1, C, PLANES, Y, ZT)
 
 

time: 147 us -> 147 us (level)
  no operation moved by 1% of the time
where the time goes in v5:
time: 147 us; the launch traced here: 146 us
  Pallas kernels  69.3 us (47%)
  starting transfers between devices  35.4 us (24%)
  blocking collectives  21.6 us (15%)
  waiting for transfers between devices  18.4 us (13%)
    all_to_all x3, starting transfers between devices, exchange(): lax.all_to_all(grouped, 'space', split_axis=0, concat_axis=0, tiled=True)  33.5 us
    all_to_all x1, blocking collectives, exchange(): lax.all_to_all(grouped, 'space', split_axis=0, concat_axis=0, tiled=True)  21.6 us
    all_to_all x3, waiting for transfers between devices, exchange(): lax.all_to_all(grouped, 'space', split_axis=0, concat_axis=0, tiled=True)  15.8 us
    pallas_call x1, Pallas kernels, turn_call(): pl.pallas_call(turn_kernel, grid=(STEPS,), in_specs=[field_spec()] + [IN_...  15 us
    pallas_call x2, Pallas kernels, local_term(): pl.pallas_call(local_kernel, grid=(PLANES, Y // LOCAL_ROWS), in_specs=[pl...  14.7 us
    pallas_call x1, Pallas kernels, arrange_weights(): pl.pallas_call(arrange_kernel, grid=(1,), in_specs=[IN_HBM] * KX_GROUPS +...  12.4 us
    pallas_call x1, Pallas kernels, inverse_call(): pl.pallas_call(inverse_kernel, grid=(STEPS,), in_specs=[field_spec()] + [...  11.4 us
    pallas_call x2, Pallas kernels, mix_call(): pl.pallas_call(mix_kernel, grid=(1,), in_specs=[pl.BlockSpec(memory_space...  8.19 us
  transfers between devices with their start and end apart: 6, of which 4 were waited for; matrix products, arithmetic and copies ran while one was open for 1% of the time, Pallas kernels for 24%

profile of v5, /device:TPU:2, one launch (start us, length us, event | category | flops | bytes accessed | tf_op | source)
XLA Modules:
  0.0 146.1 jit_solution(12404027397859079145)
XLA Ops:
  0.0 0.0 copy-start.5
  0.0 0.0 copy-start.1
  0.0 0.0 collective-permute-start
  0.0 1.7 %collective-permute-start.1 = (bf16[6,36,2,800]{3,2,1,0:T(2,128)(2,1)}, bf16[6,36,2,800]{3,2,1,0:T(2,128)(2,1)}, u32[]{:S(2)}, u32[]{:S(2)}) collective-permute-start(bf16[6,36,2,800]{3,2,1,0:T(2,128)(2,1)} %bitcast.33), channel_id=1, source_target_pairs={{0,2},{1,3},{2,0},{3,1},{4,6},{5,7},{6,4},{7,5},{8,10},{9,11},{10,... | collective-permute-start | bytes 2073608 | tf_op jit(solution)/shard_map/ppermute | solution.py:481
  1.7 7.6 %forward_zt_y.1 = bf16[1536,128]{1,0:T(8,128)(2,1)} custom-call(bf16[2,10,2,128,512]{4,3,2,1,0:T(8,128)(2,1)} %bitcast.27, bf16[512,256]{1,0:T(8,128)(2,1)} %constant.24.clone.zt_ref.zt_fwd, bf16[192,1024]{1,0:T(8,128)(2,1)} %constant.26.clone.y_ref.y_fwd), custom_call_target="tpu_custom_call" | custom-call | tf_op jit(solution)/shard_map/forward_zt_y/pallas_call | solution.py:232
  9.3 0.0 collective-permute-done.near
  9.3 0.0 copy-start.10
  9.3 14.5 %all-to-all-start = ((bf16[64,24,128]{2,1,0:T(8,128)(2,1)}), bf16[64,24,128]{2,1,0:T(8,128)(2,1)S(1)}, u32[]{:S(2)}, u32[]{:S(2)}) async-start(bf16[64,24,128]{2,1,0:T(8,128)(2,1)} %bitcast.29), calls=%async_computation | async-start | bytes 786432 | tf_op jit(solution)/shard_map/all_to_all | solution.py:492
  23.8 0.0 collective-permute-done.1.far
  23.8 0.3 collective-permute-start.2
  24.1 2.6 %collective-permute-done.2.across = bf16[6,36,2,800]{3,2,1,0:T(2,128)(2,1)} collective-permute-done((bf16[6,36,2,800]{3,2,1,0:T(2,128)(2,1)}, bf16[6,36,2,800]{3,2,1,0:T(2,128)(2,1)}, u32[]{:S(2)}, u32[]{:S(2)}) %collective-permute-start.2) | collective-permute-done | bytes 691232 | tf_op jit(solution)/shard_map/ppermute | solution.py:481
  26.7 0.0 copy-done.5
  26.7 0.0 copy-done.1
  26.7 12.4 %arrange_weights.1 = (bf16[4,1440,128]{2,1,0:T(8,128)(2,1)}, bf16[4,1440,128]{2,1,0:T(8,128)(2,1)}) custom-call(bf16[6,36,2,800]{3,2,1,0:T(2,128)(2,1)} %bitcast.34, bf16[6,36,2,800]{3,2,1,0:T(2,128)(2,1)} %collective-permute-done.near, bf16[6,36,2,800]{3,2,1,0:T(2,128)(2,1)} %collective-permute-done.1.far, ...), custom_call_target="tpu_custom_call" | custom-call | tf_op jit(solution)/shard_map/arrange_weights/pallas_call | solution.py:462
  39.1 0.6 all-to-all-done
  39.7 4.0 %mix_x.2 = bf16[1536,128]{1,0:T(8,128)(2,1)} custom-call(s32[1]{0:T(128)} %bitcast.5.place_ref, bf16[1536,128]{1,0:T(8,128)(2,1)S(1)} %bitcast.24, bf16[192,512]{1,0:T(8,128)(2,1)} %constant.28.clone.x_hbm, bf16[128,128]{1,0:T(8,128)(2,1)} %constant.30.clone.same_hbm, bf16[512,384]{1,0:T(8,128)(2,1)} %constant.29.clone.inv_hbm, ...), custom_call_target="tpu_custom_call" | custom-call | tf_op jit(solution)/shard_map/mix_x/pallas_call | solution.py:397
  43.7 12.2 %all-to-all-start.1 = ((bf16[64,24,128]{2,1,0:T(8,128)(2,1)}), bf16[64,24,128]{2,1,0:T(8,128)(2,1)S(1)}, u32[]{:S(2)}, u32[]{:S(2)}) async-start(bf16[64,24,128]{2,1,0:T(8,128)(2,1)} %bitcast.30), calls=%async_computation.1 | async-start | bytes 786432 | tf_op jit(solution)/shard_map/all_to_all | solution.py:492
  55.9 0.8 fusion
  56.7 0.1 copy.17
  56.8 0.0 copy-done.10
  56.8 0.0 copy-start
  56.8 0.0 copy-start.3
  56.8 0.0 copy-start.6
  56.8 0.0 copy-start.7
  56.9 7.3 %local_mixing.2.local_ref = bf16[2,10,2,128,512]{4,3,2,1,0:T(8,128)(2,1)} custom-call(f32[20]{0:T(128)S(1)} %get-tuple-element.23.offset_ref, bf16[20,20]{1,0:T(8,128)(2,1)S(1)} %multiply_bitcast_fusion.weight_ref, bf16[2,10,2,128,512]{4,3,2,1,0:T(8,128)(2,1)} %bitcast.28), custom_call_target="tpu_custom_call" | custom-call | tf_op jit(solution)/shard_map/local_mixing/pallas_call | solution.py:523
  64.2 7.6 %all-to-all-done.1 = bf16[64,24,128]{2,1,0:T(8,128)(2,1)S(1)} async-done(((bf16[64,24,128]{2,1,0:T(8,128)(2,1)}), bf16[64,24,128]{2,1,0:T(8,128)(2,1)S(1)}, u32[]{:S(2)}, u32[]{:S(2)}) %all-to-all-start.1) | async-done | bytes 393248 | tf_op jit(solution)/shard_map/all_to_all | solution.py:492
  71.7 0.0 copy-done
  71.8 0.0 copy-done.3
  71.8 0.0 copy-done.6
  71.8 0.0 copy-done.7
  71.8 15.0 %inverse_then_forward.1 = (bf16[2,10,2,128,512]{4,3,2,1,0:T(8,128)(2,1)}, bf16[1536,128]{1,0:T(8,128)(2,1)}) custom-call(bf16[2,10,2,128,512]{4,3,2,1,0:T(8,128)(2,1)} %local_mixing.2.local_ref, bf16[1536,128]{1,0:T(8,128)(2,1)S(1)} %bitcast.25, bf16[1024,192]{1,0:T(8,128)(2,1)S(1)} %copy-done, bf16[256,512]{1,0:T(8,128)(2,1)S(1)} %copy-done.6, ...), custom_call_target="tpu_custom_call" | custom-call | tf_op jit(solution)/shard_map/inverse_then_forward/pallas_call | solution.py:320
  86.8 6.8 %all-to-all-start.2 = ((bf16[64,24,128]{2,1,0:T(8,128)(2,1)}), bf16[64,24,128]{2,1,0:T(8,128)(2,1)S(1)}, u32[]{:S(2)}, u32[]{:S(2)}) async-start(bf16[64,24,128]{2,1,0:T(8,128)(2,1)} %bitcast.35), calls=%async_computation.2 | async-start | bytes 786432 | tf_op jit(solution)/shard_map/all_to_all | solution.py:492
  93.6 0.1 copy.16
  93.7 0.0 copy-start.2
  93.7 0.0 copy-start.4
  93.7 0.0 copy-start.8
  93.7 0.0 copy-start.9
  93.8 7.4 %local_mixing.3.local_ref = bf16[2,10,2,128,512]{4,3,2,1,0:T(8,128)(2,1)} custom-call(f32[20]{0:T(128)S(1)} %get-tuple-element.24.offset_ref, bf16[20,20]{1,0:T(8,128)(2,1)S(1)} %multiply_bitcast_fusion.1.weight_ref, bf16[2,10,2,128,512]{4,3,2,1,0:T(8,128)(2,1)} %get-tuple-element.17.field_ref), custom_call_target="tpu_custom_call" | custom-call | tf_op jit(solution)/shard_map/local_mixing/pallas_call | solution.py:523
  101.1 7.7 %all-to-all-done.2 = bf16[64,24,128]{2,1,0:T(8,128)(2,1)S(1)} async-done(((bf16[64,24,128]{2,1,0:T(8,128)(2,1)}), bf16[64,24,128]{2,1,0:T(8,128)(2,1)S(1)}, u32[]{:S(2)}, u32[]{:S(2)}) %all-to-all-start.2) | async-done | bytes 393248 | tf_op jit(solution)/shard_map/all_to_all | solution.py:492
  108.9 0.0 copy-done.2
  108.9 0.0 copy-done.4
  108.9 0.0 copy-done.8
  108.9 0.0 copy-done.9
  108.9 4.2 %mix_x.3 = bf16[1536,128]{1,0:T(8,128)(2,1)} custom-call(s32[1]{0:T(128)} %bitcast.5.place_ref, bf16[1536,128]{1,0:T(8,128)(2,1)S(1)} %bitcast.26, bf16[192,512]{1,0:T(8,128)(2,1)S(1)} %copy-done.8, bf16[128,128]{1,0:T(8,128)(2,1)S(1)} %copy-done.9, bf16[512,384]{1,0:T(8,128)(2,1)S(1)} %copy-done.2, bf16[4,1440,128]{2,1,0:T(8,128)(2,1)S(1)} %copy-done.4), custom_call_target="tpu_custom_call" | custom-call | tf_op jit(solution)/shard_map/mix_x/pallas_call | solution.py:397
  113.1 21.6 %all_to_all.20 = bf16[64,24,128]{2,1,0:T(8,128)(2,1)S(1)} all-to-all(bf16[64,24,128]{2,1,0:T(8,128)(2,1)} %bitcast.31), channel_id=1, replica_groups=mesh['space'=64,'batch'=4] {'space'}, dimensions={0} | all-to-all | bytes 786432 | tf_op jit(solution)/shard_map/all_to_all | solution.py:492
  134.7 11.4 %inverse_zt_y.1 = bf16[2,10,2,128,512]{4,3,2,1,0:T(8,128)(2,1)} custom-call(bf16[2,10,2,128,512]{4,3,2,1,0:T(8,128)(2,1)} %local_mixing.3.local_ref, bf16[1536,128]{1,0:T(8,128)(2,1)S(1)} %bitcast.23, bf16[1024,192]{1,0:T(8,128)(2,1)S(1)} %copy-done, bf16[256,512]{1,0:T(8,128)(2,1)S(1)} %copy-done.6), custom_call_target="tpu_custom_call" | custom-call | tf_op jit(solution)/shard_map/inverse_zt_y/pallas_call | solution.py:285
  (3 shorter events, 0.0 us)
Async XLA Ops:
  0.0 26.7 %copy-start.5 = (bf16[720,768]{1,0:T(8,128)(2,1)S(1)}, bf16[720,768]{1,0:T(8,128)(2,1)}, u32[]{:S(2)}) copy-start(bf16[720,768]{1,0:T(8,128)(2,1)} %constant.32.clone.place_ref) | copy-start | bytes 3317764
  0.0 26.7 %copy-start.1 = (bf16[800,1280]{1,0:T(8,128)(2,1)S(1)}, bf16[800,1280]{1,0:T(8,128)(2,1)}, u32[]{:S(2)}) copy-start(bf16[800,1280]{1,0:T(8,128)(2,1)} %constant.31.clone.select_ref) | copy-start | bytes 6144004
  0.0 9.3 %collective-permute-start = (bf16[6,36,2,800]{3,2,1,0:T(2,128)(2,1)}, bf16[6,36,2,800]{3,2,1,0:T(2,128)(2,1)}, u32[]{:S(2)}, u32[]{:S(2)}) collective-permute-start(bf16[6,36,2,800]{3,2,1,0:T(2,128)(2,1)} %bitcast.32), channel_id=1, source_target_pairs={{0,1},{1,0},{2,3},{3,2},{4,5},{5,4},{6,7},{7,6},{8,9},{9,8},{10,11... | collective-permute-start | bytes 2073608 | tf_op jit(solution)/shard_map/ppermute | solution.py:481
  0.0 23.8 %collective-permute-start.1 = (bf16[6,36,2,800]{3,2,1,0:T(2,128)(2,1)}, bf16[6,36,2,800]{3,2,1,0:T(2,128)(2,1)}, u32[]{:S(2)}, u32[]{:S(2)}) collective-permute-start(bf16[6,36,2,800]{3,2,1,0:T(2,128)(2,1)} %bitcast.33), channel_id=1, source_target_pairs={{0,2},{1,3},{2,0},{3,1},{4,6},{5,7},{6,4},{7,5},{8,10},{9,11},{10,... | collective-permute-start | bytes 2073608 | tf_op jit(solution)/shard_map/ppermute | solution.py:481
  9.3 47.5 %copy-start.10 = (f32[2,20]{1,0:T(2,128)S(1)}, f32[2,20]{1,0:T(2,128)}, u32[]{:S(2)}) copy-start(f32[2,20]{1,0:T(2,128)} %param.16) | copy-start | bytes 484
  9.3 30.4 %all-to-all-start = ((bf16[64,24,128]{2,1,0:T(8,128)(2,1)}), bf16[64,24,128]{2,1,0:T(8,128)(2,1)S(1)}, u32[]{:S(2)}, u32[]{:S(2)}) async-start(bf16[64,24,128]{2,1,0:T(8,128)(2,1)} %bitcast.29), calls=%async_computation | async-start | bytes 786432 | tf_op jit(solution)/shard_map/all_to_all | solution.py:492
  23.8 2.9 %collective-permute-start.2 = (bf16[6,36,2,800]{3,2,1,0:T(2,128)(2,1)}, bf16[6,36,2,800]{3,2,1,0:T(2,128)(2,1)}, u32[]{:S(2)}, u32[]{:S(2)}) collective-permute-start(bf16[6,36,2,800]{3,2,1,0:T(2,128)(2,1)} %collective-permute-done.1.far), channel_id=1, source_target_pairs={{0,1},{1,0},{2,3},{3,2},{4,5},{5,4},{6,7},{7,6},{8,9},{9,8},{10,11... | collective-permute-start | bytes 2073608 | tf_op jit(solution)/shard_map/ppermute | solution.py:481
  43.7 28.1 %all-to-all-start.1 = ((bf16[64,24,128]{2,1,0:T(8,128)(2,1)}), bf16[64,24,128]{2,1,0:T(8,128)(2,1)S(1)}, u32[]{:S(2)}, u32[]{:S(2)}) async-start(bf16[64,24,128]{2,1,0:T(8,128)(2,1)} %bitcast.30), calls=%async_computation.1 | async-start | bytes 786432 | tf_op jit(solution)/shard_map/all_to_all | solution.py:492
  56.8 14.9 %copy-start = (bf16[1024,192]{1,0:T(8,128)(2,1)S(1)}, bf16[1024,192]{1,0:T(8,128)(2,1)}, u32[]{:S(2)}) copy-start(bf16[1024,192]{1,0:T(8,128)(2,1)} %constant.27.clone.y_inv.y_ref) | copy-start | bytes 1179652
  56.8 14.9 %copy-start.3 = (bf16[192,1024]{1,0:T(8,128)(2,1)S(1)}, bf16[192,1024]{1,0:T(8,128)(2,1)}, u32[]{:S(2)}) copy-start(bf16[192,1024]{1,0:T(8,128)(2,1)} %constant.26.clone.y_ref.y_fwd) | copy-start | bytes 1179652
  56.8 14.9 %copy-start.6 = (bf16[256,512]{1,0:T(8,128)(2,1)S(1)}, bf16[256,512]{1,0:T(8,128)(2,1)}, u32[]{:S(2)}) copy-start(bf16[256,512]{1,0:T(8,128)(2,1)} %constant.25.clone.zt_inv.zt_ref) | copy-start | bytes 786436
  56.8 14.9 %copy-start.7 = (bf16[512,256]{1,0:T(8,128)(2,1)S(1)}, bf16[512,256]{1,0:T(8,128)(2,1)}, u32[]{:S(2)}) copy-start(bf16[512,256]{1,0:T(8,128)(2,1)} %constant.24.clone.zt_ref.zt_fwd) | copy-start | bytes 786436
  86.8 22.1 %all-to-all-start.2 = ((bf16[64,24,128]{2,1,0:T(8,128)(2,1)}), bf16[64,24,128]{2,1,0:T(8,128)(2,1)S(1)}, u32[]{:S(2)}, u32[]{:S(2)}) async-start(bf16[64,24,128]{2,1,0:T(8,128)(2,1)} %bitcast.35), calls=%async_computation.2 | async-start | bytes 786432 | tf_op jit(solution)/shard_map/all_to_all | solution.py:492
  93.7 15.2 %copy-start.2 = (bf16[512,384]{1,0:T(8,128)(2,1)S(1)}, bf16[512,384]{1,0:T(8,128)(2,1)}, u32[]{:S(2)}) copy-start(bf16[512,384]{1,0:T(8,128)(2,1)} %constant.29.clone.inv_hbm) | copy-start | bytes 1179652
  93.7 15.2 %copy-start.4 = (bf16[4,1440,128]{2,1,0:T(8,128)(2,1)S(1)}, bf16[4,1440,128]{2,1,0:T(8,128)(2,1)}, u32[]{:S(2)}) copy-start(bf16[4,1440,128]{2,1,0:T(8,128)(2,1)} %get-tuple-element.20.weights_hbm) | copy-start | bytes 4423684
  93.7 15.2 %copy-start.8 = (bf16[192,512]{1,0:T(8,128)(2,1)S(1)}, bf16[192,512]{1,0:T(8,128)(2,1)}, u32[]{:S(2)}) copy-start(bf16[192,512]{1,0:T(8,128)(2,1)} %constant.28.clone.x_hbm) | copy-start | bytes 589828
  93.7 15.1 %copy-start.9 = (bf16[128,128]{1,0:T(8,128)(2,1)S(1)}, bf16[128,128]{1,0:T(8,128)(2,1)}, u32[]{:S(2)}) copy-start(bf16[128,128]{1,0:T(8,128)(2,1)} %constant.30.clone.same_hbm) | copy-start | bytes 98308
